TPU v7x, 32 devices: a whole 2x2x4 slice. The times are simulated.
32 devices in a mesh: dp: 8 (over y, x, core), tensor: 4 (over z).
Axes of the slice: x: 2, y: 2, z: 4, core: 2. Of those that a mesh axis runs over, the one named last changes fastest.
Arguments:
- inputs: bfloat16 [8192, 1024], P(('dp', 'tensor')), may hold values from -6 to 6
- segments: int32 [8, 1024], P('dp'), may hold values from 0 to 15, never falling along the last dimension, each value on 1 to 512 neighbouring positions
- cotangent: bfloat16 [8192, 1024], P(('dp', 'tensor')), may hold values from -6 to 6
- norm_in: float32 [1024], replicated, may hold values from 0.5 to 1.5
- w_in: bfloat16 [1024, 6144], P('dp', 'tensor'), may hold values from -0.1875 to 0.1875
- w_alpha_beta: bfloat16 [1024, 16], P('dp', 'tensor'), may hold values from -0.1875 to 0.1875
- conv_weight: float32 [4, 4096], replicated, may hold values from -3 to 3
- a_log: float32 [8], replicated, may hold values from -6.5 to -2.5
- dt_bias: float32 [8], replicated, may hold values from -1 to 1
- out_gain: float32 [256], replicated, may hold values from 0.5 to 1.5
- w_out: bfloat16 [2048, 1024], P('tensor', 'dp'), may hold values from -0.125 to 0.125
- norm_ffn: float32 [1024], replicated, may hold values from 0.5 to 1.5
- w_gate: bfloat16 [1024, 2816], P('dp', 'tensor'), may hold values from -0.1875 to 0.1875
- w_up: bfloat16 [1024, 2816], P('dp', 'tensor'), may hold values from -0.1875 to 0.1875
- w_down: bfloat16 [2816, 1024], P('tensor', 'dp'), may hold values from -0.109375 to 0.109375
Outputs:
- output: bfloat16 [8192, 1024], P(('dp', 'tensor'))
- d_inputs: float32 [8192, 1024], P(('dp', 'tensor'))
- grad_norm_in: float32 [1024], replicated
- grad_w_in: float32 [1024, 6144], P('dp', 'tensor')
- grad_w_alpha_beta: float32 [1024, 16], P('dp', 'tensor')
- grad_conv_weight: float32 [4, 4096], replicated
- grad_a_log: float32 [8], replicated
- grad_dt_bias: float32 [8], replicated
- grad_out_gain: float32 [256], replicated
- grad_w_out: float32 [2048, 1024], P('tensor', 'dp')
- grad_norm_ffn: float32 [1024], replicated
- grad_w_gate: float32 [1024, 2816], P('dp', 'tensor')
- grad_w_up: float32 [1024, 2816], P('dp', 'tensor')
- grad_w_down: float32 [2816, 1024], P('tensor', 'dp')
Inputs may be any that keep to these rules, and one draw needn't show every extreme that they name: `segments`: within a sequence the numbers never fall, and each number covers at most 512 positions.
All inputs are finite; a program needn't handle non-finite values.
Results may differ from a plain program's by a relative error of at most 0.017.
Values may be sent and summed in bfloat16 or wider, within the bound.
No kernel may reach another device: no remote copies, remote signals or barrier semaphores. Data moves between devices by JAX's collectives and lax.ppermute only.
A program may use at most 256 MiB of HBM per device.

v0:
```python
import jax
import jax.numpy as jnp
from jax import lax
from jax.sharding import PartitionSpec as P

DK = 128
DV = 256
SPAN = 64


EXACT_PRECISION = lax.Precision.HIGHEST
EPSILON = 1e-06


def rms_rows(values, gain):
    return values * lax.rsqrt(jnp.mean(values * values, axis=-1, keepdims=True) + EPSILON) * gain


def rms_back(values, gain, grad_normed):
    scale = lax.rsqrt(jnp.mean(values * values, axis=-1, keepdims=True) + EPSILON)
    weighted = grad_normed * gain
    inner = jnp.mean(weighted * values, axis=-1, keepdims=True)
    grad_values = scale * weighted - values * scale * scale * scale * inner
    return (grad_values, jnp.sum(grad_normed * values * scale, axis=0))


def times_transposed(left, right):
    return lax.dot_general(
        left, right, (((1,), (1,)), ((), ())), preferred_element_type=jnp.float32
    )


def transposed_times(left, right):
    return lax.dot_general(
        left, right, (((0,), (0,)), ((), ())), preferred_element_type=jnp.float32
    )


def short_conv(signal, kernel, doc_ids):
    length = signal.shape[0]
    running = signal * kernel[0]
    for offset in range(1, kernel.shape[0]):
        shifted = jnp.concatenate(
            [jnp.zeros((offset, signal.shape[1]), jnp.float32), signal[: length - offset]], axis=0
        )
        shifted_ids = jnp.concatenate(
            [jnp.full((offset,), -1, jnp.int32), doc_ids[: length - offset]]
        )
        running = running + jnp.where(
            (shifted_ids == doc_ids)[:, None], shifted * kernel[offset], 0.0
        )
    return running


def delta_spans(queries, keys_in, values, decays, beta_gate, doc_ids):
    length = queries.shape[0]
    head_count = queries.shape[1]
    block_count = length // SPAN
    places = jnp.arange(SPAN)
    strict = places[:, None] > places[None, :]
    within = places[:, None] >= places[None, :]
    identity = jnp.eye(SPAN, dtype=jnp.float32)

    def to_blocks(array):
        return array.reshape((block_count, SPAN) + array.shape[1:])

    def block_step(carried, block_in):
        recurrent_carry_state, last_doc = carried
        query_b, key_b, value_b, decay_b, beta_b, doc_b = block_in
        cum_decay = jnp.transpose(jnp.cumsum(decay_b, axis=0))
        log_gap = cum_decay[:, :, None] - cum_decay[:, None, :]
        same_doc = doc_b[:, None] == doc_b[None, :]
        strict_mask = (strict & same_doc)[None]
        within_mask = (within & same_doc)[None]
        fade_strict = jnp.where(strict_mask, jnp.exp(jnp.where(strict_mask, log_gap, 0.0)), 0.0)
        fade_within = jnp.where(within_mask, jnp.exp(jnp.where(within_mask, log_gap, 0.0)), 0.0)
        visible_extent = jnp.where((doc_b == last_doc)[None, :], jnp.exp(cum_decay), 0.0)
        key_per_head = jnp.transpose(key_b, (1, 0, 2))
        query_per_head = jnp.transpose(query_b, (1, 0, 2))
        value_h = jnp.transpose(value_b, (1, 0, 2))
        beta_h = jnp.transpose(beta_b)
        key_key = jnp.einsum("hik,hjk->hij", key_per_head, key_per_head, precision=EXACT_PRECISION)
        system = identity[None] + beta_h[:, :, None] * key_key * fade_strict
        solved_values = jax.scipy.linalg.solve_triangular(
            system, beta_h[:, :, None] * value_h, lower=True, unit_diagonal=True
        )
        solved_keys = jax.scipy.linalg.solve_triangular(
            system,
            (beta_h * visible_extent)[:, :, None] * key_per_head,
            lower=True,
            unit_diagonal=True,
        )
        delta_update_rows = solved_values - jnp.einsum(
            "sty,syo->sto", solved_keys, recurrent_carry_state, precision=EXACT_PRECISION
        )
        query_key = (
            jnp.einsum("hik,hjk->hij", query_per_head, key_per_head, precision=EXACT_PRECISION)
            * fade_within
        )
        computed_output = visible_extent[:, :, None] * jnp.einsum(
            "sty,syo->sto", query_per_head, recurrent_carry_state, precision=EXACT_PRECISION
        )
        computed_output = computed_output + jnp.einsum(
            "hij,hjv->hiv", query_key, delta_update_rows, precision=EXACT_PRECISION
        )
        trailing_decay = jnp.where(
            (doc_b == doc_b[-1])[None, :], jnp.exp(cum_decay[:, -1:] - cum_decay), 0.0
        )
        keep_factor = jnp.where(doc_b[-1] == last_doc, jnp.exp(cum_decay[:, -1]), 0.0)
        updated_state = keep_factor[:, None, None] * recurrent_carry_state
        updated_state = updated_state + jnp.einsum(
            "fgb,fgn->fbn",
            trailing_decay[:, :, None] * key_per_head,
            delta_update_rows,
            precision=EXACT_PRECISION,
        )
        return ((updated_state, doc_b[-1]), jnp.transpose(computed_output, (1, 0, 2)))

    initial = (
        jnp.zeros((head_count, keys_in.shape[2], values.shape[2]), jnp.float32),
        jnp.array(-1, jnp.int32),
    )
    blocks_in = (
        to_blocks(queries),
        to_blocks(keys_in),
        to_blocks(values),
        to_blocks(decays),
        to_blocks(beta_gate),
        to_blocks(doc_ids),
    )
    final_state, block_outs = lax.scan(block_step, initial, blocks_in)
    return block_outs.reshape(length, head_count, values.shape[2])


def mixer_local(projected, alpha_beta, kernel, a_log, dt_bias, out_gain, doc_ids):
    length = projected.shape[0]
    head_count = a_log.shape[0]
    per_head = projected.reshape(length, head_count, 2 * DK + 2 * DV)
    conv_in = per_head[:, :, : 2 * DK + DV].reshape(length, head_count * (2 * DK + DV))
    gate_out = per_head[:, :, 2 * DK + DV :]
    conv_out = jax.nn.silu(short_conv(conv_in, kernel, doc_ids)).reshape(
        length, head_count, 2 * DK + DV
    )
    queries = conv_out[:, :, :DK]
    keys_in = conv_out[:, :, DK : 2 * DK]
    values = conv_out[:, :, 2 * DK :]
    queries = (
        queries
        * lax.rsqrt(jnp.sum(queries * queries, axis=-1, keepdims=True) + EPSILON)
        * DK ** (-0.5)
    )
    keys_in = keys_in * lax.rsqrt(jnp.sum(keys_in * keys_in, axis=-1, keepdims=True) + EPSILON)
    pair_rows = alpha_beta.reshape(length, head_count, 2)
    decays = -jnp.exp(a_log) * jax.nn.softplus(pair_rows[:, :, 0] + dt_bias)
    beta_gate = jax.nn.sigmoid(pair_rows[:, :, 1])
    recurrent = delta_spans(queries, keys_in, values, decays, beta_gate, doc_ids)
    normed = rms_rows(recurrent, out_gain)
    return (normed * jax.nn.silu(gate_out)).reshape(length, head_count * DV)


def mixer_front(row_inputs, norm_in, w_in, w_alpha_beta, w_out):
    normed = rms_rows(row_inputs, norm_in).astype(jnp.bfloat16)
    seq_rows = lax.all_gather(normed, "tensor", axis=0, tiled=True)
    whole_in, whole_pair, whole_out = (
        lax.all_gather(w_in, "dp", axis=0, tiled=True),
        lax.all_gather(w_alpha_beta, "dp", axis=0, tiled=True),
        lax.all_gather(w_out, "dp", axis=1, tiled=True),
    )
    projected = jnp.dot(seq_rows, whole_in, preferred_element_type=jnp.float32)
    alpha_beta = jnp.dot(seq_rows, whole_pair, preferred_element_type=jnp.float32)
    return (seq_rows, whole_in, whole_pair, whole_out, projected, alpha_beta)


def ffn_front(resid, norm_ffn, w_gate, w_up, w_down):
    normed = rms_rows(resid, norm_ffn).astype(jnp.bfloat16)
    seq_rows = lax.all_gather(normed, "tensor", axis=0, tiled=True)
    whole_gate, whole_up, whole_down = (
        lax.all_gather(w_gate, "dp", axis=0, tiled=True),
        lax.all_gather(w_up, "dp", axis=0, tiled=True),
        lax.all_gather(w_down, "dp", axis=1, tiled=True),
    )
    gate_pre = jnp.dot(seq_rows, whole_gate, preferred_element_type=jnp.float32)
    up_pre = jnp.dot(seq_rows, whole_up, preferred_element_type=jnp.float32)
    hidden = (jax.nn.silu(gate_pre) * up_pre).astype(jnp.bfloat16)
    return (seq_rows, whole_gate, whole_up, whole_down, gate_pre, up_pre, hidden)


def local(
    inputs,
    segments,
    cotangent,
    norm_in,
    w_in,
    w_alpha_beta,
    conv_weight,
    a_log,
    dt_bias,
    out_gain,
    w_out,
    norm_ffn,
    w_gate,
    w_up,
    w_down,
):
    doc_ids = segments[0]
    part_index = lax.axis_index("tensor")
    head_count = a_log.shape[0] // lax.axis_size("tensor")
    conv_width = head_count * (2 * DK + DV)
    conv_mine = lax.dynamic_slice_in_dim(conv_weight, part_index * conv_width, conv_width, 1)
    alog_mine = lax.dynamic_slice_in_dim(a_log, part_index * head_count, head_count, 0)
    bias_mine = lax.dynamic_slice_in_dim(dt_bias, part_index * head_count, head_count, 0)

    def local_mixer(projected, alpha_beta, kernel, alog_part, bias_part, gain_part):
        return mixer_local(projected, alpha_beta, kernel, alog_part, bias_part, gain_part, doc_ids)

    input_rows = inputs.astype(jnp.float32)
    seq_rows, whole_in, whole_pair, whole_out, projected, alpha_beta = mixer_front(
        input_rows, norm_in, w_in, w_alpha_beta, w_out
    )
    gated_full, pullback = jax.vjp(
        local_mixer, projected, alpha_beta, conv_mine, alog_mine, bias_mine, out_gain
    )
    gated = gated_full.astype(jnp.bfloat16)
    resid = input_rows + lax.psum_scatter(
        jnp.dot(gated, whole_out, preferred_element_type=jnp.float32),
        "tensor",
        scatter_dimension=0,
        tiled=True,
    )
    ffn_seq, whole_gate, whole_up, whole_down, gate_pre, up_pre, hidden = ffn_front(
        resid, norm_ffn, w_gate, w_up, w_down
    )
    output = (
        resid
        + lax.psum_scatter(
            jnp.dot(hidden, whole_down, preferred_element_type=jnp.float32).astype(jnp.bfloat16),
            "tensor",
            scatter_dimension=0,
            tiled=True,
        ).astype(jnp.float32)
    ).astype(jnp.bfloat16)
    back_seq = lax.all_gather(cotangent, "tensor", axis=0, tiled=True)
    d_hidden = times_transposed(back_seq, whole_down)
    sigmoid_gate = jax.nn.sigmoid(gate_pre)
    d_up = (d_hidden * gate_pre * sigmoid_gate).astype(jnp.bfloat16)
    d_gate = (d_hidden * up_pre * sigmoid_gate * (1.0 + gate_pre * (1.0 - sigmoid_gate))).astype(
        jnp.bfloat16
    )
    d_normed_ffn = lax.psum_scatter(
        (times_transposed(d_gate, whole_gate) + times_transposed(d_up, whole_up)).astype(
            jnp.bfloat16
        ),
        "tensor",
        scatter_dimension=0,
        tiled=True,
    ).astype(jnp.float32)
    resid_from_norm, gain_ffn_part = rms_back(resid, norm_ffn, d_normed_ffn)
    d_resid = cotangent.astype(jnp.float32) + resid_from_norm
    mixer_back_seq = lax.all_gather(d_resid.astype(jnp.bfloat16), "tensor", axis=0, tiled=True)
    d_gated = times_transposed(mixer_back_seq, whole_out)
    d_projected, d_pair, d_conv, d_alog, d_bias, d_gain_out = pullback(d_gated)
    d_projected = d_projected.astype(jnp.bfloat16)
    d_pair = d_pair.astype(jnp.bfloat16)
    d_normed_in = lax.psum_scatter(
        (times_transposed(d_projected, whole_in) + times_transposed(d_pair, whole_pair)).astype(
            jnp.bfloat16
        ),
        "tensor",
        scatter_dimension=0,
        tiled=True,
    ).astype(jnp.float32)
    input_from_norm, gain_in_part = rms_back(input_rows, norm_in, d_normed_in)
    d_inputs = d_resid + input_from_norm
    conv_full = lax.dynamic_update_slice_in_dim(
        jnp.zeros(conv_weight.shape, jnp.float32), d_conv, part_index * conv_width, 1
    )
    alog_full = lax.dynamic_update_slice_in_dim(
        jnp.zeros(a_log.shape, jnp.float32), d_alog, part_index * head_count, 0
    )
    bias_full = lax.dynamic_update_slice_in_dim(
        jnp.zeros(dt_bias.shape, jnp.float32), d_bias, part_index * head_count, 0
    )
    small_sums = lax.psum(
        (gain_in_part, gain_ffn_part, conv_full, alog_full, bias_full, d_gain_out), ("dp", "tensor")
    )
    owned_in, owned_pair, owned_out, owned_gate, owned_up, owned_down = (
        lax.psum_scatter(
            transposed_times(seq_rows, d_projected), "dp", scatter_dimension=0, tiled=True
        ),
        lax.psum_scatter(transposed_times(seq_rows, d_pair), "dp", scatter_dimension=0, tiled=True),
        lax.psum_scatter(
            transposed_times(mixer_back_seq, gated), "dp", scatter_dimension=0, tiled=True
        ),
        lax.psum_scatter(transposed_times(ffn_seq, d_gate), "dp", scatter_dimension=0, tiled=True),
        lax.psum_scatter(transposed_times(ffn_seq, d_up), "dp", scatter_dimension=0, tiled=True),
        lax.psum_scatter(transposed_times(back_seq, hidden), "dp", scatter_dimension=0, tiled=True),
    )
    return (
        output,
        d_inputs,
        small_sums[0],
        owned_in,
        owned_pair,
        small_sums[2],
        small_sums[3],
        small_sums[4],
        small_sums[5],
        jnp.transpose(owned_out),
        small_sums[1],
        owned_gate,
        owned_up,
        jnp.transpose(owned_down),
    )


def solution(mesh):
    return jax.shard_map(
        local,
        mesh=mesh,
        in_specs=(
            P(("dp", "tensor"), None),
            P("dp", None),
            P(("dp", "tensor"), None),
            P(),
            P("dp", "tensor"),
            P("dp", "tensor"),
            P(),
            P(),
            P(),
            P(),
            P("tensor", "dp"),
            P(),
            P("dp", "tensor"),
            P("dp", "tensor"),
            P("tensor", "dp"),
        ),
        out_specs=(
            P(("dp", "tensor"), None),
            P(("dp", "tensor"), None),
            P(),
            P("dp", "tensor"),
            P("dp", "tensor"),
            P(),
            P(),
            P(),
            P(),
            P("tensor", "dp"),
            P(),
            P("dp", "tensor"),
            P("dp", "tensor"),
            P("tensor", "dp"),
        ),
        check_vma=False,
    )
```

profile of v0, /device:TPU:0, one launch (start us, length us, event | category | flops | bytes accessed | tf_op | source)
XLA Modules:
  0.0 2444.6 jit_solution(11858924694969538608)
XLA Ops:
  13.2 10.4 all_gather.31
  25.9 33.8 %all-gather.10.cloned.1.call-done = bf16[1024,1024]{1,0:T(8,128)(2,1)} async-done(((bf16[256,1024]{1,0:T(8,128)(2,1)}), bf16[1024,1024]{1,0:T(8,128)(2,1)}) %all-gather.10.cloned.1.call-update) | async-done | bytes 2097168 | tf_op jit(solution)/shard_map/all_gather | solution.py:163
  63.0 29.6 %all-gather.12.cloned.1.call-done = bf16[1024,1536]{1,0:T(8,128)(2,1)} async-done(((bf16[128,1536]{1,0:T(8,128)(2,1)}), bf16[1024,1536]{1,0:T(8,128)(2,1)}) %all-gather.12.cloned.1.call-update) | async-done | bytes 3145744 | tf_op jit(solution)/shard_map/all_gather | solution.py:165
  173.1 501.5 %while.117 = (s32[]{:T(128)}, f32[2,128,256]{2,1,0:T(8,128)S(1)}, s32[]{:T(128)}, f32[16,64,2,256]{3,1,2,0:T(8,128)}, pred[16,2,64,64]{3,2,1,0:T(32,128)(4,1)}, ...) while((s32[]{:T(128)}, f32[2,128,256]{2,1,0:T(8,128)S(1)}, ...), condition=%wide.region_5.6_spmd.clone, body=%wide.region_3.5_spmd.clone.sunk | while | flops 239911872 | bytes 5524639 | solution.py:131
  175.8 9.8 custom-call.76
  207.1 9.8 custom-call.76
  238.4 9.8 custom-call.76
  269.8 9.8 custom-call.76
  551.7 9.8 custom-call.76
  692.4 76.3 %reduce-scatter.13.cloned.1.call-done = f32[256,1024]{1,0:T(8,128)} async-done(((f32[1024,1024]{1,0:T(8,128)}), f32[256,1024]{1,0:T(8,128)}) %reduce-scatter.13.cloned.1.call-update) | async-done | bytes 1048592 | tf_op jit(solution)/shard_map/reduce_scatter | solution.py:224
  773.7 22.4 all-gather.18.cloned.1.call-done
  796.1 47.7 %all-gather.16.cloned.1.call-done = bf16[1024,1024]{1,0:T(8,128)(2,1)} async-done(((bf16[256,1024]{1,0:T(8,128)(2,1)}), bf16[1024,1024]{1,0:T(8,128)(2,1)}) %all-gather.16.cloned.1.call-update) | async-done | bytes 2097168 | tf_op jit(solution)/shard_map/all_gather | solution.py:176
  849.1 20.6 all-gather.20.cloned.1.call-done
  875.0 21.9 all-gather.22.cloned.1.call-done
  896.9 47.3 %all-gather.24.cloned.1.call-done = bf16[1024,1024]{1,0:T(8,128)(2,1)} async-done(((bf16[256,1024]{1,0:T(8,128)(2,1)}), bf16[1024,1024]{1,0:T(8,128)(2,1)}) %all-gather.24.cloned.1.call-update) | async-done | bytes 2097168 | tf_op jit(solution)/shard_map/all_gather | solution.py:242
  957.5 42.5 %reduce-scatter.17.cloned.1.call-done = bf16[256,1024]{1,0:T(8,128)(2,1)} async-done(((bf16[1024,1024]{1,0:T(8,128)(2,1)}), bf16[256,1024]{1,0:T(8,128)(2,1)}) %reduce-scatter.17.cloned.1.call-update) | async-done | bytes 524304 | tf_op jit(solution)/shard_map/reduce_scatter | solution.py:249
  1004.0 44.9 %all-gather.26.cloned.1.call-done = bf16[1024,1024]{1,0:T(8,128)(2,1)} async-done(((bf16[256,1024]{1,0:T(8,128)(2,1)}), bf16[1024,1024]{1,0:T(8,128)(2,1)}) %all-gather.26.cloned.1.call-update) | async-done | bytes 2097168 | tf_op jit(solution)/shard_map/all_gather | solution.py:259
  1066.9 834.0 %while.118 = (s32[]{:T(128)}, f32[2,128,256]{2,1,0:T(8,128)S(1)}, f32[16,64,2,128]{3,1,0,2:T(8,128)}, f32[16,64,2,128]{3,1,0,2:T(8,128)}, f32[16,64,2,256]{3,1,0...) while((s32[]{:T(128)}, f32[2,128,256]{2,1,0:T(8,128)S(1)}, ...), condition=%wide.region_24.26_spmd.clone.clone, body=%wide.region_13.25_spmd.clone.clone.sunk | while | flops 492090816 | bytes 8559127 | solution.py:131
  1278.8 9.8 custom-call.77
  1346.9 9.8 custom-call.78
  1399.0 9.8 custom-call.78
  1487.4 9.8 custom-call.77
  1555.3 9.8 custom-call.78
  1800.0 9.8 custom-call.77
  1868.1 9.8 custom-call.78
  2008.7 44.0 %reduce-scatter.19.cloned.1.call-done = bf16[256,1024]{1,0:T(8,128)(2,1)} async-done(((bf16[1024,1024]{1,0:T(8,128)(2,1)}), bf16[256,1024]{1,0:T(8,128)(2,1)}) %reduce-scatter.19.cloned.1.call-update) | async-done | bytes 524304 | tf_op jit(solution)/shard_map/reduce_scatter | solution.py:264
  2054.1 42.3 %all-reduce.21 = (f32[1024]{0:T(1024)}, f32[8]{0:T(128)}, f32[8]{0:T(128)}, f32[256]{0:T(256)}, f32[1024]{0:T(1024)}) all-reduce(f32[1024]{0:T(1024)S(1)} %get-tuple-element.2991, f32[8]{0:T(128)S(1)} %multiply_dynamic-update-slice_fusion, f32[8]{0:T(128)S(1)} %dynamic_update_slice.370, ...), channel_id=1, replica_groups=mesh['dp'=8,'tensor'=4] {'dp','tensor'}, use_global_device_ids=true, to_apply=%region_30.32 | all-reduce | flops 2320 | bytes 18560 | tf_op jit(solution)/shard_map/psum | solution.py:283
  2101.8 44.7 %reduce-scatter.27.cloned.1.call-done = f32[128,704]{0,1:T(8,128)} async-done(((f32[1024,704]{0,1:T(8,128)}), f32[128,704]{0,1:T(8,128)}) %reduce-scatter.27.cloned.1.call-update) | async-done | bytes 360464 | tf_op jit(solution)/shard_map/reduce_scatter | solution.py:295
  2146.6 48.5 %reduce-scatter.25.cloned.1.call-done = f32[128,704]{0,1:T(8,128)} async-done(((f32[1024,704]{0,1:T(8,128)}), f32[128,704]{0,1:T(8,128)}) %reduce-scatter.25.cloned.1.call-update) | async-done | bytes 360464 | tf_op jit(solution)/shard_map/reduce_scatter | solution.py:294
  2195.1 48.6 %reduce-scatter.29.cloned.1.call-done = f32[128,704]{0,1:T(8,128)} async-done(((f32[1024,704]{0,1:T(8,128)}), f32[128,704]{0,1:T(8,128)}) %reduce-scatter.29.cloned.1.call-update) | async-done | bytes 360464 | tf_op jit(solution)/shard_map/reduce_scatter | solution.py:296
  2243.7 125.6 %all-reduce.24.cloned.1.call-done = f32[4,4096]{1,0:T(4,128)} async-done(((f32[4,4096]{1,0:T(4,128)}), f32[4,4096]{1,0:T(4,128)}) %all-reduce.24.cloned.1.call-update) | async-done | bytes 65552 | tf_op jit(solution)/shard_map/psum | solution.py:283
  2369.2 66.8 %reduce-scatter.21.cloned.1.call-done = f32[128,1536]{1,0:T(8,128)} async-done(((f32[1024,1536]{1,0:T(8,128)}), f32[128,1536]{1,0:T(8,128)}) %reduce-scatter.21.cloned.1.call-update) | async-done | bytes 786448 | tf_op jit(solution)/shard_map/reduce_scatter | solution.py:287
  (1641 shorter events, 1468.1 us)
Async XLA Ops:
  7.2 16.9 copy-start.25
  7.2 52.4 %all-gather.10.cloned.1.call-start = ((), (), s32[]{:S(2)}) async-start(), calls=%async_computation.10 | async-start | bytes 2621440 | tf_op jit(solution)/shard_map/all_gather | solution.py:163
  11.1 81.4 %all-gather.12.cloned.1.call-start = ((), (), s32[]{:S(2)}) async-start(), calls=%async_computation.11 | async-start | bytes 3538944 | tf_op jit(solution)/shard_map/all_gather | solution.py:165
  11.9 675.0 %all-gather.14.cloned.1.call-start = ((), (), s32[]{:S(2)}) async-start(), calls=%async_computation.12 | async-start | bytes 1179648 | tf_op jit(solution)/shard_map/all_gather | solution.py:167
  12.6 756.1 %reduce-scatter.13.cloned.1.call-start = ((), (), s32[]{:S(2)}) async-start(), calls=%async_computation.13 | async-start | bytes 5242880 | tf_op jit(solution)/shard_map/reduce_scatter | solution.py:224
  23.6 38.5 %copy-start.26 = (bf16[1024,4]{0,1:T(4,128)(2,1)}, bf16[1024,4]{0,1:T(4,128)(2,1)S(1)}, u32[]{:S(2)}) copy-start(bf16[1024,4]{0,1:T(4,128)(2,1)S(1)} %all_gather.31) | copy-start | bytes 24580
  59.7 32.9 %copy-start.15 = (bf16[1024,1024]{1,0:T(8,128)(2,1)S(1)}, bf16[1024,1024]{1,0:T(8,128)(2,1)}, u32[]{:S(2)}) copy-start(bf16[1024,1024]{1,0:T(8,128)(2,1)} %all-gather.10.cloned.1.call-done) | copy-start | bytes 6291460
  62.3 37.9 %copy-start.19 = (f32[1024,2,1]{1,0,2:T(8,128)}, f32[1024,2,1]{1,0,2:T(8,128)S(1)}, u32[]{:S(2)}) copy-start(f32[1024,2,1]{1,0,2:T(8,128)S(1)} %copy.473) | copy-start | bytes 24580
  561.5 15.9 copy-start.39
  655.7 16.0 copy-start.39
  691.7 78.5 %copy-start.28 = (f32[1024]{0:T(1024)S(1)}, f32[1024]{0:T(1024)}, u32[]{:S(2)}) copy-start(f32[1024]{0:T(1024)} %param.32) | copy-start | bytes 12292
  691.7 104.4 %all-gather.18.cloned.1.call-start = ((), (), s32[]{:S(2)}) async-start(), calls=%async_computation.15 | async-start | bytes 1622016 | tf_op jit(solution)/shard_map/all_gather | solution.py:178
  692.3 151.5 %all-gather.16.cloned.1.call-start = ((), (), s32[]{:S(2)}) async-start(), calls=%async_computation.14 | async-start | bytes 2621440 | tf_op jit(solution)/shard_map/all_gather | solution.py:176
  771.2 98.5 %all-gather.20.cloned.1.call-start = ((), (), s32[]{:S(2)}) async-start(), calls=%async_computation.16 | async-start | bytes 1622016 | tf_op jit(solution)/shard_map/all_gather | solution.py:179
  772.0 124.9 %all-gather.22.cloned.1.call-start = ((), (), s32[]{:S(2)}) async-start(), calls=%async_computation.17 | async-start | bytes 1622016 | tf_op jit(solution)/shard_map/all_gather | solution.py:180
  772.7 171.4 %all-gather.24.cloned.1.call-start = ((), (), s32[]{:S(2)}) async-start(), calls=%async_computation.19 | async-start | bytes 2621440 | tf_op jit(solution)/shard_map/all_gather | solution.py:242
  773.5 226.6 %reduce-scatter.17.cloned.1.call-start = ((), (), s32[]{:S(2)}) async-start(), calls=%async_computation.20 | async-start | bytes 2621440 | tf_op jit(solution)/shard_map/reduce_scatter | solution.py:249
  957.5 91.4 %all-gather.26.cloned.1.call-start = ((), (), s32[]{:S(2)}) async-start(), calls=%async_computation.21 | async-start | bytes 2621440 | tf_op jit(solution)/shard_map/all_gather | solution.py:259
  1003.8 999.7 %reduce-scatter.31.cloned.1.call-start = ((), (), s32[]{:S(2)}) async-start(), calls=%async_computation.29 | async-start | bytes 589824
  1929.4 77.5 %reduce-scatter.23.cloned.1.call-start = ((), (), s32[]{:S(2)}) async-start(), calls=%async_computation.25 | async-start | bytes 2359296 | tf_op jit(solution)/shard_map/reduce_scatter | solution.py:291
  1934.0 118.7 %reduce-scatter.19.cloned.1.call-start = ((), (), s32[]{:S(2)}) async-start(), calls=%async_computation.22 | async-start | bytes 2621440 | tf_op jit(solution)/shard_map/reduce_scatter | solution.py:264
  1970.7 128.1 %reduce-scatter.15.cloned.1.call-start = ((), (), s32[]{:S(2)}) async-start(), calls=%async_computation.18 | async-start | bytes 2621440 | tf_op jit(solution)/shard_map/reduce_scatter | solution.py:235
  1975.8 170.8 %reduce-scatter.27.cloned.1.call-start = ((), (), s32[]{:S(2)}) async-start(), calls=%async_computation.27 | async-start | bytes 3244032 | tf_op jit(solution)/shard_map/reduce_scatter | solution.py:295
  1981.4 213.8 %reduce-scatter.25.cloned.1.call-start = ((), (), s32[]{:S(2)}) async-start(), calls=%async_computation.26 | async-start | bytes 3244032 | tf_op jit(solution)/shard_map/reduce_scatter | solution.py:294
  1986.7 257.0 %reduce-scatter.29.cloned.1.call-start = ((), (), s32[]{:S(2)}) async-start(), calls=%async_computation.28 | async-start | bytes 3244032 | tf_op jit(solution)/shard_map/reduce_scatter | solution.py:296
  1992.0 377.2 %all-reduce.24.cloned.1.call-start = ((), (), s32[]{:S(2)}) async-start(), calls=%async_computation.24 | async-start | bytes 131072 | tf_op jit(solution)/shard_map/psum | solution.py:283
  1992.8 443.3 %reduce-scatter.21.cloned.1.call-start = ((), (), s32[]{:S(2)}) async-start(), calls=%async_computation.23 | async-start | bytes 7077888 | tf_op jit(solution)/shard_map/reduce_scatter | solution.py:287
  2000.4 52.3 %copy-start.14 = (bf16[256,1024]{1,0:T(8,128)(2,1)S(1)}, bf16[256,1024]{1,0:T(8,128)(2,1)}, u32[]{:S(2)}) copy-start(bf16[256,1024]{1,0:T(8,128)(2,1)} %param.21) | copy-start | bytes 1572868
  2000.4 52.3 %copy-start.29 = (f32[1024]{0:T(1024)S(1)}, f32[1024]{0:T(1024)}, u32[]{:S(2)}) copy-start(f32[1024]{0:T(1024)} %param.24) | copy-start | bytes 12292
  2000.4 52.3 %copy-start.31 = (f32[256]{0:T(256)S(1)}, f32[256]{0:T(256)}, u32[]{:S(2)}) copy-start(f32[256]{0:T(256)} %copy-done.30) | copy-start | bytes 3076
  2001.5 97.3 %copy-start.21 = (bf16[256,1024]{1,0:T(8,128)(2,1)S(1)}, bf16[256,1024]{1,0:T(8,128)(2,1)}, u32[]{:S(2)}) copy-start(bf16[256,1024]{1,0:T(8,128)(2,1)} %param.23) | copy-start | bytes 1572868
  2001.5 97.3 %copy-start.22 = (bf16[256,1024]{1,0:T(8,128)(2,1)S(1)}, bf16[256,1024]{1,0:T(8,128)(2,1)}, u32[]{:S(2)}) copy-start(bf16[256,1024]{1,0:T(8,128)(2,1)} %reduce-scatter.17.cloned.1.call-done) | copy-start | bytes 1572868
  (62 other events, 372.5 us)
Sparse Core Ops, SparseCore 0:
  11.2 48.3 all-gather.9
  61.5 30.9 all-gather.11
  94.4 23.4 all-gather.13
  691.8 76.7 reduce-scatter.12
  770.4 25.7 all-gather.17
  798.1 45.6 all-gather.15
  845.7 23.9 all-gather.19
  871.6 25.1 all-gather.21
  898.4 45.6 all-gather.23
  957.6 42.4 reduce-scatter.16
  1004.0 44.8 all-gather.25
  1929.5 32.9 reduce-scatter.30
  1965.8 41.1 reduce-scatter.22
  2009.1 43.5 reduce-scatter.18
  2054.9 43.8 reduce-scatter.14
  2102.6 43.9 reduce-scatter.26
  2150.4 44.6 reduce-scatter.24
  2198.9 44.6 reduce-scatter.28
  2249.8 119.3 all-reduce.23
  2373.0 62.9 reduce-scatter.20
where the time goes:
time: 2470 us; the launch traced here: 2440 us
  waiting for transfers between devices  774 us (31%)
  other arithmetic  724 us (29%)
  matrix products  572 us (23%)
  local copies, waits for them, and re-layouts  280 us (11%)
  blocking collectives  52.7 us (2%)
  loops' own time  25.2 us (1%)
    another operation x112, other arithmetic, block_step(): jax.scipy.linalg.solve_triangular(system, (beta_h * visible_extent)[:, :,...  343 us
    another operation x64, other arithmetic, block_step(): jax.scipy.linalg.solve_triangular(system, beta_h[:, :, None] * value_h, l...  160 us
    psum x1, waiting for transfers between devices, local(): lax.psum((gain_in_part, gain_ffn_part, conv_full, alog_full, bias_full, d...  126 us
    dynamic_update_slice x144, local copies, waits for them, and re-layouts, delta_spans(): final_state, block_outs = lax.scan(block_step, initial, blocks_in)  84.9 us
    reduce_scatter x1, waiting for transfers between devices, local(): lax.psum_scatter(jnp.dot(gated, whole_out, preferred_element_type=jnp.flo...  76.3 us
    dot_general x48, matrix products, block_step(): jnp.einsum('hik,hjk->hij', query_per_head, key_per_head, precision=EXACT_...  75.3 us
    dot_general x48, matrix products, block_step(): jnp.einsum('sty,syo->sto', query_per_head, recurrent_carry_state, precisi...  74 us
    another operation x48, matrix products, block_step(): jax.scipy.linalg.solve_triangular(system, beta_h[:, :, None] * value_h, l...  67 us
  transfers between devices with their start and end apart: 20, of which 18 were waited for; matrix products, arithmetic and copies ran while one was open for 27% of the time, Pallas kernels for 0%

commit v1 on v0

v1 whole, which is shorter than its diff:
```python
import functools
import jax
import jax.numpy as jnp
from jax import lax
from jax.experimental import pallas as pl
from jax.experimental.pallas import tpu as pltpu

from jax.sharding import PartitionSpec as P

DK = 128
DV = 256
CONVW = 2 * DK + DV
HEADW = 2 * DK + 2 * DV
CHUNK = 128
EPSILON = 1e-06
F32 = jnp.float32
BF16 = jnp.bfloat16
NN = (((1,), (0,)), ((), ()))
NT = (((1,), (1,)), ((), ()))
TN = (((0,), (0,)), ((), ()))


def split(value):
    high = value.astype(BF16)
    return high, (value - high.astype(F32)).astype(BF16)


def dot1(left, right, dims=NN):
    return lax.dot_general(
        left.astype(BF16), right.astype(BF16), dims, preferred_element_type=F32
    )


def dot3(left, right, dims=NN):
    lh, ll = left if isinstance(left, tuple) else split(left)
    rh, rl = right if isinstance(right, tuple) else split(right)
    d = functools.partial(lax.dot_general, dimension_numbers=dims, preferred_element_type=F32)
    return d(lh, rh) + (d(lh, rl) + d(ll, rh))


def sigmoid(x):
    return 1.0 / (1.0 + jnp.exp(-x))


def softplus(x):
    return jnp.maximum(x, 0.0) + jnp.log(1.0 + jnp.exp(-jnp.abs(x)))


def place(shape, axis):
    return lax.broadcasted_iota(jnp.int32, shape, axis)


def cumulate(value, backwards=False):
    length = value.shape[0]
    row = place(value.shape, 0)
    step = 1
    while step < length:
        if backwards:
            moved = pltpu.roll(value, length - step, 0)
            value = value + jnp.where(row < length - step, moved, 0.0)
        else:
            moved = pltpu.roll(value, step, 0)
            value = value + jnp.where(row >= step, moved, 0.0)
        step *= 2
    return value


def conv_parts(before, rows, doc_before, docs):
    length = rows.shape[0]
    tall = jnp.concatenate([before, rows], axis=0)
    tall_docs = jnp.concatenate([doc_before, docs], axis=0)
    parts = [rows]
    for offset in range(1, 4):
        same = tall_docs[8 - offset : 8 - offset + length, :1] == docs[:, :1]
        parts.append(jnp.where(same, tall[8 - offset : 8 - offset + length], 0.0))
    return parts


def head_decay(cum, lane, docs, doc_row, doc_carried):
    square = docs.shape
    g_col = jnp.broadcast_to(cum[:, lane : lane + 1], square)
    g_row = jnp.transpose(g_col)
    row, col = place(square, 0), place(square, 1)
    seen = (row >= col) & (docs == doc_row)
    fade = jnp.where(seen, jnp.exp(jnp.where(seen, g_col - g_row, 0.0)), 0.0)
    strict = jnp.where(row > col, fade, 0.0)
    reach = jnp.where(docs == doc_carried, jnp.exp(g_col), 0.0)
    g_last = g_col[-1:, :]
    doc_last = docs[-1:, :]
    trail = jnp.where(docs == doc_last, jnp.exp(g_last - g_col), 0.0)
    keep = jnp.where(doc_last == doc_carried, jnp.exp(g_last), 0.0)
    return fade, strict, reach, trail, keep


def unit_lower_inverse(lower):
    square = lower.shape
    row, col = place(square, 0), place(square, 1)
    apart = row ^ col
    inverse = jnp.where(row == col, 1.0, jnp.where(apart == 1, -lower, 0.0))
    level = 1
    while (1 << level) < square[0]:
        part = jnp.where((apart >> level) == 1, lower, 0.0)
        pair = split(inverse)
        inverse = inverse - dot3(pair, dot3(part, pair))
        level += 1
    return inverse


def activations(proj_ref, before_ref, conv_ref, docs, doc_before, head):
    base = head * HEADW
    rows = proj_ref[:, base : base + CONVW]
    before = before_ref[:, base : base + CONVW]
    taps = conv_ref[:, head * CONVW : (head + 1) * CONVW]
    parts = conv_parts(before, rows, doc_before, docs)
    pre = sum(parts[s] * taps[s : s + 1] for s in range(4))
    gate = sigmoid(pre)
    post = pre * gate
    q_raw, k_raw, value = post[:, :DK], post[:, DK : 2 * DK], post[:, 2 * DK :]
    q_scale = lax.rsqrt(jnp.sum(q_raw * q_raw, axis=-1, keepdims=True) + EPSILON)
    k_scale = lax.rsqrt(jnp.sum(k_raw * k_raw, axis=-1, keepdims=True) + EPSILON)
    query = q_raw * q_scale * DK ** (-0.5)
    key = k_raw * k_scale
    return parts, taps, pre, gate, q_raw, k_raw, q_scale, k_scale, query, key, value


def doc_context(doc_ref, doc_before_ref, chunk):
    docs = doc_ref[...]
    doc_before = jnp.where(chunk > 0, doc_before_ref[...], -1.0)
    return docs, jnp.transpose(docs), doc_before, doc_before[-1:, :]


def forward_kernel(
    heads, proj_ref, before_ref, doc_ref, doc_before_ref, conv_ref, vec_ref, gain_ref,
    gated_ref, recur_ref, inverse_ref, solved_ref, mix_ref, key_ref, tilde_ref, start_ref, state,
):
    chunk = pl.program_id(0)

    @pl.when(chunk == 0)
    def _():
        state[...] = jnp.zeros_like(state)

    docs, doc_row, doc_before, doc_carried = doc_context(doc_ref, doc_before_ref, chunk)
    pair = proj_ref[:, heads * HEADW :]
    decay = -vec_ref[0:1, :] * softplus(pair + vec_ref[1:2, :])
    write = sigmoid(pair)
    cum = cumulate(decay)
    eye = place(docs.shape, 0) == place(docs.shape, 1)
    for head in range(heads):
        acts = activations(proj_ref, before_ref, conv_ref, docs, doc_before, head)
        query, key, value = acts[8:]
        fade, strict, reach, trail, keep = head_decay(cum, 2 * head, docs, doc_row, doc_carried)
        beta = write[:, 2 * head + 1 : 2 * head + 2]
        key_pair = split(key)
        both = dot3(jnp.concatenate([key, query], axis=0), key_pair, NT)
        key_key = both[:CHUNK] * strict
        mix = both[CHUNK:] * fade
        inverse = unit_lower_inverse(beta * key_key)
        rhs = jnp.concatenate([beta * reach * key, beta * value], axis=1)
        solved = dot3(inverse, rhs)
        trailing = jnp.transpose(trail * key)
        outer = dot3(jnp.concatenate([trailing, mix], axis=0), solved)
        step = jnp.where(eye, keep, 0.0) - outer[:CHUNK, :DK]
        q_tilde = reach * query - outer[CHUNK:, :DK]
        tilde = jnp.concatenate([step, q_tilde], axis=0)
        start = state[head]
        moved = dot3(tilde, start)
        state[head] = moved[:CHUNK] + outer[:CHUNK, DK:]
        recurrent = moved[CHUNK:] + outer[CHUNK:, DK:]
        inverse_ref[0, head] = inverse
        solved_ref[0, head] = solved
        mix_ref[0, head] = mix
        key_ref[0, head] = key_key
        tilde_ref[0, head] = tilde
        start_ref[0, head] = start
        recur_ref[:, head * DV : (head + 1) * DV] = recurrent
        scale = lax.rsqrt(jnp.mean(recurrent * recurrent, axis=-1, keepdims=True) + EPSILON)
        z = proj_ref[:, head * HEADW + CONVW : (head + 1) * HEADW]
        gated = recurrent * scale * gain_ref[...] * (z * sigmoid(z))
        gated_ref[:, head * DV : (head + 1) * DV] = gated.astype(BF16)


def backward_kernel(
    heads, chunks, proj_ref, before_ref, doc_ref, doc_before_ref, doc_after_ref,
    conv_ref, vec_ref, gain_ref, recur_ref, inverse_ref, solved_ref, mix_ref, key_ref, tilde_ref,
    start_ref, grad_ref,
    d_proj_ref, d_conv_ref, d_vec_ref, d_gain_ref, d_state, d_after,
):
    step_index = pl.program_id(0)
    chunk = chunks - 1 - step_index

    @pl.when(step_index == 0)
    def _():
        d_state[...] = jnp.zeros_like(d_state)
        d_after[...] = jnp.zeros_like(d_after)
        d_conv_ref[...] = jnp.zeros_like(d_conv_ref)
        d_vec_ref[...] = jnp.zeros_like(d_vec_ref)
        d_gain_ref[...] = jnp.zeros_like(d_gain_ref)

    docs, doc_row, doc_before, doc_carried = doc_context(doc_ref, doc_before_ref, chunk)
    tall_docs = jnp.concatenate([docs, doc_after_ref[...]], axis=0)
    pair = proj_ref[:, heads * HEADW :]
    shifted = pair + vec_ref[1:2, :]
    decay = -vec_ref[0:1, :] * softplus(shifted)
    write = sigmoid(pair)
    cum = cumulate(decay)
    lanes = place(docs.shape, 1)
    last_row = place(docs.shape, 0) == CHUNK - 1
    d_cum = jnp.zeros_like(docs)
    d_write = jnp.zeros_like(docs)
    for head in range(heads):
        acts = activations(proj_ref, before_ref, conv_ref, docs, doc_before, head)
        parts, taps, pre, gate, q_raw, k_raw, q_scale, k_scale, query, key, value = acts
        fade, strict, reach, trail, keep = head_decay(cum, 2 * head, docs, doc_row, doc_carried)
        beta = write[:, 2 * head + 1 : 2 * head + 2]
        grad = grad_ref[:, head * DV : (head + 1) * DV].astype(F32)
        recurrent = recur_ref[:, head * DV : (head + 1) * DV]
        scale = lax.rsqrt(jnp.mean(recurrent * recurrent, axis=-1, keepdims=True) + EPSILON)
        z = proj_ref[:, head * HEADW + CONVW : (head + 1) * HEADW]
        z_gate = sigmoid(z)
        unit = recurrent * scale
        gain = gain_ref[...]
        d_normed = grad * (z * z_gate)
        d_z = grad * unit * gain * (z_gate * (1.0 + z * (1.0 - z_gate)))
        d_gain_ref[...] += jnp.sum(d_normed * unit, axis=0, keepdims=True)
        weighted = d_normed * gain
        d_out = scale * (weighted - unit * jnp.mean(weighted * unit, axis=-1, keepdims=True))
        inverse = inverse_ref[0, head]
        solved = solved_ref[0, head]
        mix = mix_ref[0, head]
        key_key = key_ref[0, head]
        tilde = tilde_ref[0, head]
        start = start_ref[0, head]
        d_next = d_state[head]
        flow = jnp.concatenate([d_next, d_out], axis=0)
        d_state[head] = dot3(tilde, flow, TN)
        start_pair = split(start)
        delta = solved[:, DK:] - dot3(solved[:, :DK], start_pair)
        trailing = trail * key
        d_delta = dot3(jnp.concatenate([trailing, jnp.transpose(mix)], axis=1), flow)
        d_rhs = dot3(inverse, d_delta, TN)
        grads = jnp.concatenate([d_out, d_rhs], axis=0)
        outer = dot3(grads, delta, NT)
        onto = dot3(grads, start_pair, NT)
        d_mix = outer[:CHUNK]
        d_lower = -outer[CHUNK:]
        from_next = dot3(delta, d_next, NT)
        mixed = d_mix * fade
        lowered = d_lower * strict * beta
        d_query = reach * onto[:CHUNK] + dot3(mixed, key)
        d_key = (
            dot3(jnp.transpose(mixed), query)
            + dot3(lowered + jnp.transpose(lowered), key)
            + trail * from_next
            - beta * reach * onto[CHUNK:]
        )
        d_value = beta * d_rhs
        crossed = d_lower * key_key
        net = d_mix * mix + beta * crossed
        reach_col = reach[:, :1]
        sum_query = jnp.sum(query * onto[:CHUNK], axis=-1, keepdims=True)
        sum_key = jnp.sum(key * onto[CHUNK:], axis=-1, keepdims=True)
        sum_trail = jnp.sum(trailing * from_next, axis=-1, keepdims=True)
        d_beta = (
            jnp.sum(crossed, axis=-1, keepdims=True)
            + jnp.sum(d_rhs * value, axis=-1, keepdims=True)
            - reach_col * sum_key
        )
        d_g = (
            jnp.sum(net - jnp.transpose(net), axis=-1, keepdims=True)
            + reach_col * sum_query
            - beta * reach_col * sum_key
            - sum_trail
        )
        kept = keep[:, :1] * jnp.sum(
            jnp.sum(start * d_next, axis=-1, keepdims=True), axis=0, keepdims=True
        )
        d_last = jnp.sum(sum_trail, axis=0, keepdims=True) + kept
        d_g = d_g + jnp.where(last_row[:, :1], d_last, 0.0)
        d_cum = jnp.where(lanes == 2 * head, d_g, d_cum)
        d_write = jnp.where(lanes == 2 * head + 1, d_beta, d_write)
        d_q_raw = (
            (d_query - q_raw * (q_scale * q_scale) * jnp.sum(d_query * q_raw, axis=-1, keepdims=True))
            * q_scale * DK ** (-0.5)
        )
        d_k_raw = (
            d_key - k_raw * (k_scale * k_scale) * jnp.sum(d_key * k_raw, axis=-1, keepdims=True)
        ) * k_scale
        d_post = jnp.concatenate([d_q_raw, d_k_raw, d_value], axis=1)
        d_pre = d_post * gate * (1.0 + pre * (1.0 - gate))
        columns = slice(head * CONVW, (head + 1) * CONVW)
        d_conv_ref[:, columns] += jnp.concatenate(
            [jnp.sum(d_pre * parts[s], axis=0, keepdims=True) for s in range(4)], axis=0
        )
        tall = jnp.concatenate([d_pre, d_after[:, columns]], axis=0)
        d_rows = d_pre * taps[0:1]
        for offset in range(1, 4):
            same = tall_docs[offset : offset + CHUNK, :1] == docs[:, :1]
            d_rows = d_rows + jnp.where(
                same, tall[offset : offset + CHUNK] * taps[offset : offset + 1], 0.0
            )
        d_after[:, columns] = d_pre[:8]
        d_proj_ref[:, head * HEADW : head * HEADW + CONVW] = d_rows.astype(BF16)
        d_proj_ref[:, head * HEADW + CONVW : (head + 1) * HEADW] = d_z.astype(BF16)
    d_decay = cumulate(d_cum, backwards=True)
    d_shifted = d_decay * -vec_ref[0:1, :] * sigmoid(shifted)
    d_written = d_write * write * (1.0 - write)
    used = lanes < 2 * heads
    even = (lanes & 1) == 0
    d_proj_ref[:, heads * HEADW :] = jnp.where(used, jnp.where(even, d_shifted, d_written), 0.0).astype(BF16)
    d_vec_ref[0:1, :] += jnp.sum(d_decay * decay, axis=0, keepdims=True)
    d_vec_ref[1:2, :] += jnp.sum(d_shifted, axis=0, keepdims=True)


def chunk_specs(heads, chunks, where):
    per8 = CHUNK // 8

    def rows(width):
        return pl.BlockSpec((CHUNK, width), lambda c: (where(c), 0))

    def before(width):
        return pl.BlockSpec((8, width), lambda c: (jnp.maximum(where(c) * per8 - 1, 0), 0))

    def after(width):
        return pl.BlockSpec(
            (8, width), lambda c: (jnp.minimum((where(c) + 1) * per8, chunks * per8 - 1), 0)
        )

    def whole(shape):
        return pl.BlockSpec(shape, lambda c: (0,) * len(shape))

    def saved(height, width):
        return pl.BlockSpec((1, heads, height, width), lambda c: (where(c), 0, 0, 0))

    return rows, before, after, whole, saved


def saved_shapes(heads, chunks):
    sizes = ((CHUNK, CHUNK), (CHUNK, DK + DV), (CHUNK, CHUNK), (CHUNK, CHUNK), (2 * CHUNK, DK), (DK, DV))
    return sizes


def mixer_forward(projected, docs, taps, vectors, gain, interpret=False):
    length, width = projected.shape
    heads = (width - CHUNK) // HEADW
    chunks = length // CHUNK
    rows, before, after, whole, saved = chunk_specs(heads, chunks, lambda c: c)
    sizes = saved_shapes(heads, chunks)
    return pl.pallas_call(
        functools.partial(forward_kernel, heads),
        grid=(chunks,),
        in_specs=[
            rows(width), before(width), rows(CHUNK), before(CHUNK),
            whole((4, heads * CONVW)), whole((8, CHUNK)), whole((1, DV)),
        ],
        out_specs=[rows(heads * DV), rows(heads * DV)] + [saved(*s) for s in sizes],
        out_shape=[
            jax.ShapeDtypeStruct((length, heads * DV), BF16),
            jax.ShapeDtypeStruct((length, heads * DV), F32),
        ]
        + [jax.ShapeDtypeStruct((chunks, heads) + s, F32) for s in sizes],
        scratch_shapes=[pltpu.VMEM((heads, DK, DV), F32)],
        name="mixer_forward",
        interpret=interpret,
    )(projected, projected, docs, docs, taps, vectors, gain)


def mixer_backward(projected, docs, taps, vectors, gain, kept, grad, interpret=False):
    length, width = projected.shape
    heads = (width - CHUNK) // HEADW
    chunks = length // CHUNK
    rows, before, after, whole, saved = chunk_specs(heads, chunks, lambda c: chunks - 1 - c)
    sizes = saved_shapes(heads, chunks)
    return pl.pallas_call(
        functools.partial(backward_kernel, heads, chunks),
        grid=(chunks,),
        in_specs=[
            rows(width), before(width), rows(CHUNK), before(CHUNK), after(CHUNK),
            whole((4, heads * CONVW)), whole((8, CHUNK)), whole((1, DV)), rows(heads * DV),
        ]
        + [saved(*s) for s in sizes]
        + [rows(heads * DV)],
        out_specs=[
            rows(width), whole((4, heads * CONVW)), whole((8, CHUNK)), whole((1, DV)),
        ],
        out_shape=[
            jax.ShapeDtypeStruct((length, width), BF16),
            jax.ShapeDtypeStruct((4, heads * CONVW), F32),
            jax.ShapeDtypeStruct((8, CHUNK), F32),
            jax.ShapeDtypeStruct((1, DV), F32),
        ],
        scratch_shapes=[pltpu.VMEM((heads, DK, DV), F32), pltpu.VMEM((8, heads * CONVW), F32)],
        name="mixer_backward",
        interpret=interpret,
    )(projected, projected, docs, docs, docs, taps, vectors, gain, *kept, grad)


def rms_rows(values, gain):
    return values * lax.rsqrt(jnp.mean(values * values, axis=-1, keepdims=True) + EPSILON) * gain


def rms_back(values, gain, grad_normed):
    scale = lax.rsqrt(jnp.mean(values * values, axis=-1, keepdims=True) + EPSILON)
    weighted = grad_normed * gain
    inner = jnp.mean(weighted * values, axis=-1, keepdims=True)
    grad_values = scale * weighted - values * scale * scale * scale * inner
    return (grad_values, jnp.sum(grad_normed * values * scale, axis=0))


def times_transposed(left, right):
    return lax.dot_general(left, right, NT, preferred_element_type=F32)


def transposed_times(left, right):
    return lax.dot_general(left, right, TN, preferred_element_type=F32)


def ffn_front(resid, norm_ffn, w_gate, w_up, w_down):
    normed = rms_rows(resid, norm_ffn).astype(jnp.bfloat16)
    seq_rows = lax.all_gather(normed, "tensor", axis=0, tiled=True)
    whole_gate, whole_up, whole_down = (
        lax.all_gather(w_gate, "dp", axis=0, tiled=True),
        lax.all_gather(w_up, "dp", axis=0, tiled=True),
        lax.all_gather(w_down, "dp", axis=1, tiled=True),
    )
    gate_pre = jnp.dot(seq_rows, whole_gate, preferred_element_type=jnp.float32)
    up_pre = jnp.dot(seq_rows, whole_up, preferred_element_type=jnp.float32)
    hidden = (jax.nn.silu(gate_pre) * up_pre).astype(jnp.bfloat16)
    return (seq_rows, whole_gate, whole_up, whole_down, gate_pre, up_pre, hidden)


def local(
    inputs,
    segments,
    cotangent,
    norm_in,
    w_in,
    w_alpha_beta,
    conv_weight,
    a_log,
    dt_bias,
    out_gain,
    w_out,
    norm_ffn,
    w_gate,
    w_up,
    w_down,
):
    doc_ids = segments[0]
    part_index = lax.axis_index("tensor")
    head_count = a_log.shape[0] // lax.axis_size("tensor")
    conv_width = head_count * (2 * DK + DV)
    conv_mine = lax.dynamic_slice_in_dim(conv_weight, part_index * conv_width, conv_width, 1)
    alog_mine = lax.dynamic_slice_in_dim(a_log, part_index * head_count, head_count, 0)
    bias_mine = lax.dynamic_slice_in_dim(dt_bias, part_index * head_count, head_count, 0)

    length = doc_ids.shape[0]
    docs = jnp.broadcast_to(doc_ids.astype(F32)[:, None], (length, CHUNK))
    vectors = jnp.zeros((8, CHUNK), F32)
    vectors = vectors.at[0, 0 : 2 * head_count : 2].set(jnp.exp(alog_mine))
    vectors = vectors.at[1, 0 : 2 * head_count : 2].set(bias_mine)
    gain_row = out_gain[None, :]

    input_rows = inputs.astype(jnp.float32)
    normed = rms_rows(input_rows, norm_in).astype(BF16)
    seq_rows = lax.all_gather(normed, "tensor", axis=0, tiled=True)
    joined = jnp.concatenate(
        [w_in, jnp.pad(w_alpha_beta, ((0, 0), (0, CHUNK - w_alpha_beta.shape[1])))], axis=1
    )
    whole_in = lax.all_gather(joined, "dp", axis=0, tiled=True)
    whole_out = lax.all_gather(w_out, "dp", axis=1, tiled=True)
    projected = jnp.dot(seq_rows, whole_in, preferred_element_type=F32)
    gated, *kept = mixer_forward(projected, docs, conv_mine, vectors, gain_row)
    resid = input_rows + lax.psum_scatter(
        jnp.dot(gated, whole_out, preferred_element_type=jnp.float32),
        "tensor",
        scatter_dimension=0,
        tiled=True,
    )
    ffn_seq, whole_gate, whole_up, whole_down, gate_pre, up_pre, hidden = ffn_front(
        resid, norm_ffn, w_gate, w_up, w_down
    )
    output = (
        resid
        + lax.psum_scatter(
            jnp.dot(hidden, whole_down, preferred_element_type=jnp.float32).astype(jnp.bfloat16),
            "tensor",
            scatter_dimension=0,
            tiled=True,
        ).astype(jnp.float32)
    ).astype(jnp.bfloat16)
    back_seq = lax.all_gather(cotangent, "tensor", axis=0, tiled=True)
    d_hidden = times_transposed(back_seq, whole_down)
    sigmoid_gate = jax.nn.sigmoid(gate_pre)
    d_up = (d_hidden * gate_pre * sigmoid_gate).astype(jnp.bfloat16)
    d_gate = (d_hidden * up_pre * sigmoid_gate * (1.0 + gate_pre * (1.0 - sigmoid_gate))).astype(
        jnp.bfloat16
    )
    d_normed_ffn = lax.psum_scatter(
        (times_transposed(d_gate, whole_gate) + times_transposed(d_up, whole_up)).astype(
            jnp.bfloat16
        ),
        "tensor",
        scatter_dimension=0,
        tiled=True,
    ).astype(jnp.float32)
    resid_from_norm, gain_ffn_part = rms_back(resid, norm_ffn, d_normed_ffn)
    d_resid = cotangent.astype(jnp.float32) + resid_from_norm
    mixer_back_seq = lax.all_gather(d_resid.astype(jnp.bfloat16), "tensor", axis=0, tiled=True)
    d_gated = times_transposed(mixer_back_seq, whole_out)
    d_projected, d_conv, d_vectors, d_gain_row = mixer_backward(
        projected, docs, conv_mine, vectors, gain_row, kept, d_gated
    )
    d_alog = d_vectors[0, 0 : 2 * head_count : 2]
    d_bias = d_vectors[1, 0 : 2 * head_count : 2]
    d_gain_out = d_gain_row[0]
    d_normed_in = lax.psum_scatter(
        times_transposed(d_projected, whole_in).astype(BF16),
        "tensor",
        scatter_dimension=0,
        tiled=True,
    ).astype(jnp.float32)
    input_from_norm, gain_in_part = rms_back(input_rows, norm_in, d_normed_in)
    d_inputs = d_resid + input_from_norm
    conv_full = lax.dynamic_update_slice_in_dim(
        jnp.zeros(conv_weight.shape, jnp.float32), d_conv, part_index * conv_width, 1
    )
    alog_full = lax.dynamic_update_slice_in_dim(
        jnp.zeros(a_log.shape, jnp.float32), d_alog, part_index * head_count, 0
    )
    bias_full = lax.dynamic_update_slice_in_dim(
        jnp.zeros(dt_bias.shape, jnp.float32), d_bias, part_index * head_count, 0
    )
    small_sums = lax.psum(
        (gain_in_part, gain_ffn_part, conv_full, alog_full, bias_full, d_gain_out), ("dp", "tensor")
    )
    owned_joined, owned_out, owned_gate, owned_up, owned_down = (
        lax.psum_scatter(
            transposed_times(seq_rows, d_projected), "dp", scatter_dimension=0, tiled=True
        ),
        lax.psum_scatter(
            transposed_times(mixer_back_seq, gated), "dp", scatter_dimension=0, tiled=True
        ),
        lax.psum_scatter(transposed_times(ffn_seq, d_gate), "dp", scatter_dimension=0, tiled=True),
        lax.psum_scatter(transposed_times(ffn_seq, d_up), "dp", scatter_dimension=0, tiled=True),
        lax.psum_scatter(transposed_times(back_seq, hidden), "dp", scatter_dimension=0, tiled=True),
    )
    return (
        output,
        d_inputs,
        small_sums[0],
        owned_joined[:, : w_in.shape[1]],
        owned_joined[:, w_in.shape[1] : w_in.shape[1] + w_alpha_beta.shape[1]],
        small_sums[2],
        small_sums[3],
        small_sums[4],
        small_sums[5],
        jnp.transpose(owned_out),
        small_sums[1],
        owned_gate,
        owned_up,
        jnp.transpose(owned_down),
    )


def solution(mesh):
    return jax.shard_map(
        local,
        mesh=mesh,
        in_specs=(
            P(("dp", "tensor"), None),
            P("dp", None),
            P(("dp", "tensor"), None),
            P(),
            P("dp", "tensor"),
            P("dp", "tensor"),
            P(),
            P(),
            P(),
            P(),
            P("tensor", "dp"),
            P(),
            P("dp", "tensor"),
            P("dp", "tensor"),
            P("tensor", "dp"),
        ),
        out_specs=(
            P(("dp", "tensor"), None),
            P(("dp", "tensor"), None),
            P(),
            P("dp", "tensor"),
            P("dp", "tensor"),
            P(),
            P(),
            P(),
            P(),
            P("tensor", "dp"),
            P(),
            P("dp", "tensor"),
            P("dp", "tensor"),
            P("tensor", "dp"),
        ),
        check_vma=False,
    )
```

time: 2470 us -> 1010 us (0.41)
  other arithmetic: 724 us -> 14.7 us
  matrix products: 572 us -> 87.3 us
  local copies, waits for them, and re-layouts: 280 us -> 12.3 us
  Pallas kernels: 0 us -> 85.3 us
  loops' own time: 25.2 us -> 0 us
    another operation x239 -> x0, other arithmetic: 510 us -> none  [the longest x112 343 us: block_step(): jax.scipy.linalg.solve_triangular(system, (beta_h * visible_extent)[:, :,...]
    dot_general x333 -> x11, matrix products: 461 us -> 67.1 us  [the longest x5 29.8 us: transposed_times(): return lax.dot_general(left, right, TN, preferred_element_type=F32)]
    another operation x96 -> x0, matrix products: 89.1 us -> none  [the longest x48 67 us: block_step(): jax.scipy.linalg.solve_triangular(system, beta_h[:, :, None] * value_h, l...]
    pallas_call x0 -> x2, Pallas kernels: none -> 85.3 us  [the longest x1 53.8 us: mixer_forward(): pl.pallas_call(functools.partial(forward_kernel, heads), grid=(chunks,),...]
    dynamic_update_slice x144 -> x2, local copies, waits for them, and re-layouts: 84.9 us -> 0.12 us  [the longest x1 0.1 us: local(): lax.dynamic_update_slice_in_dim(jnp.zeros(a_log.shape, jnp.float32), d_al...]
    reduce_sum x71 -> x0, other arithmetic: 71.3 us -> none  [the longest x16 18.3 us: block_step(): visible_extent[:, :, None]]
    dynamic_update_slice x66 -> x0, other arithmetic: 56.6 us -> none  [the longest x64 56.4 us: delta_spans(): final_state, block_outs = lax.scan(block_step, initial, blocks_in)]
    slice x29 -> x4, local copies, waits for them, and re-layouts: 60 us -> 4.52 us  [the longest x1 2.07 us: local(): owned_joined[:, :w_in.shape[1]]]
  transfers between devices with their start and end apart: 20 -> 19, of which waited for: 18 -> 17; matrix products, arithmetic and copies ran while one was open for 27% -> 8% of each run, Pallas kernels for 0% -> 8%
where the time goes in v1:
time: 1010 us
  waiting for transfers between devices  750 us (74%)
  matrix products  87.3 us (9%)
  Pallas kernels  85.3 us (8%)
  blocking collectives  40.1 us (4%)
  other arithmetic  14.7 us (1%)
  between operations  14.7 us (1%)
  local copies, waits for them, and re-layouts  12.3 us (1%)
    psum x1, waiting for transfers between devices, local(): lax.psum((gain_in_part, gain_ffn_part, conv_full, alog_full, bias_full, d...  126 us
    reduce_scatter x1, waiting for transfers between devices, local(): lax.psum_scatter(jnp.dot(gated, whole_out, preferred_element_type=jnp.flo...  76.3 us
    pallas_call x1, Pallas kernels, mixer_forward(): pl.pallas_call(functools.partial(forward_kernel, heads), grid=(chunks,),...  53.8 us
    reduce_scatter x1, waiting for transfers between devices, local(): lax.psum_scatter(transposed_times(ffn_seq, d_up), 'dp', scatter_dimension...  48.6 us
    reduce_scatter x1, waiting for transfers between devices, local(): lax.psum_scatter(transposed_times(back_seq, hidden), 'dp', scatter_dimens...  48.5 us
    all_gather x1, waiting for transfers between devices, ffn_front(): seq_rows = lax.all_gather(normed, 'tensor', axis=0, tiled=True)  47.7 us
    all_gather x1, waiting for transfers between devices, local(): back_seq = lax.all_gather(cotangent, 'tensor', axis=0, tiled=True)  47.3 us
    reduce_scatter x1, waiting for transfers between devices, local(): lax.psum_scatter(transposed_times(ffn_seq, d_gate), 'dp', scatter_dimensi...  45 us
  transfers between devices with their start and end apart: 19, of which 17 were waited for; matrix products, arithmetic and copies ran while one was open for 8% of the time, Pallas kernels for 8%

profile of v1, /device:TPU:0, one launch (start us, length us, event | category | flops | bytes accessed | tf_op | source)
XLA Modules:
  0.0 1005.4 jit_solution(16240285373326339461)
XLA Ops:
  14.6 44.6 %all-gather.10.cloned.1.call-done = bf16[1024,1024]{1,0:T(8,128)(2,1)} async-done(((bf16[256,1024]{1,0:T(8,128)(2,1)}), bf16[1024,1024]{1,0:T(8,128)(2,1)}) %all-gather.10.cloned.1.call-update) | async-done | bytes 2097168 | tf_op jit(solution)/shard_map/all_gather | solution.py:465
  59.2 34.6 %all-gather.12.cloned.1.call-done = bf16[1024,1664]{1,0:T(8,128)(2,1)} async-done(((bf16[128,1664]{1,0:T(8,128)(2,1)}), bf16[1024,1664]{1,0:T(8,128)(2,1)}) %all-gather.12.cloned.1.call-update) | async-done | bytes 3407888 | tf_op jit(solution)/shard_map/all_gather | solution.py:469
  93.8 9.3 fusion.22.proj_ref.before_ref
  104.2 53.8 %mixer_forward.1 = (bf16[1024,512]{1,0:T(8,128)(2,1)}, f32[1024,512]{1,0:T(8,128)}, f32[8,2,128,128]{3,2,1,0:T(8,128)}, f32[8,2,128,384]{3,2,1,0:T(8,128)}, f32[...) custom-call(f32[1024,1664]{1,0:T(8,128)} %fusion.22.proj_ref.before_, ...), custom_call_target="tpu_custom_call" | custom-call | tf_op jit(solution)/shard_map/mixer_forward/pallas_call | solution.py:348
  158.0 4.8 fusion.23
  163.5 76.3 %reduce-scatter.10.cloned.1.call-done = f32[256,1024]{1,0:T(8,128)} async-done(((f32[1024,1024]{1,0:T(8,128)}), f32[256,1024]{1,0:T(8,128)}) %reduce-scatter.10.cloned.1.call-update) | async-done | bytes 1048592 | tf_op jit(solution)/shard_map/reduce_scatter | solution.py:473
  244.6 22.6 %all-gather.18.cloned.1.call-done = bf16[1024,704]{0,1:T(8,128)(2,1)} async-done(((bf16[128,704]{0,1:T(8,128)(2,1)}), bf16[1024,704]{0,1:T(8,128)(2,1)}) %all-gather.18.cloned.1.call-update) | async-done | bytes 1441808 | tf_op jit(solution)/shard_map/all_gather | solution.py:421
  267.2 47.7 %all-gather.16.cloned.1.call-done = bf16[1024,1024]{1,0:T(8,128)(2,1)} async-done(((bf16[256,1024]{1,0:T(8,128)(2,1)}), bf16[1024,1024]{1,0:T(8,128)(2,1)}) %all-gather.16.cloned.1.call-update) | async-done | bytes 2097168 | tf_op jit(solution)/shard_map/all_gather | solution.py:419
  314.9 5.3 fusion.24
  320.2 20.7 %all-gather.20.cloned.1.call-done = bf16[1024,704]{0,1:T(8,128)(2,1)} async-done(((bf16[128,704]{0,1:T(8,128)(2,1)}), bf16[1024,704]{0,1:T(8,128)(2,1)}) %all-gather.20.cloned.1.call-update) | async-done | bytes 1441808 | tf_op jit(solution)/shard_map/all_gather | solution.py:422
  340.8 5.2 fusion.25
  346.1 21.9 %all-gather.22.cloned.1.call-done = bf16[704,1024]{1,0:T(8,128)(2,1)} async-done(((bf16[704,128]{1,0:T(8,128)(2,1)}), bf16[704,1024]{1,0:T(8,128)(2,1)}) %all-gather.22.cloned.1.call-update) | async-done | bytes 1441808 | tf_op jit(solution)/shard_map/all_gather | solution.py:423
  368.0 47.3 %all-gather.24.cloned.1.call-done = bf16[1024,1024]{1,0:T(8,128)(2,1)} async-done(((bf16[256,1024]{1,0:T(8,128)(2,1)}), bf16[1024,1024]{1,0:T(8,128)(2,1)}) %all-gather.24.cloned.1.call-update) | async-done | bytes 2097168 | tf_op jit(solution)/shard_map/all_gather | solution.py:491
  415.2 7.5 multiply_convert_fusion
  430.5 42.5 %reduce-scatter.14.cloned.1.call-done = bf16[256,1024]{1,0:T(8,128)(2,1)} async-done(((bf16[1024,1024]{1,0:T(8,128)(2,1)}), bf16[256,1024]{1,0:T(8,128)(2,1)}) %reduce-scatter.14.cloned.1.call-update) | async-done | bytes 524304 | tf_op jit(solution)/shard_map/reduce_scatter | solution.py:498
  476.7 45.0 %all-gather.26.cloned.1.call-done = bf16[1024,1024]{1,0:T(8,128)(2,1)} async-done(((bf16[256,1024]{1,0:T(8,128)(2,1)}), bf16[1024,1024]{1,0:T(8,128)(2,1)}) %all-gather.26.cloned.1.call-update) | async-done | bytes 2097168 | tf_op jit(solution)/shard_map/all_gather | solution.py:508
  526.4 4.5 fusion.27.grad_ref
  530.9 31.5 %mixer_backward.1 = (bf16[1024,1664]{1,0:T(8,128)(2,1)}, f32[4,1024]{1,0:T(4,128)}, f32[8,128]{1,0:T(8,128)}, f32[1,256]{1,0:T(1,128)}) custom-call(f32[1024,1664]{1,0:T(8,128)} %fusion.22.proj_ref.before_ref, f32[1024,1664]{1,0:T(8,128)} %fusion.22.proj_ref.before_ref, f32[1024,128]{1,0:T(8,128)} %broadcast_in_dim.8.doc_ref.doc_before_ref.doc_after_ref, ...), custom_call_target="tpu_custom_call" | custom-call | tf_op jit(solution)/shard_map/mixer_backward/pallas_call | solution.py:373
  562.4 8.3 convolution_convert_fusion
  570.8 4.9 convolution_convert_fusion.1
  576.0 9.4 fusion.28
  585.6 5.3 fusion.30
  590.9 5.3 fusion.31
  596.3 5.3 convolution_bitcast_fusion
  605.8 7.5 reduce-scatter.16.cloned.1.call-done
  614.7 43.6 %reduce-scatter.12.cloned.1.call-done = bf16[256,1024]{1,0:T(8,128)(2,1)} async-done(((bf16[1024,1024]{1,0:T(8,128)(2,1)}), bf16[256,1024]{1,0:T(8,128)(2,1)}) %reduce-scatter.12.cloned.1.call-update) | async-done | bytes 524304 | tf_op jit(solution)/shard_map/reduce_scatter | solution.py:484
  661.4 40.1 %all-reduce.3 = (f32[1024]{0:T(1024)}, f32[8]{0:T(128)}, f32[8]{0:T(128)}, f32[256]{0:T(256)}, f32[1024]{0:T(1024)}) all-reduce(f32[1024]{0:T(1024)S(1)} %get-tuple-element.54, f32[8]{0:T(128)S(1)} %bitcast_dynamic-update-slice_fusion.1, ...), channel_id=1, replica_groups=mesh['dp'=8,'tensor'=4] {'dp','tensor'}, use_global_device_ids=true, to_apply=%region_11.12 | all-reduce | flops 2320 | bytes 18560 | tf_op jit(solution)/shard_map/psum | solution.py:533
  701.5 24.2 %reduce-scatter.18.cloned.1.call-done = f32[128,1664]{1,0:T(8,128)} async-done(((f32[1024,1664]{1,0:T(8,128)}), f32[128,1664]{1,0:T(8,128)}) %reduce-scatter.18.cloned.1.call-update) | async-done | bytes 851984 | tf_op jit(solution)/shard_map/reduce_scatter | solution.py:537
  729.3 45.0 %reduce-scatter.22.cloned.1.call-done = f32[128,704]{0,1:T(8,128)} async-done(((f32[1024,704]{0,1:T(8,128)}), f32[128,704]{0,1:T(8,128)}) %reduce-scatter.22.cloned.1.call-update) | async-done | bytes 360464 | tf_op jit(solution)/shard_map/reduce_scatter | solution.py:543
  774.3 48.6 %reduce-scatter.24.cloned.1.call-done = f32[128,704]{0,1:T(8,128)} async-done(((f32[1024,704]{0,1:T(8,128)}), f32[128,704]{0,1:T(8,128)}) %reduce-scatter.24.cloned.1.call-update) | async-done | bytes 360464 | tf_op jit(solution)/shard_map/reduce_scatter | solution.py:544
  822.8 48.5 %reduce-scatter.26.cloned.1.call-done = f32[128,704]{0,1:T(8,128)} async-done(((f32[1024,704]{0,1:T(8,128)}), f32[128,704]{0,1:T(8,128)}) %reduce-scatter.26.cloned.1.call-update) | async-done | bytes 360464 | tf_op jit(solution)/shard_map/reduce_scatter | solution.py:545
  871.4 125.6 %all-reduce.6.cloned.1.call-done = f32[4,4096]{1,0:T(4,128)} async-done(((f32[4,4096]{1,0:T(4,128)}), f32[4,4096]{1,0:T(4,128)}) %all-reduce.6.cloned.1.call-update) | async-done | bytes 65552 | tf_op jit(solution)/shard_map/psum | solution.py:533
  (118 shorter events, 44.0 us)
Async XLA Ops:
  7.2 6.8 copy-start
  7.2 5.3 copy-start.11
  7.2 5.3 copy-start.15
  7.2 5.4 copy-start.16
  7.2 52.0 %all-gather.10.cloned.1.call-start = ((), (), s32[]{:S(2)}) async-start(), calls=%async_computation.9 | async-start | bytes 2621440 | tf_op jit(solution)/shard_map/all_gather | solution.py:465
  10.7 83.1 %all-gather.12.cloned.1.call-start = ((), (), s32[]{:S(2)}) async-start(), calls=%async_computation.10 | async-start | bytes 3833856 | tf_op jit(solution)/shard_map/all_gather | solution.py:469
  11.7 146.3 %all-gather.14.cloned.1.call-start = ((), (), s32[]{:S(2)}) async-start(), calls=%async_computation.11 | async-start | bytes 1179648 | tf_op jit(solution)/shard_map/all_gather | solution.py:470
  12.4 227.3 %reduce-scatter.10.cloned.1.call-start = ((), (), s32[]{:S(2)}) async-start(), calls=%async_computation.12 | async-start | bytes 5242880 | tf_op jit(solution)/shard_map/reduce_scatter | solution.py:473
  14.0 89.2 %copy-start.2 = (f32[8,128]{1,0:T(8,128)}, f32[8,128]{1,0:T(8,128)S(1)}, u32[]{:S(2)}) copy-start(f32[8,128]{1,0:T(8,128)S(1)} %scatter_fusion.1) | copy-start | bytes 12292
  162.8 77.0 %copy-start.3 = (bf16[256,1024]{1,0:T(8,128)(2,1)S(1)}, bf16[256,1024]{1,0:T(8,128)(2,1)}, u32[]{:S(2)}) copy-start(bf16[256,1024]{1,0:T(8,128)(2,1)} %param.15) | copy-start | bytes 1572868
  162.8 78.4 %copy-start.8 = (f32[1024]{0:T(1024)S(1)}, f32[1024]{0:T(1024)}, u32[]{:S(2)}) copy-start(f32[1024]{0:T(1024)} %param.26) | copy-start | bytes 12292
  162.8 104.4 %all-gather.18.cloned.1.call-start = ((), (), s32[]{:S(2)}) async-start(), calls=%async_computation.14 | async-start | bytes 1622016 | tf_op jit(solution)/shard_map/all_gather | solution.py:421
  163.4 151.5 %all-gather.16.cloned.1.call-start = ((), (), s32[]{:S(2)}) async-start(), calls=%async_computation.13 | async-start | bytes 2621440 | tf_op jit(solution)/shard_map/all_gather | solution.py:419
  242.2 98.7 %all-gather.20.cloned.1.call-start = ((), (), s32[]{:S(2)}) async-start(), calls=%async_computation.15 | async-start | bytes 1622016 | tf_op jit(solution)/shard_map/all_gather | solution.py:422
  242.9 125.0 %all-gather.22.cloned.1.call-start = ((), (), s32[]{:S(2)}) async-start(), calls=%async_computation.16 | async-start | bytes 1622016 | tf_op jit(solution)/shard_map/all_gather | solution.py:423
  243.7 171.5 %all-gather.24.cloned.1.call-start = ((), (), s32[]{:S(2)}) async-start(), calls=%async_computation.18 | async-start | bytes 2621440 | tf_op jit(solution)/shard_map/all_gather | solution.py:491
  244.4 228.6 %reduce-scatter.14.cloned.1.call-start = ((), (), s32[]{:S(2)}) async-start(), calls=%async_computation.19 | async-start | bytes 2621440 | tf_op jit(solution)/shard_map/reduce_scatter | solution.py:498
  422.8 4.4 copy-start.14
  430.4 44.0 %copy-start.4 = (bf16[256,1024]{1,0:T(8,128)(2,1)S(1)}, bf16[256,1024]{1,0:T(8,128)(2,1)}, u32[]{:S(2)}) copy-start(bf16[256,1024]{1,0:T(8,128)(2,1)} %param.17) | copy-start | bytes 1572868
  430.4 91.2 %all-gather.26.cloned.1.call-start = ((), (), s32[]{:S(2)}) async-start(), calls=%async_computation.20 | async-start | bytes 2621440 | tf_op jit(solution)/shard_map/all_gather | solution.py:508
  476.7 127.3 %reduce-scatter.20.cloned.1.call-start = ((), (), s32[]{:S(2)}) async-start(), calls=%async_computation.24 | async-start | bytes 2359296 | tf_op jit(solution)/shard_map/reduce_scatter | solution.py:540
  526.1 87.2 %reduce-scatter.16.cloned.1.call-start = ((), (), s32[]{:S(2)}) async-start(), calls=%async_computation.21 | async-start | bytes 2621440 | tf_op jit(solution)/shard_map/reduce_scatter | solution.py:516
  570.7 87.6 %reduce-scatter.12.cloned.1.call-start = ((), (), s32[]{:S(2)}) async-start(), calls=%async_computation.17 | async-start | bytes 2621440 | tf_op jit(solution)/shard_map/reduce_scatter | solution.py:484
  575.7 150.0 %reduce-scatter.18.cloned.1.call-start = ((), (), s32[]{:S(2)}) async-start(), calls=%async_computation.22 | async-start | bytes 7667712 | tf_op jit(solution)/shard_map/reduce_scatter | solution.py:537
  585.5 188.8 %reduce-scatter.22.cloned.1.call-start = ((), (), s32[]{:S(2)}) async-start(), calls=%async_computation.25 | async-start | bytes 3244032 | tf_op jit(solution)/shard_map/reduce_scatter | solution.py:543
  590.9 232.0 %reduce-scatter.24.cloned.1.call-start = ((), (), s32[]{:S(2)}) async-start(), calls=%async_computation.26 | async-start | bytes 3244032 | tf_op jit(solution)/shard_map/reduce_scatter | solution.py:544
  596.2 275.1 %reduce-scatter.26.cloned.1.call-start = ((), (), s32[]{:S(2)}) async-start(), calls=%async_computation.27 | async-start | bytes 3244032 | tf_op jit(solution)/shard_map/reduce_scatter | solution.py:545
  601.6 11.7 %copy-start.9 = (f32[1024]{0:T(1024)S(1)}, f32[1024]{0:T(1024)}, u32[]{:S(2)}) copy-start(f32[1024]{0:T(1024)} %param.18) | copy-start | bytes 12292
  601.6 56.7 %copy-start.5 = (bf16[256,1024]{1,0:T(8,128)(2,1)S(1)}, bf16[256,1024]{1,0:T(8,128)(2,1)}, u32[]{:S(2)}) copy-start(bf16[256,1024]{1,0:T(8,128)(2,1)} %reduce-scatter.14.cloned.1.call-done) | copy-start | bytes 1572868
  601.6 395.3 %all-reduce.6.cloned.1.call-start = ((), (), s32[]{:S(2)}) async-start(), calls=%async_computation.23 | async-start | bytes 131072 | tf_op jit(solution)/shard_map/psum | solution.py:533
  614.7 46.7 %copy-start.13 = (f32[1,256]{1,0:T(1,128)S(1)}, f32[1,256]{1,0:T(1,128)}, u32[]{:S(2)}) copy-start(f32[1,256]{1,0:T(1,128)} %get-tuple-element.37) | copy-start | bytes 3076
  658.3 340.1 %copy-start.1 = (f32[4,4096]{1,0:T(4,128)S(1)}, f32[4,4096]{1,0:T(4,128)}, u32[]{:S(2)}) copy-start(f32[4,4096]{1,0:T(4,128)} %param.21) | copy-start | bytes 196612
  (6 other events, 18.3 us)
Sparse Core Ops, SparseCore 0:
  10.8 48.3 all-gather.9
  61.7 32.0 all-gather.11
  95.7 23.5 all-gather.13
  162.9 76.7 reduce-scatter.9
  241.5 25.7 all-gather.17
  269.2 45.6 all-gather.15
  316.8 23.9 all-gather.19
  342.7 25.1 all-gather.21
  369.5 45.6 all-gather.23
  430.6 42.4 reduce-scatter.13
  476.8 44.8 all-gather.25
  526.2 39.9 reduce-scatter.19
  570.8 42.4 reduce-scatter.15
  615.5 42.8 reduce-scatter.11
  661.6 64.0 reduce-scatter.17
  729.5 44.6 reduce-scatter.21
  778.1 44.7 reduce-scatter.23
  826.6 44.6 reduce-scatter.25
  877.5 119.3 all-reduce.5

commit v2 on v1

--- a/solution.py
+++ b/solution.py
@@ -394,18 +394,6 @@
     )(projected, projected, docs, docs, docs, taps, vectors, gain, *kept, grad)
 
 
-def rms_rows(values, gain):
-    return values * lax.rsqrt(jnp.mean(values * values, axis=-1, keepdims=True) + EPSILON) * gain
-
-
-def rms_back(values, gain, grad_normed):
-    scale = lax.rsqrt(jnp.mean(values * values, axis=-1, keepdims=True) + EPSILON)
-    weighted = grad_normed * gain
-    inner = jnp.mean(weighted * values, axis=-1, keepdims=True)
-    grad_values = scale * weighted - values * scale * scale * scale * inner
-    return (grad_values, jnp.sum(grad_normed * values * scale, axis=0))
-
-
 def times_transposed(left, right):
     return lax.dot_general(left, right, NT, preferred_element_type=F32)
 
@@ -414,18 +402,139 @@
     return lax.dot_general(left, right, TN, preferred_element_type=F32)
 
 
-def ffn_front(resid, norm_ffn, w_gate, w_up, w_down):
-    normed = rms_rows(resid, norm_ffn).astype(jnp.bfloat16)
-    seq_rows = lax.all_gather(normed, "tensor", axis=0, tiled=True)
-    whole_gate, whole_up, whole_down = (
-        lax.all_gather(w_gate, "dp", axis=0, tiled=True),
-        lax.all_gather(w_up, "dp", axis=0, tiled=True),
-        lax.all_gather(w_down, "dp", axis=1, tiled=True),
-    )
-    gate_pre = jnp.dot(seq_rows, whole_gate, preferred_element_type=jnp.float32)
-    up_pre = jnp.dot(seq_rows, whole_up, preferred_element_type=jnp.float32)
-    hidden = (jax.nn.silu(gate_pre) * up_pre).astype(jnp.bfloat16)
-    return (seq_rows, whole_gate, whole_up, whole_down, gate_pre, up_pre, hidden)
+def times(left, right):
+    return lax.dot_general(left, right, NN, preferred_element_type=F32)
+
+
+def block_source(me_ref, place_index, width):
+    return pl.ds(pl.multiple_of((me_ref[0] ^ place_index) * width, width), width)
+
+
+def row_scale(values):
+    return lax.rsqrt(jnp.mean(values * values, axis=-1, keepdims=True) + EPSILON)
+
+
+def prepare_kernel(
+    me_ref, x_ref, cot_ref, gain_in_ref, gain_ffn_ref,
+    x_out, cot_out, normed_out, gain_in_out, gain_ffn_out,
+):
+    scale = row_scale(x_ref[...].astype(F32))
+    for p in range(x_ref.shape[1] // CHUNK):
+        here, source = pl.ds(p * CHUNK, CHUNK), block_source(me_ref, p, CHUNK)
+        part = x_ref[:, source]
+        gain = gain_in_ref[:, source]
+        x_out[:, here] = part
+        cot_out[:, here] = cot_ref[:, source]
+        normed_out[:, here] = (part.astype(F32) * scale * gain).astype(BF16)
+        gain_in_out[:, here] = gain
+        gain_ffn_out[:, here] = gain_ffn_ref[:, source]
+
+
+def middle_kernel(x_ref, mixed_ref, gain_ref, resid_out, normed_out):
+    resid = x_ref[...].astype(F32) + mixed_ref[...].astype(F32)
+    resid_out[...] = resid
+    normed_out[...] = (resid * row_scale(resid) * gain_ref[...]).astype(BF16)
+
+
+def ffn_back_kernel(me_ref, resid_ref, cot_ref, grad_ref, gain_ref, d_resid_out, d_mixed_out, d_gain_out):
+    resid = resid_ref[...]
+    grad = grad_ref[...].astype(F32)
+    scale = row_scale(resid)
+    unit = resid * scale
+    weighted = grad * gain_ref[...]
+    inner = jnp.mean(weighted * unit, axis=-1, keepdims=True)
+    d_resid = cot_ref[...].astype(F32) + scale * (weighted - unit * inner)
+    d_resid_out[...] = d_resid
+    d_mixed_out[...] = d_resid.astype(BF16)
+    sums = jnp.sum(grad * unit, axis=0, keepdims=True)
+    for p in range(resid.shape[1] // CHUNK):
+        d_gain_out[:, block_source(me_ref, p, CHUNK)] = sums[:, p * CHUNK : (p + 1) * CHUNK]
+
+
+def output_kernel(me_ref, resid_ref, ffn_ref, out_ref):
+    for p in range(resid_ref.shape[1] // CHUNK):
+        here = pl.ds(p * CHUNK, CHUNK)
+        total = resid_ref[:, here] + ffn_ref[:, here].astype(F32)
+        out_ref[:, block_source(me_ref, p, CHUNK)] = total.astype(BF16)
+
+
+def gain_kernel(me_ref, grad_ref, normed_ref, gain_ref, out_ref):
+    sums = jnp.sum(grad_ref[...].astype(F32) * normed_ref[...].astype(F32), axis=0, keepdims=True)
+    sums = sums / gain_ref[...]
+    for p in range(grad_ref.shape[1] // CHUNK):
+        out_ref[:, block_source(me_ref, p, CHUNK)] = sums[:, p * CHUNK : (p + 1) * CHUNK]
+
+
+def finish_kernel(me_ref, x_ref, d_resid_ref, grad_ref, gain_ref, out_ref):
+    x = x_ref[...].astype(F32)
+    scale = row_scale(x)
+    unit = x * scale
+    weighted = grad_ref[...].astype(F32) * gain_ref[...]
+    inner = jnp.mean(weighted * unit, axis=-1, keepdims=True)
+    total = d_resid_ref[...] + scale * (weighted - unit * inner)
+    for p in range(x.shape[1] // CHUNK):
+        out_ref[:, block_source(me_ref, p, CHUNK)] = total[:, p * CHUNK : (p + 1) * CHUNK]
+
+
+def row_call(kernel, name, outs, *args):
+    def space(arg):
+        kind = pltpu.SMEM if arg.dtype == jnp.int32 else pltpu.VMEM
+        return pl.BlockSpec(memory_space=kind)
+
+    return pl.pallas_call(
+        kernel,
+        in_specs=[space(a) for a in args],
+        out_specs=[pl.BlockSpec(memory_space=pltpu.VMEM)] * len(outs),
+        out_shape=[jax.ShapeDtypeStruct(s, d) for s, d in outs],
+        name=name,
+    )(*args)
+
+
+def swap(value, axis, mask):
+    pairs = [(i, i ^ mask) for i in range(lax.axis_size(axis))]
+    return lax.ppermute(value, axis, pairs)
+
+
+def small_dp():
+    return lax.axis_size("dp") == 8
+
+
+def gather_pieces(own):
+    across = [own] + [swap(own, "dp", 2 * q) for q in range(1, 4)]
+    beside = [swap(piece, "dp", 1) for piece in across]
+    return [piece for pair in zip(across, beside) for piece in pair]
+
+
+def gather_dp(own, axis):
+    if small_dp():
+        return jnp.concatenate(gather_pieces(own), axis=axis)
+    return lax.all_gather(own, "dp", axis=axis, tiled=True)
+
+
+def scatter_dp(partial, axis):
+    if not small_dp():
+        return lax.psum_scatter(partial, "dp", scatter_dimension=axis, tiled=True).astype(F32)
+    blocks = jnp.split(partial, 8, axis=axis)
+    sent = swap(jnp.concatenate(blocks[1::2], axis=axis), "dp", 1)
+    halves = [
+        (mine.astype(F32) + other.astype(F32)).astype(BF16)
+        for mine, other in zip(blocks[0::2], jnp.split(sent, 4, axis=axis))
+    ]
+    total = halves[0].astype(F32)
+    for q in range(1, 4):
+        total = total + swap(halves[q], "dp", 2 * q).astype(F32)
+    return total
+
+
+def tree_sum(value, axis):
+    parts = [value] + [swap(value, axis, mask) for mask in range(1, lax.axis_size(axis))]
+    while len(parts) > 1:
+        parts = [left + right for left, right in zip(parts[0::2], parts[1::2])]
+    return parts[0]
+
+
+def after(value, anchor):
+    return lax.optimization_barrier((value, anchor))[0]
 
 
 def local(
@@ -446,119 +555,127 @@
     w_down,
 ):
     doc_ids = segments[0]
+    length = doc_ids.shape[0]
+    rows, features = inputs.shape
     part_index = lax.axis_index("tensor")
-    head_count = a_log.shape[0] // lax.axis_size("tensor")
-    conv_width = head_count * (2 * DK + DV)
+    parts = lax.axis_size("tensor")
+    head_count = a_log.shape[0] // parts
+    conv_width = head_count * CONVW
+    hidden_units = w_down.shape[0]
+    order = lax.axis_index("dp") if small_dp() else jnp.zeros((), jnp.int32)
+    me = order.astype(jnp.int32)[None]
     conv_mine = lax.dynamic_slice_in_dim(conv_weight, part_index * conv_width, conv_width, 1)
     alog_mine = lax.dynamic_slice_in_dim(a_log, part_index * head_count, head_count, 0)
     bias_mine = lax.dynamic_slice_in_dim(dt_bias, part_index * head_count, head_count, 0)
-
-    length = doc_ids.shape[0]
     docs = jnp.broadcast_to(doc_ids.astype(F32)[:, None], (length, CHUNK))
-    vectors = jnp.zeros((8, CHUNK), F32)
-    vectors = vectors.at[0, 0 : 2 * head_count : 2].set(jnp.exp(alog_mine))
-    vectors = vectors.at[1, 0 : 2 * head_count : 2].set(bias_mine)
+    lane_pair = jnp.stack([jnp.exp(alog_mine), bias_mine])
+    spread = jnp.stack([lane_pair, jnp.zeros_like(lane_pair)], axis=-1).reshape(2, 2 * head_count)
+    vectors = jnp.pad(spread, ((0, 6), (0, CHUNK - 2 * head_count)))
     gain_row = out_gain[None, :]
 
-    input_rows = inputs.astype(jnp.float32)
-    normed = rms_rows(input_rows, norm_in).astype(BF16)
-    seq_rows = lax.all_gather(normed, "tensor", axis=0, tiled=True)
+    token_bf, token_f32 = ((rows, features), BF16), ((rows, features), F32)
+    gain_shape = ((1, features), F32)
+    x, cot, normed, gain_in, gain_ffn = row_call(
+        prepare_kernel, "prepare", [token_bf, token_bf, token_bf, gain_shape, gain_shape],
+        me, inputs, cotangent, norm_in[None], norm_ffn[None],
+    )
     joined = jnp.concatenate(
         [w_in, jnp.pad(w_alpha_beta, ((0, 0), (0, CHUNK - w_alpha_beta.shape[1])))], axis=1
     )
-    whole_in = lax.all_gather(joined, "dp", axis=0, tiled=True)
-    whole_out = lax.all_gather(w_out, "dp", axis=1, tiled=True)
-    projected = jnp.dot(seq_rows, whole_in, preferred_element_type=F32)
+    seq_rows = lax.all_gather(normed, "tensor", axis=0, tiled=True)
+    whole_in = gather_dp(joined, 0)
+    unit_weights = jnp.concatenate([w_gate.T, w_up.T, w_down, w_out], axis=0)
+    whole_units = gather_dp(after(unit_weights, whole_in), 1)
+    whole_pre = whole_units[: 2 * hidden_units]
+    whole_down = whole_units[2 * hidden_units : 3 * hidden_units]
+    whole_out = whole_units[3 * hidden_units :]
+    projected = times(seq_rows, whole_in)
+    back_seq = lax.all_gather(after(cot, seq_rows), "tensor", axis=0, tiled=True)
     gated, *kept = mixer_forward(projected, docs, conv_mine, vectors, gain_row)
-    resid = input_rows + lax.psum_scatter(
-        jnp.dot(gated, whole_out, preferred_element_type=jnp.float32),
-        "tensor",
-        scatter_dimension=0,
-        tiled=True,
-    )
-    ffn_seq, whole_gate, whole_up, whole_down, gate_pre, up_pre, hidden = ffn_front(
-        resid, norm_ffn, w_gate, w_up, w_down
-    )
-    output = (
-        resid
-        + lax.psum_scatter(
-            jnp.dot(hidden, whole_down, preferred_element_type=jnp.float32).astype(jnp.bfloat16),
-            "tensor",
-            scatter_dimension=0,
-            tiled=True,
-        ).astype(jnp.float32)
-    ).astype(jnp.bfloat16)
-    back_seq = lax.all_gather(cotangent, "tensor", axis=0, tiled=True)
-    d_hidden = times_transposed(back_seq, whole_down)
-    sigmoid_gate = jax.nn.sigmoid(gate_pre)
-    d_up = (d_hidden * gate_pre * sigmoid_gate).astype(jnp.bfloat16)
-    d_gate = (d_hidden * up_pre * sigmoid_gate * (1.0 + gate_pre * (1.0 - sigmoid_gate))).astype(
-        jnp.bfloat16
-    )
+    mixed = lax.psum_scatter(
+        times(gated, whole_out).astype(BF16), "tensor", scatter_dimension=0, tiled=True
+    )
+    resid, normed_ffn = row_call(middle_kernel, "middle", [token_f32, token_bf], x, mixed, gain_ffn)
+
+    ffn_seq = lax.all_gather(normed_ffn, "tensor", axis=0, tiled=True)
+    pre = times_transposed(whole_pre, ffn_seq)
+    gate_pre, up_pre = pre[:hidden_units], pre[hidden_units:]
+    d_hidden = times_transposed(whole_down, back_seq)
+    sig = jax.nn.sigmoid(gate_pre)
+    hidden = (gate_pre * sig * up_pre).astype(BF16)
+    d_up = (d_hidden * gate_pre * sig).astype(BF16)
+    d_gate = (d_hidden * up_pre * sig * (1.0 + gate_pre * (1.0 - sig))).astype(BF16)
+    d_pre = jnp.concatenate([d_gate, d_up], axis=0)
     d_normed_ffn = lax.psum_scatter(
-        (times_transposed(d_gate, whole_gate) + times_transposed(d_up, whole_up)).astype(
-            jnp.bfloat16
-        ),
-        "tensor",
-        scatter_dimension=0,
-        tiled=True,
-    ).astype(jnp.float32)
-    resid_from_norm, gain_ffn_part = rms_back(resid, norm_ffn, d_normed_ffn)
-    d_resid = cotangent.astype(jnp.float32) + resid_from_norm
-    mixer_back_seq = lax.all_gather(d_resid.astype(jnp.bfloat16), "tensor", axis=0, tiled=True)
+        transposed_times(d_pre, whole_pre).astype(BF16), "tensor", scatter_dimension=0, tiled=True
+    )
+    grad_pre = scatter_dp(times(d_pre, ffn_seq).astype(BF16), 1)
+    grad_down = scatter_dp(times(hidden, back_seq).astype(BF16), 1)
+    d_resid, d_mixed, gain_ffn_part = row_call(
+        ffn_back_kernel, "ffn_back", [token_f32, token_bf, gain_shape],
+        me, resid, cot, d_normed_ffn, gain_ffn,
+    )
+
+    mixer_back_seq = lax.all_gather(d_mixed, "tensor", axis=0, tiled=True)
+    ffn_part = after(transposed_times(hidden, whole_down).astype(BF16), mixer_back_seq)
+    ffn_out = lax.psum_scatter(ffn_part, "tensor", scatter_dimension=0, tiled=True)
+    (output,) = row_call(output_kernel, "output", [token_bf], me, resid, ffn_out)
     d_gated = times_transposed(mixer_back_seq, whole_out)
-    d_projected, d_conv, d_vectors, d_gain_row = mixer_backward(
+    grad_out = scatter_dp(transposed_times(gated, mixer_back_seq).astype(BF16), 1)
+    d_projected, d_conv, d_vectors, d_gain_out = mixer_backward(
         projected, docs, conv_mine, vectors, gain_row, kept, d_gated
     )
-    d_alog = d_vectors[0, 0 : 2 * head_count : 2]
-    d_bias = d_vectors[1, 0 : 2 * head_count : 2]
-    d_gain_out = d_gain_row[0]
-    d_normed_in = lax.psum_scatter(
-        times_transposed(d_projected, whole_in).astype(BF16),
-        "tensor",
-        scatter_dimension=0,
-        tiled=True,
-    ).astype(jnp.float32)
-    input_from_norm, gain_in_part = rms_back(input_rows, norm_in, d_normed_in)
-    d_inputs = d_resid + input_from_norm
-    conv_full = lax.dynamic_update_slice_in_dim(
-        jnp.zeros(conv_weight.shape, jnp.float32), d_conv, part_index * conv_width, 1
-    )
-    alog_full = lax.dynamic_update_slice_in_dim(
-        jnp.zeros(a_log.shape, jnp.float32), d_alog, part_index * head_count, 0
-    )
-    bias_full = lax.dynamic_update_slice_in_dim(
-        jnp.zeros(dt_bias.shape, jnp.float32), d_bias, part_index * head_count, 0
-    )
-    small_sums = lax.psum(
-        (gain_in_part, gain_ffn_part, conv_full, alog_full, bias_full, d_gain_out), ("dp", "tensor")
-    )
-    owned_joined, owned_out, owned_gate, owned_up, owned_down = (
-        lax.psum_scatter(
-            transposed_times(seq_rows, d_projected), "dp", scatter_dimension=0, tiled=True
-        ),
-        lax.psum_scatter(
-            transposed_times(mixer_back_seq, gated), "dp", scatter_dimension=0, tiled=True
-        ),
-        lax.psum_scatter(transposed_times(ffn_seq, d_gate), "dp", scatter_dimension=0, tiled=True),
-        lax.psum_scatter(transposed_times(ffn_seq, d_up), "dp", scatter_dimension=0, tiled=True),
-        lax.psum_scatter(transposed_times(back_seq, hidden), "dp", scatter_dimension=0, tiled=True),
-    )
+    d_part = times_transposed(d_projected, whole_in).astype(BF16)
+    d_normed_in = lax.psum_scatter(d_part, "tensor", scatter_dimension=0, tiled=True)
+    grad_joined = scatter_dp(transposed_times(seq_rows, d_projected).astype(BF16), 0)
+    (gain_in_part,) = row_call(gain_kernel, "gain", [gain_shape], me, d_part, seq_rows, gain_in)
+    (d_inputs,) = row_call(
+        finish_kernel, "finish", [token_f32], me, x, d_resid, d_normed_in, gain_in
+    )
+
+    last = jnp.concatenate(
+        [
+            d_gain_out,
+            d_vectors[:1, : 2 * head_count],
+            d_vectors[1:2, : 2 * head_count],
+        ],
+        axis=1,
+    )
+    last = jnp.pad(last, ((0, 0), (0, conv_width - last.shape[1])))
+    if conv_width == features:
+        table = jnp.concatenate([d_conv, gain_in_part, gain_ffn_part, last], axis=0)
+        table = tree_sum(table, "dp") if small_dp() else lax.psum(table, "dp")
+        tables = [table] + [swap(table, "tensor", mask) for mask in range(1, parts)]
+    else:
+        raise ValueError("conv width")
+    shared = [t[4:] for t in tables]
+    while len(shared) > 1:
+        shared = [left + right for left, right in zip(shared[0::2], shared[1::2])]
+    shared = shared[0]
+    grad_conv = jnp.zeros(conv_weight.shape, F32)
+    own = jnp.zeros((2, a_log.shape[0]), F32)
+    width = out_gain.shape[0]
+    for mask, t in enumerate(tables):
+        place_index = part_index ^ mask
+        grad_conv = lax.dynamic_update_slice_in_dim(grad_conv, t[:4], place_index * conv_width, 1)
+        pair = t[6, width : width + 4 * head_count].reshape(2, 2 * head_count)[:, ::2]
+        own = lax.dynamic_update_slice_in_dim(own, pair, place_index * head_count, 1)
+    columns = w_in.shape[1]
     return (
         output,
         d_inputs,
-        small_sums[0],
-        owned_joined[:, : w_in.shape[1]],
-        owned_joined[:, w_in.shape[1] : w_in.shape[1] + w_alpha_beta.shape[1]],
-        small_sums[2],
-        small_sums[3],
-        small_sums[4],
-        small_sums[5],
-        jnp.transpose(owned_out),
-        small_sums[1],
-        owned_gate,
-        owned_up,
-        jnp.transpose(owned_down),
+        shared[0],
+        grad_joined[:, :columns],
+        grad_joined[:, columns : columns + w_alpha_beta.shape[1]],
+        grad_conv,
+        own[0],
+        own[1],
+        shared[2, :width],
+        grad_out,
+        shared[1],
+        grad_pre[:hidden_units].T,
+        grad_pre[hidden_units:].T,
+        grad_down,
     )
 
 

time: 1010 us -> 555 us (0.55)
  waiting for transfers between devices: 750 us -> 279 us
  blocking collectives: 40.1 us -> 0 us
  starting transfers between devices: 1.41 us -> 35.4 us
  matrix products: 87.3 us -> 66.1 us
  local copies, waits for them, and re-layouts: 12.3 us -> 30.6 us
  Pallas kernels: 85.3 us -> 103 us
    reduce_scatter x9 -> x4, waiting for transfers between devices: 336 us -> 87.3 us  [the longest x1 44.8 us: local(): lax.psum_scatter(times(gated, whole_out).astype(BF16), 'tensor', scatter_...]
    all_gather x8 -> x3, waiting for transfers between devices: 240 us -> 110 us  [the longest x1 44.2 us: local(): ffn_seq = lax.all_gather(normed_ffn, 'tensor', axis=0, tiled=True)]
    psum x1 -> x0, waiting for transfers between devices: 126 us -> none  [local(): lax.psum((gain_in_part, gain_ffn_part, conv_full, alog_full, bias_full, d...]
    ppermute x0 -> x40, waiting for transfers between devices: none -> 80.3 us  [swap(): return lax.ppermute(value, axis, pairs)]
    all_gather x1, waiting for transfers between devices: 44.6 us -> 0.01 us  [local(): seq_rows = lax.all_gather(normed, 'tensor', axis=0, tiled=True)]
    psum x1 -> x0, blocking collectives: 40.1 us -> none  [local(): lax.psum((gain_in_part, gain_ffn_part, conv_full, alog_full, bias_full, d...]
    ppermute x0 -> x40, starting transfers between devices: none -> 34.7 us  [swap(): return lax.ppermute(value, axis, pairs)]
    pallas_call x0 -> x6, Pallas kernels: none -> 17 us  [row_call(): pl.pallas_call(kernel, in_specs=[space(a) for a in args], out_specs=[pl.B...]
  transfers between devices with their start and end apart: 19 -> 48, of which waited for: 17 -> 20; matrix products, arithmetic and copies ran while one was open for 8% -> 14% of each run, Pallas kernels for 8% -> 7%
where the time goes in v2:
time: 555 us; the launch traced here: 547 us
  waiting for transfers between devices  279 us (50%)
  Pallas kernels  103 us (19%)
  matrix products  66.1 us (12%)
  starting transfers between devices  35.4 us (6%)
  local copies, waits for them, and re-layouts  30.6 us (6%)
  other arithmetic  18.3 us (3%)
  between operations  15.1 us (3%)
    ppermute x40, waiting for transfers between devices, swap(): return lax.ppermute(value, axis, pairs)  80.3 us
    pallas_call x1, Pallas kernels, mixer_forward(): pl.pallas_call(functools.partial(forward_kernel, heads), grid=(chunks,),...  53.8 us
    reduce_scatter x1, waiting for transfers between devices, local(): lax.psum_scatter(times(gated, whole_out).astype(BF16), 'tensor', scatter_...  44.8 us
    all_gather x1, waiting for transfers between devices, local(): ffn_seq = lax.all_gather(normed_ffn, 'tensor', axis=0, tiled=True)  44.2 us
    reduce_scatter x1, waiting for transfers between devices, local(): lax.psum_scatter(transposed_times(d_pre, whole_pre).astype(BF16), 'tensor...  42.5 us
    all_gather x1, waiting for transfers between devices, local(): lax.all_gather(after(cot, seq_rows), 'tensor', axis=0, tiled=True)  38.3 us
    ppermute x40, starting transfers between devices, swap(): return lax.ppermute(value, axis, pairs)  34.7 us
    pallas_call x1, Pallas kernels, mixer_backward(): pl.pallas_call(functools.partial(backward_kernel, heads, chunks), grid=(c...  31.8 us
  transfers between devices with their start and end apart: 48, of which 20 were waited for; matrix products, arithmetic and copies ran while one was open for 14% of the time, Pallas kernels for 7%

profile of v2, /device:TPU:0, one launch (start us, length us, event | category | flops | bytes accessed | tf_op | source)
XLA Modules:
  0.0 546.8 jit_solution(1676220270391326392)
XLA Ops:
  10.1 3.0 collective-permute-start.1
  14.6 2.8 prepare.1
  17.6 6.2 %collective-permute-done.1 = bf16[128,1664]{1,0:T(8,128)(2,1)S(1)} collective-permute-done((bf16[128,1664]{1,0:T(8,128)(2,1)S(1)}, bf16[128,1664]{1,0:T(8,128)(2,1)S(1)}, u32[]{:S(2)}, u32[]{:S(2)}) %collective-permute-start.1) | collective-permute-done | bytes 426016 | tf_op jit(solution)/shard_map/ppermute | solution.py:495
  23.7 9.7 %collective-permute-done.3 = bf16[128,1664]{1,0:T(8,128)(2,1)S(1)} collective-permute-done((bf16[128,1664]{1,0:T(8,128)(2,1)S(1)}, bf16[128,1664]{1,0:T(8,128)(2,1)S(1)}, u32[]{:S(2)}, u32[]{:S(2)}) %collective-permute-start.3) | collective-permute-done | bytes 426016 | tf_op jit(solution)/shard_map/ppermute | solution.py:495
  45.5 12.0 %collective-permute-done.8 = bf16[2624,128]{1,0:T(8,128)(2,1)S(1)} collective-permute-done((bf16[2624,128]{1,0:T(8,128)(2,1)S(1)}, bf16[2624,128]{1,0:T(8,128)(2,1)S(1)}, u32[]{:S(2)}, u32[]{:S(2)}) %collective-permute-start.8) | collective-permute-done | bytes 671776 | tf_op jit(solution)/shard_map/ppermute | solution.py:495
  57.5 13.2 %collective-permute-done.10 = bf16[2624,128]{1,0:T(8,128)(2,1)S(1)} collective-permute-done((bf16[2624,128]{1,0:T(8,128)(2,1)S(1)}, bf16[2624,128]{1,0:T(8,128)(2,1)S(1)}, u32[]{:S(2)}, u32[]{:S(2)}) %collective-permute-start.10) | collective-permute-done | bytes 671776 | tf_op jit(solution)/shard_map/ppermute | solution.py:495
  79.1 9.3 %fusion.24.proj_ref.before_ref = f32[1024,1664]{1,0:T(8,128)} fusion(bf16[1024,1024]{1,0:T(8,128)(2,1)} %all-gather.5.cloned.1.call-done.normed_ref, bf16[1024,1664]{1,0:T(8,128)(2,1)} %constant_dynamic-update-slice_fusion), kind=kOutput, calls=%fused_computation.99 | convolution fusion | flops 3489660928 | bytes 12320768 | tf_op jit(solution)/shard_map/dot_general | solution.py:406
  89.4 53.8 %mixer_forward.1 = (bf16[1024,512]{1,0:T(8,128)(2,1)}, f32[1024,512]{1,0:T(8,128)}, f32[8,2,128,128]{3,2,1,0:T(8,128)}, f32[8,2,128,384]{3,2,1,0:T(8,128)}, f32[...) custom-call(f32[1024,1664]{1,0:T(8,128)} %fusion.24.proj_ref.before_, ...), custom_call_target="tpu_custom_call" | custom-call | tf_op jit(solution)/shard_map/mixer_forward/pallas_call | solution.py:348
  143.2 4.1 convolution_convert_fusion.3
  147.4 44.8 %reduce-scatter.5.cloned.1.call-done.mixed_ref = bf16[256,1024]{1,0:T(8,128)(2,1)} async-done(((bf16[1024,1024]{1,0:T(8,128)(2,1)}), bf16[256,1024]{1,0:T(8,128)(2,1)}) %reduce-scatter.5.cloned.1.call-update) | async-done | bytes 524304 | tf_op jit(solution)/shard_map/reduce_scatter | solution.py:595
  195.5 44.2 %all-gather.7.cloned.1.call-done = bf16[1024,1024]{1,0:T(8,128)(2,1)} async-done(((bf16[256,1024]{1,0:T(8,128)(2,1)}), bf16[1024,1024]{1,0:T(8,128)(2,1)}) %all-gather.7.cloned.1.call-update) | async-done | bytes 2097168 | tf_op jit(solution)/shard_map/all_gather | solution.py:600
  239.7 8.2 %fusion.2 = f32[1408,1024]{1,0:T(8,128)} fusion(bf16[1024,1024]{1,0:T(8,128)(2,1)} %all-gather.7.cloned.1.call-done, bf16[2624,1024]{1,0:T(8,128)(2,1)} %constant_dynamic-update-slice_fusion.8), kind=kOutput, calls=%fused_computation.9 | convolution fusion | flops 2952790016 | bytes 10747904 | tf_op jit(solution)/shard_map/dot_general | solution.py:398
  248.0 38.3 %all-gather.9.cloned.1.call-done = bf16[1024,1024]{1,0:T(8,128)(2,1)} async-done(((bf16[256,1024]{1,0:T(8,128)(2,1)}), bf16[1024,1024]{1,0:T(8,128)(2,1)}) %all-gather.9.cloned.1.call-update) | async-done | bytes 2097168 | tf_op jit(solution)/shard_map/all_gather | solution.py:593
  286.2 7.5 %multiply_convert_fusion.1 = (bf16[704,1024]{1,0:T(8,128)(2,1)S(1)}, bf16[704,1024]{1,0:T(8,128)(2,1)S(1)}, bf16[704,1024]{1,0:T(8,128)(2,1)}) fusion(f32[1408,1024]{1,0:T(8,128)} %fusion.2, bf16[1024,1024]{1,0:T(8,128)(2,1)} %all-gather.9.cloned.1.call-done, bf16[2624,1024]{1,0:T(8,128)(2,1)} %constant_dynamic-update-slice_fusion.8), kind=kOutput, calls=%fused_computation.4 | convolution fusion | flops 1487929344 | bytes 13631488 | tf_op jit(solution)/shard_map/dot_general | solution.py:398
  295.4 6.5 %fusion.4 = bf16[1024,1024]{1,0:T(8,128)(2,1)} fusion(bf16[2624,1024]{1,0:T(8,128)(2,1)} %constant_dynamic-update-slice_fusion.8, bf16[704,1024]{1,0:T(8,128)(2,1)S(1)} %get-tuple-element.79, bf16[704,1024]{1,0:T(8,128)(2,1)S(1)} %get-tuple-element.78), kind=kOutput, calls=%fused_computation.11 | convolution fusion | flops 2959605760 | bytes 7864320 | tf_op jit(solution)/shard_map/dot_general | solution.py:402
  302.0 42.5 %reduce-scatter.7.cloned.1.call-done.grad_ref = bf16[256,1024]{1,0:T(8,128)(2,1)} async-done(((bf16[1024,1024]{1,0:T(8,128)(2,1)}), bf16[256,1024]{1,0:T(8,128)(2,1)}) %reduce-scatter.7.cloned.1.call-update) | async-done | bytes 524304 | tf_op jit(solution)/shard_map/reduce_scatter | solution.py:609
  344.5 3.2 ffn_back.1
  348.0 5.6 %convolution_convert_fusion.1 = bf16[1408,1024]{1,0:T(8,128)(2,1)S(1)} fusion(bf16[1024,1024]{1,0:T(8,128)(2,1)} %all-gather.7.cloned.1.call-done, bf16[704,1024]{1,0:T(8,128)(2,1)} %copy-done.24, bf16[704,1024]{1,0:T(8,128)(2,1)} %copy-done.23), kind=kOutput, calls=%fused_computation.1 | convolution fusion | flops 2959998976 | bytes 7864320 | tf_op jit(solution)/shard_map/dot_general | solution.py:406
  360.2 4.6 convolution_convert_fusion.4
  364.8 28.0 %all-gather.11.cloned.1.call-done = bf16[1024,1024]{1,0:T(8,128)(2,1)} async-done(((bf16[256,1024]{1,0:T(8,128)(2,1)}), bf16[1024,1024]{1,0:T(8,128)(2,1)}) %all-gather.11.cloned.1.call-update) | async-done | bytes 2097168 | tf_op jit(solution)/shard_map/all_gather | solution.py:619
  404.9 8.0 %collective-permute-done.38 = bf16[704,128]{1,0:T(8,128)(2,1)} collective-permute-done((bf16[704,128]{1,0:T(8,128)(2,1)}, bf16[704,128]{1,0:T(8,128)(2,1)}, u32[]{:S(2)}, u32[]{:S(2)}) %collective-permute-start.38) | collective-permute-done | bytes 180256 | tf_op jit(solution)/shard_map/ppermute | solution.py:495
  415.0 6.5 %collective-permute-done.34 = bf16[1408,128]{1,0:T(8,128)(2,1)} collective-permute-done((bf16[1408,128]{1,0:T(8,128)(2,1)}, bf16[1408,128]{1,0:T(8,128)(2,1)}, u32[]{:S(2)}, u32[]{:S(2)}) %collective-permute-start.34) | collective-permute-done | bytes 360480 | tf_op jit(solution)/shard_map/ppermute | solution.py:495
  423.9 3.8 fusion.10.grad_ref
  427.7 31.8 %mixer_backward.1 = (bf16[1024,1664]{1,0:T(8,128)(2,1)}, f32[4,1024]{1,0:T(4,128)}, f32[8,128]{1,0:T(8,128)}, f32[1,256]{1,0:T(1,128)}) custom-call(f32[1024,1664]{1,0:T(8,128)} %fusion.24.proj_ref.before_ref, f32[1024,1664]{1,0:T(8,128)} %fusion.24.proj_ref.before_ref, f32[1024,128]{1,0:T(8,128)} %broadcast_in_dim.24.doc_ref.doc_before_ref.doc_after_ref, ...), custom_call_target="tpu_custom_call" | custom-call | tf_op jit(solution)/shard_map/mixer_backward/pallas_call | solution.py:373
  459.5 7.2 %convolution_convert_fusion.2.grad_ref = bf16[1024,1024]{1,0:T(8,128)(2,1)} fusion(bf16[1024,1664]{1,0:T(8,128)(2,1)} %get-tuple-element.58, bf16[1024,1664]{1,0:T(8,128)(2,1)S(1)} %copy-done.14), kind=kOutput, calls=%fused_computation.12 | convolution fusion | flops 3490709504 | bytes 8912896 | tf_op jit(solution)/shard_map/dot_general | solution.py:398
  466.8 3.2 gain.1
  477.5 6.2 %convolution_convert_fusion = bf16[1024,1664]{1,0:T(8,128)(2,1)S(1)} fusion(bf16[1024,1024]{1,0:T(8,128)(2,1)S(1)} %copy-done.3, bf16[1024,1664]{1,0:T(8,128)(2,1)} %get-tuple-element.58), kind=kOutput, calls=%fused_computation | convolution fusion | flops 3491364864 | bytes 8912896 | tf_op jit(solution)/shard_map/dot_general | solution.py:402
  493.5 2.9 collective-permute-start.21
  496.7 4.1 collective-permute-done.21
  514.6 8.3 %collective-permute-done.27 = bf16[128,1664]{1,0:T(8,128)(2,1)S(1)} collective-permute-done((bf16[128,1664]{1,0:T(8,128)(2,1)S(1)}, bf16[128,1664]{1,0:T(8,128)(2,1)S(1)}, u32[]{:S(2)}, u32[]{:S(2)}) %collective-permute-start.27) | collective-permute-done | bytes 426016 | tf_op jit(solution)/shard_map/ppermute | solution.py:495
  522.8 8.2 %collective-permute-done.26 = bf16[128,1664]{1,0:T(8,128)(2,1)S(1)} collective-permute-done((bf16[128,1664]{1,0:T(8,128)(2,1)S(1)}, bf16[128,1664]{1,0:T(8,128)(2,1)S(1)}, u32[]{:S(2)}, u32[]{:S(2)}) %collective-permute-start.26) | collective-permute-done | bytes 426016 | tf_op jit(solution)/shard_map/ppermute | solution.py:495
  536.4 3.0 finish.1
  (219 shorter events, 90.9 us)
Async XLA Ops:
  7.2 71.9 %all-gather.5.cloned.1.call-start = ((), (), s32[]{:S(2)}) async-start(), calls=%async_computation.4 | async-start | bytes 2621440 | tf_op jit(solution)/shard_map/all_gather | solution.py:585
  13.1 20.4 %collective-permute-start.3 = (bf16[128,1664]{1,0:T(8,128)(2,1)S(1)}, bf16[128,1664]{1,0:T(8,128)(2,1)S(1)}, u32[]{:S(2)}, u32[]{:S(2)}) collective-permute-start(bf16[128,1664]{1,0:T(8,128)(2,1)S(1)} %get-tuple-element.111), channel_id=1, source_target_pairs={{0,16},{4,20},{8,24},{12,28},{16,0},{20,4},{24,8},{28,12},{1,17},{... | collective-permute-start | bytes 1277960 | tf_op jit(solution)/shard_map/ppermute | solution.py:495
  14.6 18.9 %collective-permute-start.5 = (bf16[128,1664]{1,0:T(8,128)(2,1)S(1)}, bf16[128,1664]{1,0:T(8,128)(2,1)S(1)}, u32[]{:S(2)}, u32[]{:S(2)}) collective-permute-start(bf16[128,1664]{1,0:T(8,128)(2,1)S(1)} %get-tuple-element.111), channel_id=1, source_target_pairs={{0,24},{4,28},{8,16},{12,20},{16,8},{20,12},{24,0},{28,4},{1,25},{... | collective-permute-start | bytes 1277960 | tf_op jit(solution)/shard_map/ppermute | solution.py:495
  14.6 19.4 %collective-permute-start = (bf16[128,1664]{1,0:T(8,128)(2,1)S(1)}, bf16[128,1664]{1,0:T(8,128)(2,1)S(1)}, u32[]{:S(2)}, u32[]{:S(2)}) collective-permute-start(bf16[128,1664]{1,0:T(8,128)(2,1)S(1)} %get-tuple-element.111), channel_id=1, source_target_pairs={{0,4},{4,0},{8,12},{12,8},{16,20},{20,16},{24,28},{28,24},{1,5},{5... | collective-permute-start | bytes 1277960 | tf_op jit(solution)/shard_map/ppermute | solution.py:495
  17.4 174.8 %reduce-scatter.5.cloned.1.call-start = ((), (), s32[]{:S(2)}) async-start(), calls=%async_computation.5 | async-start | bytes 2621440 | tf_op jit(solution)/shard_map/reduce_scatter | solution.py:595
  39.5 32.9 %collective-permute-start.7 = (bf16[2624,128]{1,0:T(8,128)(2,1)S(1)}, bf16[2624,128]{1,0:T(8,128)(2,1)S(1)}, u32[]{:S(2)}, u32[]{:S(2)}) collective-permute-start(bf16[2624,128]{1,0:T(8,128)(2,1)S(1)} %pad_maximum_fusion.6), channel_id=1, source_target_pairs={{0,4},{4,0},{8,12},{12,8},{16,20},{20,16},{24,28},{28,24},{1,5},{5... | collective-permute-start | bytes 2015240 | tf_op jit(solution)/shard_map/ppermute | solution.py:495
  39.6 18.0 %collective-permute-start.8 = (bf16[2624,128]{1,0:T(8,128)(2,1)S(1)}, bf16[2624,128]{1,0:T(8,128)(2,1)S(1)}, u32[]{:S(2)}, u32[]{:S(2)}) collective-permute-start(bf16[2624,128]{1,0:T(8,128)(2,1)S(1)} %pad_maximum_fusion.6), channel_id=1, source_target_pairs={{0,8},{4,12},{8,0},{12,4},{16,24},{20,28},{24,16},{28,20},{1,9},{5... | collective-permute-start | bytes 2015240 | tf_op jit(solution)/shard_map/ppermute | solution.py:495
  40.8 30.0 %collective-permute-start.10 = (bf16[2624,128]{1,0:T(8,128)(2,1)S(1)}, bf16[2624,128]{1,0:T(8,128)(2,1)S(1)}, u32[]{:S(2)}, u32[]{:S(2)}) collective-permute-start(bf16[2624,128]{1,0:T(8,128)(2,1)S(1)} %pad_maximum_fusion.6), channel_id=1, source_target_pairs={{0,16},{4,20},{8,24},{12,28},{16,0},{20,4},{24,8},{28,12},{1,17},{... | collective-permute-start | bytes 2015240 | tf_op jit(solution)/shard_map/ppermute | solution.py:495
  41.6 30.8 %collective-permute-start.12 = (bf16[2624,128]{1,0:T(8,128)(2,1)S(1)}, bf16[2624,128]{1,0:T(8,128)(2,1)S(1)}, u32[]{:S(2)}, u32[]{:S(2)}) collective-permute-start(bf16[2624,128]{1,0:T(8,128)(2,1)S(1)} %pad_maximum_fusion.6), channel_id=1, source_target_pairs={{0,24},{4,28},{8,16},{12,20},{16,8},{20,12},{24,0},{28,4},{1,25},{... | collective-permute-start | bytes 2015240 | tf_op jit(solution)/shard_map/ppermute | solution.py:495
  57.5 16.8 %collective-permute-start.9 = (bf16[2624,128]{1,0:T(8,128)(2,1)S(1)}, bf16[2624,128]{1,0:T(8,128)(2,1)S(1)}, u32[]{:S(2)}, u32[]{:S(2)}) collective-permute-start(bf16[2624,128]{1,0:T(8,128)(2,1)S(1)} %collective-permute-done.8), channel_id=1, source_target_pairs={{0,4},{4,0},{8,12},{12,8},{16,20},{20,16},{24,28},{28,24},{1,5},{5... | collective-permute-start | bytes 2015240 | tf_op jit(solution)/shard_map/ppermute | solution.py:495
  147.3 92.4 %all-gather.7.cloned.1.call-start = ((), (), s32[]{:S(2)}) async-start(), calls=%async_computation.6 | async-start | bytes 2621440 | tf_op jit(solution)/shard_map/all_gather | solution.py:600
  194.7 91.5 %all-gather.9.cloned.1.call-start = ((), (), s32[]{:S(2)}) async-start(), calls=%async_computation.7 | async-start | bytes 2621440 | tf_op jit(solution)/shard_map/all_gather | solution.py:593
  195.3 149.2 %reduce-scatter.7.cloned.1.call-start = ((), (), s32[]{:S(2)}) async-start(), calls=%async_computation.8 | async-start | bytes 2621440 | tf_op jit(solution)/shard_map/reduce_scatter | solution.py:609
  301.9 90.8 %all-gather.11.cloned.1.call-start = ((), (), s32[]{:S(2)}) async-start(), calls=%async_computation.9 | async-start | bytes 2621440 | tf_op jit(solution)/shard_map/all_gather | solution.py:619
  347.8 186.3 %reduce-scatter.9.cloned.1.call-start = ((), (), s32[]{:S(2)}) async-start(), calls=%async_computation.10 | async-start | bytes 2621440 | tf_op jit(solution)/shard_map/reduce_scatter | solution.py:621
  355.2 43.3 %collective-permute-start.32 = (bf16[1408,512]{1,0:T(8,128)(2,1)}, bf16[1408,512]{1,0:T(8,128)(2,1)}, u32[]{:S(2)}, u32[]{:S(2)}) collective-permute-start(bf16[1408,512]{1,0:T(8,128)(2,1)} %pad_maximum_fusion.4), channel_id=1, source_target_pairs={{0,4},{4,0},{8,12},{12,8},{16,20},{20,16},{24,28},{28,24},{1,5},{5... | collective-permute-start | bytes 4325384 | tf_op jit(solution)/shard_map/ppermute | solution.py:495
  360.2 32.6 %collective-permute-start.36 = (bf16[704,512]{1,0:T(8,128)(2,1)}, bf16[704,512]{1,0:T(8,128)(2,1)}, u32[]{:S(2)}, u32[]{:S(2)}) collective-permute-start(bf16[704,512]{1,0:T(8,128)(2,1)} %pad_maximum_fusion.5), channel_id=1, source_target_pairs={{0,4},{4,0},{8,12},{12,8},{16,20},{20,16},{24,28},{28,24},{1,5},{5... | collective-permute-start | bytes 2162696 | tf_op jit(solution)/shard_map/ppermute | solution.py:495
  392.8 143.6 %reduce-scatter.11.cloned.1.call-start = ((), (), s32[]{:S(2)}) async-start(), calls=%async_computation.11 | async-start | bytes 2621440 | tf_op jit(solution)/shard_map/reduce_scatter | solution.py:629
  397.4 15.4 %collective-permute-start.38 = (bf16[704,128]{1,0:T(8,128)(2,1)}, bf16[704,128]{1,0:T(8,128)(2,1)}, u32[]{:S(2)}, u32[]{:S(2)}) collective-permute-start(bf16[704,128]{1,0:T(8,128)(2,1)} %get-tuple-element.97), channel_id=1, source_target_pairs={{0,16},{4,20},{8,24},{12,28},{16,0},{20,4},{24,8},{28,12},{1,17},{... | collective-permute-start | bytes 540680 | tf_op jit(solution)/shard_map/ppermute | solution.py:495
  398.0 14.9 %collective-permute-start.37 = (bf16[704,128]{1,0:T(8,128)(2,1)}, bf16[704,128]{1,0:T(8,128)(2,1)}, u32[]{:S(2)}, u32[]{:S(2)}) collective-permute-start(bf16[704,128]{1,0:T(8,128)(2,1)} %get-tuple-element.95), channel_id=1, source_target_pairs={{0,8},{4,12},{8,0},{12,4},{16,24},{20,28},{24,16},{28,20},{1,9},{5... | collective-permute-start | bytes 540680 | tf_op jit(solution)/shard_map/ppermute | solution.py:495
  401.0 14.0 %collective-permute-start.35 = (bf16[1408,128]{1,0:T(8,128)(2,1)}, bf16[1408,128]{1,0:T(8,128)(2,1)S(1)}, u32[]{:S(2)}, u32[]{:S(2)}) collective-permute-start(bf16[1408,128]{1,0:T(8,128)(2,1)} %get-tuple-element.85), channel_id=1, source_target_pairs={{0,24},{4,28},{8,16},{12,20},{16,8},{20,12},{24,0},{28,4},{1,25},{... | collective-permute-start | bytes 1081352 | tf_op jit(solution)/shard_map/ppermute | solution.py:495
  403.3 18.2 %collective-permute-start.34 = (bf16[1408,128]{1,0:T(8,128)(2,1)}, bf16[1408,128]{1,0:T(8,128)(2,1)}, u32[]{:S(2)}, u32[]{:S(2)}) collective-permute-start(bf16[1408,128]{1,0:T(8,128)(2,1)} %get-tuple-element.86), channel_id=1, source_target_pairs={{0,16},{4,20},{8,24},{12,28},{16,0},{20,4},{24,8},{28,12},{1,17},{... | collective-permute-start | bytes 1081352 | tf_op jit(solution)/shard_map/ppermute | solution.py:495
  403.9 17.7 %collective-permute-start.33 = (bf16[1408,128]{1,0:T(8,128)(2,1)}, bf16[1408,128]{1,0:T(8,128)(2,1)}, u32[]{:S(2)}, u32[]{:S(2)}) collective-permute-start(bf16[1408,128]{1,0:T(8,128)(2,1)} %get-tuple-element.84), channel_id=1, source_target_pairs={{0,8},{4,12},{8,0},{12,4},{16,24},{20,28},{24,16},{28,20},{1,9},{5... | collective-permute-start | bytes 1081352 | tf_op jit(solution)/shard_map/ppermute | solution.py:495
  471.5 16.8 %collective-permute-start.19 = (f32[7,1024]{1,0:T(8,128)S(1)}, f32[7,1024]{1,0:T(8,128)S(1)}, u32[]{:S(2)}, u32[]{:S(2)}) collective-permute-start(f32[7,1024]{1,0:T(8,128)S(1)} %pad_maximum_fusion.8), channel_id=1, source_target_pairs={{0,24},{4,28},{8,16},{12,20},{16,8},{20,12},{24,0},{28,4},{1,25},{... | collective-permute-start | bytes 86024 | tf_op jit(solution)/shard_map/ppermute | solution.py:495
  473.4 15.0 %collective-permute-start.20 = (f32[7,1024]{1,0:T(8,128)S(1)}, f32[7,1024]{1,0:T(8,128)S(1)}, u32[]{:S(2)}, u32[]{:S(2)}) collective-permute-start(f32[7,1024]{1,0:T(8,128)S(1)} %pad_maximum_fusion.8), channel_id=1, source_target_pairs={{0,28},{4,24},{8,20},{12,16},{16,12},{20,8},{24,4},{28,0},{1,29},{... | collective-permute-start | bytes 86024 | tf_op jit(solution)/shard_map/ppermute | solution.py:495
  473.6 16.3 %collective-permute-start.17 = (f32[7,1024]{1,0:T(8,128)S(1)}, f32[7,1024]{1,0:T(8,128)S(1)}, u32[]{:S(2)}, u32[]{:S(2)}) collective-permute-start(f32[7,1024]{1,0:T(8,128)S(1)} %pad_maximum_fusion.8), channel_id=1, source_target_pairs={{0,16},{4,20},{8,24},{12,28},{16,0},{20,4},{24,8},{28,12},{1,17},{... | collective-permute-start | bytes 86024 | tf_op jit(solution)/shard_map/ppermute | solution.py:495
  475.2 14.7 %collective-permute-start.18 = (f32[7,1024]{1,0:T(8,128)S(1)}, f32[7,1024]{1,0:T(8,128)S(1)}, u32[]{:S(2)}, u32[]{:S(2)}) collective-permute-start(f32[7,1024]{1,0:T(8,128)S(1)} %pad_maximum_fusion.8), channel_id=1, source_target_pairs={{0,20},{4,16},{8,28},{12,24},{16,4},{20,0},{24,12},{28,8},{1,21},{... | collective-permute-start | bytes 86024 | tf_op jit(solution)/shard_map/ppermute | solution.py:495
  475.9 14.5 %collective-permute-start.15 = (f32[7,1024]{1,0:T(8,128)S(1)}, f32[7,1024]{1,0:T(8,128)S(1)}, u32[]{:S(2)}, u32[]{:S(2)}) collective-permute-start(f32[7,1024]{1,0:T(8,128)S(1)} %pad_maximum_fusion.8), channel_id=1, source_target_pairs={{0,8},{4,12},{8,0},{12,4},{16,24},{20,28},{24,16},{28,20},{1,9},{5... | collective-permute-start | bytes 86024 | tf_op jit(solution)/shard_map/ppermute | solution.py:495
  489.9 17.2 %collective-permute-start.24 = (bf16[512,1664]{1,0:T(8,128)(2,1)S(1)}, bf16[512,1664]{1,0:T(8,128)(2,1)}, u32[]{:S(2)}, u32[]{:S(2)}) collective-permute-start(bf16[512,1664]{1,0:T(8,128)(2,1)S(1)} %pad_maximum_fusion.3), channel_id=1, source_target_pairs={{0,4},{4,0},{8,12},{12,8},{16,20},{20,16},{24,28},{28,24},{1,5},{5... | collective-permute-start | bytes 5111816 | tf_op jit(solution)/shard_map/ppermute | solution.py:495
  509.1 13.8 %collective-permute-start.27 = (bf16[128,1664]{1,0:T(8,128)(2,1)S(1)}, bf16[128,1664]{1,0:T(8,128)(2,1)S(1)}, u32[]{:S(2)}, u32[]{:S(2)}) collective-permute-start(bf16[128,1664]{1,0:T(8,128)(2,1)S(1)} %get-tuple-element.82), channel_id=1, source_target_pairs={{0,24},{4,28},{8,16},{12,20},{16,8},{20,12},{24,0},{28,4},{1,25},{... | collective-permute-start | bytes 1277960 | tf_op jit(solution)/shard_map/ppermute | solution.py:495
  511.3 19.8 %collective-permute-start.26 = (bf16[128,1664]{1,0:T(8,128)(2,1)S(1)}, bf16[128,1664]{1,0:T(8,128)(2,1)S(1)}, u32[]{:S(2)}, u32[]{:S(2)}) collective-permute-start(bf16[128,1664]{1,0:T(8,128)(2,1)S(1)} %get-tuple-element.83), channel_id=1, source_target_pairs={{0,16},{4,20},{8,24},{12,28},{16,0},{20,4},{24,8},{28,12},{1,17},{... | collective-permute-start | bytes 1277960 | tf_op jit(solution)/shard_map/ppermute | solution.py:495
  511.9 19.2 %collective-permute-start.25 = (bf16[128,1664]{1,0:T(8,128)(2,1)S(1)}, bf16[128,1664]{1,0:T(8,128)(2,1)S(1)}, u32[]{:S(2)}, u32[]{:S(2)}) collective-permute-start(bf16[128,1664]{1,0:T(8,128)(2,1)S(1)} %get-tuple-element.81), channel_id=1, source_target_pairs={{0,8},{4,12},{8,0},{12,4},{16,24},{20,28},{24,16},{28,20},{1,9},{5... | collective-permute-start | bytes 1277960 | tf_op jit(solution)/shard_map/ppermute | solution.py:495
  (41 other events, 343.7 us)
Sparse Core Ops, SparseCore 0:
  17.5 47.5 all-gather.4
  147.5 44.6 reduce-scatter.4
  194.8 44.8 all-gather.6
  241.7 44.4 all-gather.8
  302.1 42.4 reduce-scatter.6
  347.9 44.8 all-gather.10
  395.1 42.4 reduce-scatter.8
  477.6 43.7 reduce-scatter.10

commit v3 on v2

--- a/solution.py
+++ b/solution.py
@@ -23,12 +23,6 @@
 def split(value):
     high = value.astype(BF16)
     return high, (value - high.astype(F32)).astype(BF16)
-
-
-def dot1(left, right, dims=NN):
-    return lax.dot_general(
-        left.astype(BF16), right.astype(BF16), dims, preferred_element_type=F32
-    )
 
 
 def dot3(left, right, dims=NN):
@@ -334,7 +328,7 @@
     return rows, before, after, whole, saved
 
 
-def saved_shapes(heads, chunks):
+def saved_shapes():
     sizes = ((CHUNK, CHUNK), (CHUNK, DK + DV), (CHUNK, CHUNK), (CHUNK, CHUNK), (2 * CHUNK, DK), (DK, DV))
     return sizes
 
@@ -343,8 +337,8 @@
     length, width = projected.shape
     heads = (width - CHUNK) // HEADW
     chunks = length // CHUNK
-    rows, before, after, whole, saved = chunk_specs(heads, chunks, lambda c: c)
-    sizes = saved_shapes(heads, chunks)
+    rows, before, _, whole, saved = chunk_specs(heads, chunks, lambda c: c)
+    sizes = saved_shapes()
     return pl.pallas_call(
         functools.partial(forward_kernel, heads),
         grid=(chunks,),
@@ -369,7 +363,7 @@
     heads = (width - CHUNK) // HEADW
     chunks = length // CHUNK
     rows, before, after, whole, saved = chunk_specs(heads, chunks, lambda c: chunks - 1 - c)
-    sizes = saved_shapes(heads, chunks)
+    sizes = saved_shapes()
     return pl.pallas_call(
         functools.partial(backward_kernel, heads, chunks),
         grid=(chunks,),
@@ -436,9 +430,9 @@
     normed_out[...] = (resid * row_scale(resid) * gain_ref[...]).astype(BF16)
 
 
-def ffn_back_kernel(me_ref, resid_ref, cot_ref, grad_ref, gain_ref, d_resid_out, d_mixed_out, d_gain_out):
+def ffn_back_kernel(me_ref, resid_ref, cot_ref, grad_ref, mate_ref, gain_ref, d_resid_out, d_mixed_out, d_gain_out):
     resid = resid_ref[...]
-    grad = grad_ref[...].astype(F32)
+    grad = grad_ref[...].astype(F32) + mate_ref[...].astype(F32)
     scale = row_scale(resid)
     unit = resid * scale
     weighted = grad * gain_ref[...]
@@ -451,10 +445,11 @@
         d_gain_out[:, block_source(me_ref, p, CHUNK)] = sums[:, p * CHUNK : (p + 1) * CHUNK]
 
 
-def output_kernel(me_ref, resid_ref, ffn_ref, out_ref):
+def output_kernel(me_ref, resid_ref, own_ref, mate_ref, out_ref):
     for p in range(resid_ref.shape[1] // CHUNK):
         here = pl.ds(p * CHUNK, CHUNK)
-        total = resid_ref[:, here] + ffn_ref[:, here].astype(F32)
+        ffn = own_ref[:, here].astype(F32) + mate_ref[:, here].astype(F32)
+        total = resid_ref[:, here] + ffn
         out_ref[:, block_source(me_ref, p, CHUNK)] = total.astype(BF16)
 
 
@@ -476,7 +471,94 @@
         out_ref[:, block_source(me_ref, p, CHUNK)] = total[:, p * CHUNK : (p + 1) * CHUNK]
 
 
-def row_call(kernel, name, outs, *args):
+UNIT_STEPS = 2
+
+
+def feed_kernel(
+    tok_ref, cot_ref, *refs,
+):
+    weights, outs = (refs[:3], refs[3:6]), (refs[6:9], refs[9:12])
+    d_out, y_out, d_total, y_total = refs[12:]
+    step = pl.program_id(0)
+
+    @pl.when(step == 0)
+    def _():
+        d_total[...] = jnp.zeros_like(d_total)
+        y_total[...] = jnp.zeros_like(y_total)
+
+    tokens, cots = tok_ref[...], cot_ref[...]
+    for (gate_w, up_w, down_w), (gate_out, up_out, hidden_out) in zip(weights, outs):
+        gate_pre = times_transposed(gate_w[...], tokens)
+        up_pre = times_transposed(up_w[...], tokens)
+        d_hidden = times_transposed(down_w[...], cots)
+        sig = sigmoid(gate_pre)
+        silu = gate_pre * sig
+        hidden = (silu * up_pre).astype(BF16)
+        d_up = (d_hidden * silu).astype(BF16)
+        d_gate = (d_hidden * up_pre * (sig * (1.0 + gate_pre * (1.0 - sig)))).astype(BF16)
+        gate_out[...] = d_gate
+        up_out[...] = d_up
+        hidden_out[...] = hidden
+        d_total[...] += transposed_times(d_gate, gate_w[...]) + transposed_times(d_up, up_w[...])
+        y_total[...] += transposed_times(hidden, down_w[...])
+
+    @pl.when(step == UNIT_STEPS - 1)
+    def _():
+        d_out[...] = d_total[...].astype(BF16)
+        y_out[...] = y_total[...].astype(BF16)
+
+
+def feed_call(tokens, cots, near, far):
+    count, features = tokens.shape
+    quarter = near.shape[0] // 3
+    block = quarter // UNIT_STEPS
+
+    def part(index):
+        return pl.BlockSpec((block, features), lambda i: (UNIT_STEPS * index + i, 0))
+
+    whole = pl.BlockSpec((count, features), lambda i: (0, 0))
+    unit_out = pl.BlockSpec((block, count), lambda i: (i, 0))
+    outs = pl.pallas_call(
+        feed_kernel,
+        grid=(UNIT_STEPS,),
+        in_specs=[whole, whole] + [part(index) for index in range(3)] * 2,
+        out_specs=[unit_out] * 6 + [whole, whole],
+        out_shape=[jax.ShapeDtypeStruct((quarter, count), BF16)] * 6
+        + [jax.ShapeDtypeStruct((count, features), BF16)] * 2,
+        scratch_shapes=[pltpu.VMEM((count, features), F32)] * 2,
+    )(tokens, cots, near, near, near, far, far, far)
+    return outs[:3], outs[3:6], outs[6], outs[7]
+
+
+def unit_grad_kernel(
+    gate_o, up_o, hid_o, gate_m, up_m, hid_m, tok_o, tok_m, cot_o, cot_m, keep_out, sent_out
+):
+    quarter = gate_o.shape[0]
+    for index, (own, mate, x_own, x_mate) in enumerate(
+        ((gate_o, gate_m, tok_o, tok_m), (up_o, up_m, tok_o, tok_m), (hid_o, hid_m, cot_o, cot_m))
+    ):
+        total = (times(own[...], x_own[...]) + times(mate[...], x_mate[...])).astype(BF16)
+        rows = slice(index * quarter, (index + 1) * quarter)
+        for p in range(8):
+            target = sent_out if p % 2 else keep_out
+            target[rows, p // 2 * CHUNK : (p // 2 + 1) * CHUNK] = total[:, p * CHUNK : (p + 1) * CHUNK]
+
+
+def unit_grads(own, mate, tok_o, tok_m, cot_o, cot_m):
+    if not small_dp():
+        pre = [times(own[i], tok_o) + times(mate[i], tok_m) for i in range(2)]
+        down = times(own[2], cot_o) + times(mate[2], cot_m)
+        return [jnp.concatenate(pre + [down], axis=0).astype(BF16)]
+    half = ((3 * own[0].shape[0], tok_o.shape[1] // 2), BF16)
+    keep, sent = row_call(unit_grad_kernel, [half, half], *own, *mate, tok_o, tok_m, cot_o, cot_m)
+    got = swap(sent, "dp", 1)
+    return [
+        (mine.astype(F32) + other.astype(F32)).astype(BF16)
+        for mine, other in zip(jnp.split(keep, 4, axis=1), jnp.split(got, 4, axis=1))
+    ]
+
+
+def row_call(kernel, outs, *args):
     def space(arg):
         kind = pltpu.SMEM if arg.dtype == jnp.int32 else pltpu.VMEM
         return pl.BlockSpec(memory_space=kind)
@@ -486,7 +568,6 @@
         in_specs=[space(a) for a in args],
         out_specs=[pl.BlockSpec(memory_space=pltpu.VMEM)] * len(outs),
         out_shape=[jax.ShapeDtypeStruct(s, d) for s, d in outs],
-        name=name,
     )(*args)
 
 
@@ -495,35 +576,64 @@
     return lax.ppermute(value, axis, pairs)
 
 
+def planar_swaps(blocks):
+    moved = [blocks[0]]
+    for q in range(1, 4):
+        moved.append(swap(blocks[q], "dp", 2 * q))
+    return moved
+
+
 def small_dp():
     return lax.axis_size("dp") == 8
 
 
-def gather_pieces(own):
-    across = [own] + [swap(own, "dp", 2 * q) for q in range(1, 4)]
-    beside = [swap(piece, "dp", 1) for piece in across]
-    return [piece for pair in zip(across, beside) for piece in pair]
-
-
-def gather_dp(own, axis):
-    if small_dp():
-        return jnp.concatenate(gather_pieces(own), axis=axis)
-    return lax.all_gather(own, "dp", axis=axis, tiled=True)
-
-
-def scatter_dp(partial, axis):
+def planar_dp(own):
     if not small_dp():
-        return lax.psum_scatter(partial, "dp", scatter_dimension=axis, tiled=True).astype(F32)
-    blocks = jnp.split(partial, 8, axis=axis)
+        return [own]
+    return planar_swaps([own] * 4)
+
+
+def core_dp(across):
+    return [swap(piece, "dp", 1) for piece in across] if small_dp() else []
+
+
+def join_dp(across, beside, axis):
+    if not small_dp():
+        return lax.all_gather(across[0], "dp", axis=axis, tiled=True)
+    return jnp.concatenate([piece for pair in zip(across, beside) for piece in pair], axis=axis)
+
+
+def beside_dp(across, axis):
+    return join_dp(across, core_dp(across), axis)
+
+
+def core_sum(blocks, axis):
     sent = swap(jnp.concatenate(blocks[1::2], axis=axis), "dp", 1)
-    halves = [
+    return [
         (mine.astype(F32) + other.astype(F32)).astype(BF16)
         for mine, other in zip(blocks[0::2], jnp.split(sent, 4, axis=axis))
     ]
-    total = halves[0].astype(F32)
-    for q in range(1, 4):
-        total = total + swap(halves[q], "dp", 2 * q).astype(F32)
-    return total
+
+
+def core_half(partials):
+    if not small_dp():
+        return [jnp.concatenate(partials, axis=0)]
+    split = [jnp.split(partial, 8, axis=1) for partial in partials]
+    return core_sum([jnp.concatenate(group, axis=0) for group in zip(*split)], 1)
+
+
+def core_rows_half(partial):
+    return core_sum(jnp.split(partial, 8, axis=0), 0) if small_dp() else [partial]
+
+
+def planar_move(half, axis):
+    if not small_dp():
+        return [lax.psum_scatter(half[0], "dp", scatter_dimension=axis, tiled=True)]
+    return planar_swaps(half)
+
+
+def planar_sum(half, axis):
+    return sum(piece.astype(F32) for piece in planar_move(half, axis))
 
 
 def tree_sum(value, axis):
@@ -537,7 +647,7 @@
     return lax.optimization_barrier((value, anchor))[0]
 
 
-def local(
+def layer(
     inputs,
     segments,
     cotangent,
@@ -576,62 +686,65 @@
     token_bf, token_f32 = ((rows, features), BF16), ((rows, features), F32)
     gain_shape = ((1, features), F32)
     x, cot, normed, gain_in, gain_ffn = row_call(
-        prepare_kernel, "prepare", [token_bf, token_bf, token_bf, gain_shape, gain_shape],
+        prepare_kernel, [token_bf, token_bf, token_bf, gain_shape, gain_shape],
         me, inputs, cotangent, norm_in[None], norm_ffn[None],
     )
     joined = jnp.concatenate(
         [w_in, jnp.pad(w_alpha_beta, ((0, 0), (0, CHUNK - w_alpha_beta.shape[1])))], axis=1
     )
+    units = jnp.concatenate([w_gate.T, w_up.T, w_down], axis=0)
     seq_rows = lax.all_gather(normed, "tensor", axis=0, tiled=True)
-    whole_in = gather_dp(joined, 0)
-    unit_weights = jnp.concatenate([w_gate.T, w_up.T, w_down, w_out], axis=0)
-    whole_units = gather_dp(after(unit_weights, whole_in), 1)
-    whole_pre = whole_units[: 2 * hidden_units]
-    whole_down = whole_units[2 * hidden_units : 3 * hidden_units]
-    whole_out = whole_units[3 * hidden_units :]
+    joined, out_block = after((joined, w_out), normed)
+    whole_in = beside_dp(planar_dp(joined), 0)
+    whole_out = beside_dp(planar_dp(out_block), 1)
+    near = planar_dp(after(units, (whole_in, whole_out)))
+    far_units = swap(after(units, seq_rows), "tensor", 2)
+    mate_cot = swap(after(cot, seq_rows), "tensor", 1)
     projected = times(seq_rows, whole_in)
-    back_seq = lax.all_gather(after(cot, seq_rows), "tensor", axis=0, tiled=True)
     gated, *kept = mixer_forward(projected, docs, conv_mine, vectors, gain_row)
-    mixed = lax.psum_scatter(
-        times(gated, whole_out).astype(BF16), "tensor", scatter_dimension=0, tiled=True
+    mixed_part = times(gated, whole_out).astype(BF16)
+    mixed = lax.psum_scatter(mixed_part, "tensor", scatter_dimension=0, tiled=True)
+    far = planar_dp(after(far_units, gated))
+    near = after(near, gated)
+    weights = [beside_dp(near, 1), beside_dp(far, 1)]
+    mixed, weights, mate_cot = lax.optimization_barrier((mixed, weights, mate_cot))
+    resid, normed_ffn = row_call(middle_kernel, [token_f32, token_bf], x, mixed, gain_ffn)
+
+    mate_normed = swap(normed_ffn, "tensor", 1)
+    near_own, far_own, d_own, out_own = feed_call(normed_ffn, cot, *weights)
+    near_mate, far_mate, d_mate, out_mate = feed_call(mate_normed, mate_cot, *weights)
+    d_from_mate = swap(d_mate, "tensor", 1)
+    activations_all = (normed_ffn, mate_normed, cot, mate_cot)
+    far_half = unit_grads(after(far_own, d_mate), far_mate, *activations_all)
+    near_half = unit_grads(after(near_own, far_half), near_mate, *activations_all)
+    d_resid, d_mixed, gain_ffn_part = row_call(
+        ffn_back_kernel, [token_f32, token_bf, gain_shape],
+        me, resid, cot, d_own, d_from_mate, gain_ffn,
     )
-    resid, normed_ffn = row_call(middle_kernel, "middle", [token_f32, token_bf], x, mixed, gain_ffn)
-
-    ffn_seq = lax.all_gather(normed_ffn, "tensor", axis=0, tiled=True)
-    pre = times_transposed(whole_pre, ffn_seq)
-    gate_pre, up_pre = pre[:hidden_units], pre[hidden_units:]
-    d_hidden = times_transposed(whole_down, back_seq)
-    sig = jax.nn.sigmoid(gate_pre)
-    hidden = (gate_pre * sig * up_pre).astype(BF16)
-    d_up = (d_hidden * gate_pre * sig).astype(BF16)
-    d_gate = (d_hidden * up_pre * sig * (1.0 + gate_pre * (1.0 - sig))).astype(BF16)
-    d_pre = jnp.concatenate([d_gate, d_up], axis=0)
-    d_normed_ffn = lax.psum_scatter(
-        transposed_times(d_pre, whole_pre).astype(BF16), "tensor", scatter_dimension=0, tiled=True
-    )
-    grad_pre = scatter_dp(times(d_pre, ffn_seq).astype(BF16), 1)
-    grad_down = scatter_dp(times(hidden, back_seq).astype(BF16), 1)
-    d_resid, d_mixed, gain_ffn_part = row_call(
-        ffn_back_kernel, "ffn_back", [token_f32, token_bf, gain_shape],
-        me, resid, cot, d_normed_ffn, gain_ffn,
-    )
 
     mixer_back_seq = lax.all_gather(d_mixed, "tensor", axis=0, tiled=True)
-    ffn_part = after(transposed_times(hidden, whole_down).astype(BF16), mixer_back_seq)
-    ffn_out = lax.psum_scatter(ffn_part, "tensor", scatter_dimension=0, tiled=True)
-    (output,) = row_call(output_kernel, "output", [token_bf], me, resid, ffn_out)
+    far_grad = planar_sum(far_half, 1).astype(BF16)
+    near_half, far_grad = lax.optimization_barrier((near_half, far_grad))
+    out_mate = after(out_mate, mixer_back_seq)
+    from_far = swap(far_grad, "tensor", 2)
+    near_moved = planar_move(near_half, 1)
+    out_from_mate = swap(out_mate, "tensor", 1)
     d_gated = times_transposed(mixer_back_seq, whole_out)
-    grad_out = scatter_dp(transposed_times(gated, mixer_back_seq).astype(BF16), 1)
     d_projected, d_conv, d_vectors, d_gain_out = mixer_backward(
         projected, docs, conv_mine, vectors, gain_row, kept, d_gated
     )
     d_part = times_transposed(d_projected, whole_in).astype(BF16)
     d_normed_in = lax.psum_scatter(d_part, "tensor", scatter_dimension=0, tiled=True)
-    grad_joined = scatter_dp(transposed_times(seq_rows, d_projected).astype(BF16), 0)
-    (gain_in_part,) = row_call(gain_kernel, "gain", [gain_shape], me, d_part, seq_rows, gain_in)
-    (d_inputs,) = row_call(
-        finish_kernel, "finish", [token_f32], me, x, d_resid, d_normed_in, gain_in
-    )
+    seq_later, gated_later, back_later = after((seq_rows, gated, mixer_back_seq), d_part)
+    joined_half = core_rows_half(transposed_times(seq_later, d_projected).astype(BF16))
+    grad_joined = planar_sum(joined_half, 0)
+    (gain_in_part,) = row_call(gain_kernel, [gain_shape], me, d_part, seq_later, gain_in)
+    out_half = core_half([transposed_times(gated_later, back_later).astype(BF16)])
+    grad_out = planar_sum(after(out_half, joined_half), 1)
+    out_from_mate, near_moved, from_far = after((out_from_mate, near_moved, from_far), joined_half)
+    (output,) = row_call(output_kernel, [token_bf], me, resid, out_own, out_from_mate)
+    grad_units = sum(piece.astype(F32) for piece in near_moved) + from_far.astype(F32)
+    (d_inputs,) = row_call(finish_kernel, [token_f32], me, x, d_resid, d_normed_in, gain_in)
 
     last = jnp.concatenate(
         [
@@ -644,6 +757,7 @@
     last = jnp.pad(last, ((0, 0), (0, conv_width - last.shape[1])))
     if conv_width == features:
         table = jnp.concatenate([d_conv, gain_in_part, gain_ffn_part, last], axis=0)
+        table = after(table, joined_half)
         table = tree_sum(table, "dp") if small_dp() else lax.psum(table, "dp")
         tables = [table] + [swap(table, "tensor", mask) for mask in range(1, parts)]
     else:
@@ -653,13 +767,13 @@
         shared = [left + right for left, right in zip(shared[0::2], shared[1::2])]
     shared = shared[0]
     grad_conv = jnp.zeros(conv_weight.shape, F32)
-    own = jnp.zeros((2, a_log.shape[0]), F32)
+    own_rows = jnp.zeros((2, a_log.shape[0]), F32)
     width = out_gain.shape[0]
     for mask, t in enumerate(tables):
         place_index = part_index ^ mask
         grad_conv = lax.dynamic_update_slice_in_dim(grad_conv, t[:4], place_index * conv_width, 1)
         pair = t[6, width : width + 4 * head_count].reshape(2, 2 * head_count)[:, ::2]
-        own = lax.dynamic_update_slice_in_dim(own, pair, place_index * head_count, 1)
+        own_rows = lax.dynamic_update_slice_in_dim(own_rows, pair, place_index * head_count, 1)
     columns = w_in.shape[1]
     return (
         output,
@@ -668,20 +782,20 @@
         grad_joined[:, :columns],
         grad_joined[:, columns : columns + w_alpha_beta.shape[1]],
         grad_conv,
-        own[0],
-        own[1],
+        own_rows[0],
+        own_rows[1],
         shared[2, :width],
         grad_out,
         shared[1],
-        grad_pre[:hidden_units].T,
-        grad_pre[hidden_units:].T,
-        grad_down,
+        grad_units[:hidden_units].T,
+        grad_units[hidden_units : 2 * hidden_units].T,
+        grad_units[2 * hidden_units :],
     )
 
 
 def solution(mesh):
     return jax.shard_map(
-        local,
+        layer,
         mesh=mesh,
         in_specs=(
             P(("dp", "tensor"), None),

time: 555 us -> 460 us (0.83)
  waiting for transfers between devices: 279 us -> 162 us
  Pallas kernels: 103 us -> 142 us
  matrix products: 66.1 us -> 36 us
  starting transfers between devices: 35.4 us -> 50.7 us
    all_gather x4 -> x2, waiting for transfers between devices: 110 us -> 28.8 us  [the longest x1 28.8 us: layer(): mixer_back_seq = lax.all_gather(d_mixed, 'tensor', axis=0, tiled=True)]
    reduce_scatter x4 -> x2, waiting for transfers between devices: 87.3 us -> 9.4 us  [the longest x1 9.4 us: layer(): lax.psum_scatter(mixed_part, 'tensor', scatter_dimension=0, tiled=True)]
    ppermute x40 -> x60, waiting for transfers between devices: 80.3 us -> 123 us  [swap(): return lax.ppermute(value, axis, pairs)]
    pallas_call x0 -> x2, Pallas kernels: none -> 26.1 us  [feed_call(): pl.pallas_call(feed_kernel, grid=(UNIT_STEPS,), in_specs=[whole, whole] +...]
    ppermute x40 -> x60, starting transfers between devices: 34.7 us -> 50.2 us  [swap(): return lax.ppermute(value, axis, pairs)]
    dot_general x4 -> x2, matrix products: 26.8 us -> 12.7 us  [times_transposed(): return lax.dot_general(left, right, NT, preferred_element_type=F32)]
    pallas_call x6 -> x8, Pallas kernels: 17 us -> 30.8 us  [row_call(): pl.pallas_call(kernel, in_specs=[space(a) for a in args], out_specs=[pl.B...]
    dot_general x4 -> x2, matrix products: 18.6 us -> 9.81 us  [transposed_times(): return lax.dot_general(left, right, TN, preferred_element_type=F32)]
  transfers between devices with their start and end apart: 48 -> 64, of which waited for: 20 -> 18; matrix products, arithmetic and copies ran while one was open for 14% -> 18% of each run, Pallas kernels for 7% -> 26%
where the time goes in v3:
time: 460 us; the launch traced here: 452 us
  waiting for transfers between devices  162 us (35%)
  Pallas kernels  142 us (31%)
  starting transfers between devices  50.7 us (11%)
  matrix products  36 us (8%)
  local copies, waits for them, and re-layouts  28.8 us (6%)
  other arithmetic  17.9 us (4%)
  between operations  15 us (3%)
    ppermute x60, waiting for transfers between devices, swap(): return lax.ppermute(value, axis, pairs)  123 us
    pallas_call x1, Pallas kernels, mixer_forward(): pl.pallas_call(functools.partial(forward_kernel, heads), grid=(chunks,),...  53.8 us
    ppermute x60, starting transfers between devices, swap(): return lax.ppermute(value, axis, pairs)  50.2 us
    pallas_call x1, Pallas kernels, mixer_backward(): pl.pallas_call(functools.partial(backward_kernel, heads, chunks), grid=(c...  31.6 us
    pallas_call x8, Pallas kernels, row_call(): pl.pallas_call(kernel, in_specs=[space(a) for a in args], out_specs=[pl.B...  30.8 us
    all_gather x1, waiting for transfers between devices, layer(): mixer_back_seq = lax.all_gather(d_mixed, 'tensor', axis=0, tiled=True)  28.8 us
    pallas_call x2, Pallas kernels, feed_call(): pl.pallas_call(feed_kernel, grid=(UNIT_STEPS,), in_specs=[whole, whole] +...  26.1 us
    unnamed x75, local copies, waits for them, and re-layouts  17.5 us
  transfers between devices with their start and end apart: 64, of which 18 were waited for; matrix products, arithmetic and copies ran while one was open for 18% of the time, Pallas kernels for 26%

profile of v3, /device:TPU:0, one launch (start us, length us, event | category | flops | bytes accessed | tf_op | source)
XLA Modules:
  0.0 452.4 jit_solution(7161295905636556071)
XLA Ops:
  7.3 2.9 shard_map.254
  22.0 6.7 %collective-permute-done.8 = bf16[512,128]{1,0:T(8,128)(2,1)S(1)} collective-permute-done((bf16[512,128]{1,0:T(8,128)(2,1)}, bf16[512,128]{1,0:T(8,128)(2,1)S(1)}, u32[]{:S(2)}, u32[]{:S(2)}) %collective-permute-start.8) | collective-permute-done | bytes 131104 | tf_op jit(solution)/shard_map/ppermute | solution.py:576
  35.7 15.1 %collective-permute-done.3 = bf16[128,1664]{1,0:T(8,128)(2,1)S(1)} collective-permute-done((bf16[128,1664]{1,0:T(8,128)(2,1)S(1)}, bf16[128,1664]{1,0:T(8,128)(2,1)S(1)}, u32[]{:S(2)}, u32[]{:S(2)}) %collective-permute-start.3) | collective-permute-done | bytes 426016 | tf_op jit(solution)/shard_map/ppermute | solution.py:576
  63.0 9.3 %fusion.8.proj_ref.before_ref = f32[1024,1664]{1,0:T(8,128)} fusion(bf16[1024,1024]{1,0:T(8,128)(2,1)} %all-gather.3.cloned.1.call-done.normed_ref, bf16[1024,1664]{1,0:T(8,128)(2,1)} %constant_dynamic-update-slice_fusion), kind=kOutput, calls=%fused_computation.91 | convolution fusion | flops 3489660928 | bytes 12320768 | tf_op jit(solution)/shard_map/dot_general | solution.py:400
  73.4 53.8 %mixer_forward.1 = (bf16[1024,512]{1,0:T(8,128)(2,1)}, f32[1024,512]{1,0:T(8,128)}, f32[8,2,128,128]{3,2,1,0:T(8,128)}, f32[8,2,128,384]{3,2,1,0:T(8,128)}, f32[...) custom-call(f32[1024,1664]{1,0:T(8,128)} %fusion.8.proj_ref.before_r, ...), custom_call_target="tpu_custom_call" | custom-call | tf_op jit(solution)/shard_map/mixer_forward/pallas_call | solution.py:342
  127.1 4.1 convolution_convert_fusion.2
  140.5 8.5 %collective-permute-done.23 = bf16[2112,128]{1,0:T(8,128)(2,1)S(1)} collective-permute-done((bf16[2112,128]{1,0:T(8,128)(2,1)S(1)}, bf16[2112,128]{1,0:T(8,128)(2,1)S(1)}, u32[]{:S(2)}, u32[]{:S(2)}) %collective-permute-start.23) | collective-permute-done | bytes 540704 | tf_op jit(solution)/shard_map/ppermute | solution.py:576
  149.0 12.7 %collective-permute-done.25 = bf16[2112,128]{1,0:T(8,128)(2,1)S(1)} collective-permute-done((bf16[2112,128]{1,0:T(8,128)(2,1)S(1)}, bf16[2112,128]{1,0:T(8,128)(2,1)S(1)}, u32[]{:S(2)}, u32[]{:S(2)}) %collective-permute-start.25) | collective-permute-done | bytes 540704 | tf_op jit(solution)/shard_map/ppermute | solution.py:576
  168.4 7.7 %collective-permute-done.29.cot_ref.cot_m = bf16[256,1024]{1,0:T(8,128)(2,1)S(1)} collective-permute-done((bf16[256,1024]{1,0:T(8,128)(2,1)S(1)}, bf16[256,1024]{1,0:T(8,128)(2,1)S(1)}, u32[]{:S(2)}, u32[]{:S(2)}) %collective-permute-start.29) | collective-permute-done | bytes 524320 | tf_op jit(solution)/shard_map/ppermute | solution.py:576
  176.1 9.4 %reduce-scatter.3.cloned.1.call-done.mixed_ref = bf16[256,1024]{1,0:T(8,128)(2,1)} async-done(((bf16[1024,1024]{1,0:T(8,128)(2,1)}), bf16[256,1024]{1,0:T(8,128)(2,1)}) %reduce-scatter.3.cloned.1.call-update) | async-done | bytes 524304 | tf_op jit(solution)/shard_map/reduce_scatter | solution.py:706
  188.1 13.8 %collective-permute-done.30.tok_ref.tok_m = bf16[256,1024]{1,0:T(8,128)(2,1)S(1)} collective-permute-done((bf16[256,1024]{1,0:T(8,128)(2,1)}, bf16[256,1024]{1,0:T(8,128)(2,1)S(1)}, u32[]{:S(2)}, u32[]{:S(2)}) %collective-permute-start.30) | collective-permute-done | bytes 524320 | tf_op jit(solution)/shard_map/ppermute | solution.py:576
  202.8 13.1 %shard_map.257 = (bf16[704,256]{1,0:T(8,128)(2,1)}, bf16[704,256]{1,0:T(8,128)(2,1)}, bf16[704,256]{1,0:T(8,128)(2,1)}, bf16[704,256]{1,0:T(8,128)(2,1)}, bf16[7...) custom-call(bf16[256,1024]{1,0:T(8,128)(2,1)} %copy-done.5, ...), custom_call_target="tpu_custom_call" | custom-call | tf_op jit(solution)/shard_map/pallas_call | solution.py:521
  216.2 13.0 %shard_map.256 = (bf16[704,256]{1,0:T(8,128)(2,1)}, bf16[704,256]{1,0:T(8,128)(2,1)}, bf16[704,256]{1,0:T(8,128)(2,1)}, bf16[704,256]{1,0:T(8,128)(2,1)}, bf16[7...) custom-call(bf16[256,1024]{1,0:T(8,128)(2,1)} %get-tuple-element.113.tok_r, ...), custom_call_target="tpu_custom_call" | custom-call | tf_op jit(solution)/shard_map/pallas_call | solution.py:521
  230.1 3.4 shard_map.258
  233.8 6.6 %shard_map.259 = (bf16[2112,512]{1,0:T(8,128)(2,1)}, bf16[2112,512]{1,0:T(8,128)(2,1)}) custom-call(bf16[704,256]{1,0:T(8,128)(2,1)} %get-tuple-element.129.gate_o, bf16[704,256]{1,0:T(8,128)(2,1)} %get-tuple-element.130.up_o, bf16[704,256]{1,0:T(8,128)(2,1)} %get-tuple-element.131.hid_o, bf16[704,256]{1,0:T(8,128)(2,1)} %get-tuple-element.132.gate_m, ...), custom_call_target="tpu_custom_call" | custom-call | tf_op jit(solution)/shard_map/pallas_call | solution.py:566
  240.4 4.5 collective-permute-done.33
  251.2 28.8 %all-gather.5.cloned.1.call-done = bf16[1024,1024]{1,0:T(8,128)(2,1)} async-done(((bf16[256,1024]{1,0:T(8,128)(2,1)}), bf16[1024,1024]{1,0:T(8,128)(2,1)}) %all-gather.5.cloned.1.call-update) | async-done | bytes 2097168 | tf_op jit(solution)/shard_map/all_gather | solution.py:725
  280.0 4.4 fusion.9.grad_ref
  284.4 31.6 %mixer_backward.1 = (bf16[1024,1664]{1,0:T(8,128)(2,1)}, f32[4,1024]{1,0:T(4,128)}, f32[8,128]{1,0:T(8,128)}, f32[1,256]{1,0:T(1,128)}) custom-call(f32[1024,1664]{1,0:T(8,128)} %fusion.8.proj_ref.before_ref, f32[1024,1664]{1,0:T(8,128)} %fusion.8.proj_ref.before_ref, f32[1024,128]{1,0:T(8,128)} %broadcast_in_dim.24.doc_ref.doc_before_ref.doc_after_ref, ...), custom_call_target="tpu_custom_call" | custom-call | tf_op jit(solution)/shard_map/mixer_backward/pallas_call | solution.py:367
  316.1 8.3 %convolution_convert_fusion.1.grad_ref = bf16[1024,1024]{1,0:T(8,128)(2,1)} fusion(bf16[1024,1664]{1,0:T(8,128)(2,1)} %get-tuple-element.157, bf16[1024,1664]{1,0:T(8,128)(2,1)} %constant_dynamic-update-slice_fusion), kind=kOutput, calls=%fused_computation.1 | convolution fusion | flops 3490709504 | bytes 8912896 | tf_op jit(solution)/shard_map/dot_general | solution.py:392
  324.4 6.6 %convolution_convert_fusion = bf16[1024,1664]{1,0:T(8,128)(2,1)S(1)} fusion(bf16[1024,1024]{1,0:T(8,128)(2,1)} %all-gather.3.cloned.1.call-done.normed_ref, bf16[1024,1664]{1,0:T(8,128)(2,1)} %get-tuple-element.157), kind=kOutput, calls=%fused_computation | convolution fusion | flops 3491364864 | bytes 8912896 | tf_op jit(solution)/shard_map/dot_general | solution.py:396
  335.9 6.6 %shard_map.260 = (bf16[2112,512]{1,0:T(8,128)(2,1)}, bf16[2112,512]{1,0:T(8,128)(2,1)}) custom-call(bf16[704,256]{1,0:T(8,128)(2,1)} %get-tuple-element.137.gate_o, bf16[704,256]{1,0:T(8,128)(2,1)} %get-tuple-element.138.up_o, bf16[704,256]{1,0:T(8,128)(2,1)} %get-tuple-element.139.hid_o, bf16[704,256]{1,0:T(8,128)(2,1)} %get-tuple-element.140.gate_m, ...), custom_call_target="tpu_custom_call" | custom-call | tf_op jit(solution)/shard_map/pallas_call | solution.py:566
  343.0 3.2 convolution_convert_fusion.3
  347.4 3.0 shard_map.263
  362.3 8.0 %collective-permute-done.55 = bf16[128,1664]{1,0:T(8,128)(2,1)S(1)} collective-permute-done((bf16[128,1664]{1,0:T(8,128)(2,1)S(1)}, bf16[128,1664]{1,0:T(8,128)(2,1)S(1)}, u32[]{:S(2)}, u32[]{:S(2)}) %collective-permute-start.55) | collective-permute-done | bytes 426016 | tf_op jit(solution)/shard_map/ppermute | solution.py:576
  371.8 7.0 %collective-permute-done.54 = bf16[128,1664]{1,0:T(8,128)(2,1)S(1)} collective-permute-done((bf16[128,1664]{1,0:T(8,128)(2,1)S(1)}, bf16[128,1664]{1,0:T(8,128)(2,1)S(1)}, u32[]{:S(2)}, u32[]{:S(2)}) %collective-permute-start.54) | collective-permute-done | bytes 426016 | tf_op jit(solution)/shard_map/ppermute | solution.py:576
  385.4 5.7 %collective-permute-done.38 = bf16[2112,128]{1,0:T(8,128)(2,1)S(1)} collective-permute-done((bf16[2112,128]{1,0:T(8,128)(2,1)S(1)}, bf16[2112,128]{1,0:T(8,128)(2,1)S(1)}, u32[]{:S(2)}, u32[]{:S(2)}) %collective-permute-start.38) | collective-permute-done | bytes 540704 | tf_op jit(solution)/shard_map/ppermute | solution.py:576
  392.5 10.2 %collective-permute-done.40 = bf16[2112,128]{1,0:T(8,128)(2,1)S(1)} collective-permute-done((bf16[2112,128]{1,0:T(8,128)(2,1)S(1)}, bf16[2112,128]{1,0:T(8,128)(2,1)S(1)}, u32[]{:S(2)}, u32[]{:S(2)}) %collective-permute-start.40) | collective-permute-done | bytes 540704 | tf_op jit(solution)/shard_map/ppermute | solution.py:576
  402.7 12.8 %collective-permute-done.41 = bf16[2112,128]{1,0:T(8,128)(2,1)S(1)} collective-permute-done((bf16[2112,128]{1,0:T(8,128)(2,1)S(1)}, bf16[2112,128]{1,0:T(8,128)(2,1)S(1)}, u32[]{:S(2)}, u32[]{:S(2)}) %collective-permute-start.41) | collective-permute-done | bytes 540704 | tf_op jit(solution)/shard_map/ppermute | solution.py:576
  429.9 3.8 collective-permute-done.50
  434.3 4.2 collective-permute-done.51
  442.3 3.0 shard_map.262
  (252 shorter events, 105.3 us)
Async XLA Ops:
  7.3 53.2 %all-gather.3.cloned.1.call-start = ((), (), s32[]{:S(2)}) async-start(), calls=%async_computation.2 | async-start | bytes 2621440 | tf_op jit(solution)/shard_map/all_gather | solution.py:696
  10.2 175.3 %reduce-scatter.3.cloned.1.call-start = ((), (), s32[]{:S(2)}) async-start(), calls=%async_computation.3 | async-start | bytes 2621440 | tf_op jit(solution)/shard_map/reduce_scatter | solution.py:706
  12.1 39.1 %collective-permute-start = (bf16[128,1664]{1,0:T(8,128)(2,1)S(1)}, bf16[128,1664]{1,0:T(8,128)(2,1)S(1)}, u32[]{:S(2)}, u32[]{:S(2)}) collective-permute-start(bf16[128,1664]{1,0:T(8,128)(2,1)S(1)} %fusion.1), channel_id=1, source_target_pairs={{0,4},{4,0},{8,12},{12,8},{16,20},{20,16},{24,28},{28,24},{1,5},{5... | collective-permute-start | bytes 1277960 | tf_op jit(solution)/shard_map/ppermute | solution.py:576
  12.7 22.7 %collective-permute-start.1 = (bf16[128,1664]{1,0:T(8,128)(2,1)S(1)}, bf16[128,1664]{1,0:T(8,128)(2,1)S(1)}, u32[]{:S(2)}, u32[]{:S(2)}) collective-permute-start(bf16[128,1664]{1,0:T(8,128)(2,1)S(1)} %fusion.1), channel_id=1, source_target_pairs={{0,8},{4,12},{8,0},{12,4},{16,24},{20,28},{24,16},{28,20},{1,9},{5... | collective-permute-start | bytes 1277960 | tf_op jit(solution)/shard_map/ppermute | solution.py:576
  28.8 21.9 %collective-permute-start.3 = (bf16[128,1664]{1,0:T(8,128)(2,1)S(1)}, bf16[128,1664]{1,0:T(8,128)(2,1)S(1)}, u32[]{:S(2)}, u32[]{:S(2)}) collective-permute-start(bf16[128,1664]{1,0:T(8,128)(2,1)S(1)} %fusion.1), channel_id=1, source_target_pairs={{0,16},{4,20},{8,24},{12,28},{16,0},{20,4},{24,8},{28,12},{1,17},{... | collective-permute-start | bytes 1277960 | tf_op jit(solution)/shard_map/ppermute | solution.py:576
  32.5 18.4 %collective-permute-start.5 = (bf16[128,1664]{1,0:T(8,128)(2,1)S(1)}, bf16[128,1664]{1,0:T(8,128)(2,1)S(1)}, u32[]{:S(2)}, u32[]{:S(2)}) collective-permute-start(bf16[128,1664]{1,0:T(8,128)(2,1)S(1)} %fusion.1), channel_id=1, source_target_pairs={{0,24},{4,28},{8,16},{12,20},{16,8},{20,12},{24,0},{28,4},{1,25},{... | collective-permute-start | bytes 1277960 | tf_op jit(solution)/shard_map/ppermute | solution.py:576
  56.9 74.6 %collective-permute-start.14 = (bf16[2112,128]{1,0:T(8,128)(2,1)S(1)}, bf16[2112,128]{1,0:T(8,128)(2,1)S(1)}, u32[]{:S(2)}, u32[]{:S(2)}) collective-permute-start(bf16[2112,128]{1,0:T(8,128)(2,1)S(1)} %pad_maximum_fusion.1), channel_id=1, source_target_pairs={{0,8},{4,12},{8,0},{12,4},{16,24},{20,28},{24,16},{28,20},{1,9},{5... | collective-permute-start | bytes 1622024 | tf_op jit(solution)/shard_map/ppermute | solution.py:576
  58.5 73.1 %collective-permute-start.15 = (bf16[2112,128]{1,0:T(8,128)(2,1)S(1)}, bf16[2112,128]{1,0:T(8,128)(2,1)S(1)}, u32[]{:S(2)}, u32[]{:S(2)}) collective-permute-start(bf16[2112,128]{1,0:T(8,128)(2,1)S(1)} %pad_maximum_fusion.1), channel_id=1, source_target_pairs={{0,16},{4,20},{8,24},{12,28},{16,0},{20,4},{24,8},{28,12},{1,17},{... | collective-permute-start | bytes 1622024 | tf_op jit(solution)/shard_map/ppermute | solution.py:576
  60.0 71.6 %collective-permute-start.16 = (bf16[2112,128]{1,0:T(8,128)(2,1)S(1)}, bf16[2112,128]{1,0:T(8,128)(2,1)S(1)}, u32[]{:S(2)}, u32[]{:S(2)}) collective-permute-start(bf16[2112,128]{1,0:T(8,128)(2,1)S(1)} %pad_maximum_fusion.1), channel_id=1, source_target_pairs={{0,24},{4,28},{8,16},{12,20},{16,8},{20,12},{24,0},{28,4},{1,25},{... | collective-permute-start | bytes 1622024 | tf_op jit(solution)/shard_map/ppermute | solution.py:576
  60.4 72.4 %collective-permute-start.21 = (bf16[2112,128]{1,0:T(8,128)(2,1)S(1)}, bf16[2112,128]{1,0:T(8,128)(2,1)S(1)}, u32[]{:S(2)}, u32[]{:S(2)}) collective-permute-start(bf16[2112,128]{1,0:T(8,128)(2,1)S(1)} %pad_maximum_fusion.1), channel_id=1, source_target_pairs={{0,2},{1,3},{2,0},{3,1},{4,6},{5,7},{6,4},{7,5},{8,10},{9,11},{10,... | collective-permute-start | bytes 1622024 | tf_op jit(solution)/shard_map/ppermute | solution.py:576
  131.3 148.7 %all-gather.5.cloned.1.call-start = ((), (), s32[]{:S(2)}) async-start(), calls=%async_computation.4 | async-start | bytes 2621440 | tf_op jit(solution)/shard_map/all_gather | solution.py:725
  132.8 29.4 %collective-permute-start.22 = (bf16[2112,128]{1,0:T(8,128)(2,1)S(1)}, bf16[2112,128]{1,0:T(8,128)(2,1)S(1)}, u32[]{:S(2)}, u32[]{:S(2)}) collective-permute-start(bf16[2112,128]{1,0:T(8,128)(2,1)S(1)} %collective-permute-done.21), channel_id=1, source_target_pairs={{0,4},{4,0},{8,12},{12,8},{16,20},{20,16},{24,28},{28,24},{1,5},{5... | collective-permute-start | bytes 1622024 | tf_op jit(solution)/shard_map/ppermute | solution.py:576
  135.7 26.0 %collective-permute-start.25 = (bf16[2112,128]{1,0:T(8,128)(2,1)S(1)}, bf16[2112,128]{1,0:T(8,128)(2,1)S(1)}, u32[]{:S(2)}, u32[]{:S(2)}) collective-permute-start(bf16[2112,128]{1,0:T(8,128)(2,1)S(1)} %collective-permute-done.21), channel_id=1, source_target_pairs={{0,16},{4,20},{8,24},{12,28},{16,0},{20,4},{24,8},{28,12},{1,17},{... | collective-permute-start | bytes 1622024 | tf_op jit(solution)/shard_map/ppermute | solution.py:576
  137.7 24.0 %collective-permute-start.27 = (bf16[2112,128]{1,0:T(8,128)(2,1)S(1)}, bf16[2112,128]{1,0:T(8,128)(2,1)S(1)}, u32[]{:S(2)}, u32[]{:S(2)}) collective-permute-start(bf16[2112,128]{1,0:T(8,128)(2,1)S(1)} %collective-permute-done.21), channel_id=1, source_target_pairs={{0,24},{4,28},{8,16},{12,20},{16,8},{20,12},{24,0},{28,4},{1,25},{... | collective-permute-start | bytes 1622024 | tf_op jit(solution)/shard_map/ppermute | solution.py:576
  138.7 37.5 %collective-permute-start.29 = (bf16[256,1024]{1,0:T(8,128)(2,1)S(1)}, bf16[256,1024]{1,0:T(8,128)(2,1)S(1)}, u32[]{:S(2)}, u32[]{:S(2)}) collective-permute-start(bf16[256,1024]{1,0:T(8,128)(2,1)S(1)} %copy-done.3), channel_id=1, source_target_pairs={{0,1},{1,0},{2,3},{3,2},{4,5},{5,4},{6,7},{7,6},{8,9},{9,8},{10,11... | collective-permute-start | bytes 1572872 | tf_op jit(solution)/shard_map/ppermute | solution.py:576
  233.5 208.8 %reduce-scatter.5.cloned.1.call-start = ((), (), s32[]{:S(2)}) async-start(), calls=%async_computation.5 | async-start | bytes 2621440 | tf_op jit(solution)/shard_map/reduce_scatter | solution.py:737
  247.7 85.6 %collective-permute-start.37 = (bf16[2112,128]{1,0:T(8,128)(2,1)}, bf16[2112,128]{1,0:T(8,128)(2,1)S(1)}, u32[]{:S(2)}, u32[]{:S(2)}) collective-permute-start(bf16[2112,128]{1,0:T(8,128)(2,1)} %get-tuple-element.204), channel_id=1, source_target_pairs={{0,24},{4,28},{8,16},{12,20},{16,8},{20,12},{24,0},{28,4},{1,25},{... | collective-permute-start | bytes 1622024 | tf_op jit(solution)/shard_map/ppermute | solution.py:576
  250.0 83.3 %collective-permute-start.36 = (bf16[2112,128]{1,0:T(8,128)(2,1)}, bf16[2112,128]{1,0:T(8,128)(2,1)}, u32[]{:S(2)}, u32[]{:S(2)}) collective-permute-start(bf16[2112,128]{1,0:T(8,128)(2,1)} %get-tuple-element.205), channel_id=1, source_target_pairs={{0,16},{4,20},{8,24},{12,28},{16,0},{20,4},{24,8},{28,12},{1,17},{... | collective-permute-start | bytes 1622024 | tf_op jit(solution)/shard_map/ppermute | solution.py:576
  250.6 82.7 %collective-permute-start.35 = (bf16[2112,128]{1,0:T(8,128)(2,1)S(1)}, bf16[2112,128]{1,0:T(8,128)(2,1)}, u32[]{:S(2)}, u32[]{:S(2)}) collective-permute-start(bf16[2112,128]{1,0:T(8,128)(2,1)S(1)} %get-tuple-element.203), channel_id=1, source_target_pairs={{0,8},{4,12},{8,0},{12,4},{16,24},{20,28},{24,16},{28,20},{1,9},{5... | collective-permute-start | bytes 1622024 | tf_op jit(solution)/shard_map/ppermute | solution.py:576
  333.3 21.3 %collective-permute-start.42 = (bf16[512,1664]{1,0:T(8,128)(2,1)}, bf16[512,1664]{1,0:T(8,128)(2,1)}, u32[]{:S(2)}, u32[]{:S(2)}) collective-permute-start(bf16[512,1664]{1,0:T(8,128)(2,1)} %pad_maximum_fusion), channel_id=1, source_target_pairs={{0,4},{4,0},{8,12},{12,8},{16,20},{20,16},{24,28},{28,24},{1,5},{5... | collective-permute-start | bytes 5111816 | tf_op jit(solution)/shard_map/ppermute | solution.py:576
  347.2 37.4 %collective-permute-start.32 = (bf16[256,1024]{1,0:T(8,128)(2,1)}, bf16[256,1024]{1,0:T(8,128)(2,1)}, u32[]{:S(2)}, u32[]{:S(2)}) collective-permute-start(bf16[256,1024]{1,0:T(8,128)(2,1)} %get-tuple-element.122), channel_id=1, source_target_pairs={{0,1},{1,0},{2,3},{3,2},{4,5},{5,4},{6,7},{7,6},{8,9},{9,8},{10,11... | collective-permute-start | bytes 1572872 | tf_op jit(solution)/shard_map/ppermute | solution.py:576
  359.1 19.8 %collective-permute-start.54 = (bf16[128,1664]{1,0:T(8,128)(2,1)S(1)}, bf16[128,1664]{1,0:T(8,128)(2,1)S(1)}, u32[]{:S(2)}, u32[]{:S(2)}) collective-permute-start(bf16[128,1664]{1,0:T(8,128)(2,1)S(1)} %get-tuple-element.198), channel_id=1, source_target_pairs={{0,16},{4,20},{8,24},{12,28},{16,0},{20,4},{24,8},{28,12},{1,17},{... | collective-permute-start | bytes 1277960 | tf_op jit(solution)/shard_map/ppermute | solution.py:576
  359.6 21.6 %collective-permute-start.53 = (bf16[128,1664]{1,0:T(8,128)(2,1)S(1)}, bf16[128,1664]{1,0:T(8,128)(2,1)S(1)}, u32[]{:S(2)}, u32[]{:S(2)}) collective-permute-start(bf16[128,1664]{1,0:T(8,128)(2,1)S(1)} %get-tuple-element.196), channel_id=1, source_target_pairs={{0,8},{4,12},{8,0},{12,4},{16,24},{20,28},{24,16},{28,20},{1,9},{5... | collective-permute-start | bytes 1277960 | tf_op jit(solution)/shard_map/ppermute | solution.py:576
  360.8 30.3 %collective-permute-start.38 = (bf16[2112,128]{1,0:T(8,128)(2,1)S(1)}, bf16[2112,128]{1,0:T(8,128)(2,1)S(1)}, u32[]{:S(2)}, u32[]{:S(2)}) collective-permute-start(bf16[2112,128]{1,0:T(8,128)(2,1)S(1)} %get-tuple-element.146), channel_id=1, source_target_pairs={{0,8},{4,12},{8,0},{12,4},{16,24},{20,28},{24,16},{28,20},{1,9},{5... | collective-permute-start | bytes 1622024 | tf_op jit(solution)/shard_map/ppermute | solution.py:576
  370.3 20.7 %collective-permute-start.39 = (bf16[2112,128]{1,0:T(8,128)(2,1)S(1)}, bf16[2112,128]{1,0:T(8,128)(2,1)S(1)}, u32[]{:S(2)}, u32[]{:S(2)}) collective-permute-start(bf16[2112,128]{1,0:T(8,128)(2,1)S(1)} %get-tuple-element.147), channel_id=1, source_target_pairs={{0,16},{4,20},{8,24},{12,28},{16,0},{20,4},{24,8},{28,12},{1,17},{... | collective-permute-start | bytes 1622024 | tf_op jit(solution)/shard_map/ppermute | solution.py:576
  378.9 23.9 %collective-permute-start.40 = (bf16[2112,128]{1,0:T(8,128)(2,1)S(1)}, bf16[2112,128]{1,0:T(8,128)(2,1)S(1)}, u32[]{:S(2)}, u32[]{:S(2)}) collective-permute-start(bf16[2112,128]{1,0:T(8,128)(2,1)S(1)} %get-tuple-element.148), channel_id=1, source_target_pairs={{0,24},{4,28},{8,16},{12,20},{16,8},{20,12},{24,0},{28,4},{1,25},{... | collective-permute-start | bytes 1622024 | tf_op jit(solution)/shard_map/ppermute | solution.py:576
  381.5 34.0 %collective-permute-start.41 = (bf16[2112,128]{1,0:T(8,128)(2,1)S(1)}, bf16[2112,128]{1,0:T(8,128)(2,1)S(1)}, u32[]{:S(2)}, u32[]{:S(2)}) collective-permute-start(bf16[2112,128]{1,0:T(8,128)(2,1)S(1)} %copy-done.8), channel_id=1, source_target_pairs={{0,2},{1,3},{2,0},{3,1},{4,6},{5,7},{6,4},{7,5},{8,10},{9,11},{10,... | collective-permute-start | bytes 1622024 | tf_op jit(solution)/shard_map/ppermute | solution.py:576
  384.6 32.8 %collective-permute-start.48 = (f32[7,1024]{1,0:T(8,128)}, f32[7,1024]{1,0:T(8,128)S(1)}, u32[]{:S(2)}, u32[]{:S(2)}) collective-permute-start(f32[7,1024]{1,0:T(8,128)} %pad_maximum_fusion.3), channel_id=1, source_target_pairs={{0,24},{4,28},{8,16},{12,20},{16,8},{20,12},{24,0},{28,4},{1,25},{... | collective-permute-start | bytes 86024 | tf_op jit(solution)/shard_map/ppermute | solution.py:576
  391.1 26.4 %collective-permute-start.49 = (f32[7,1024]{1,0:T(8,128)}, f32[7,1024]{1,0:T(8,128)S(1)}, u32[]{:S(2)}, u32[]{:S(2)}) collective-permute-start(f32[7,1024]{1,0:T(8,128)} %pad_maximum_fusion.3), channel_id=1, source_target_pairs={{0,28},{4,24},{8,20},{12,16},{16,12},{20,8},{24,4},{28,0},{1,29},{... | collective-permute-start | bytes 86024 | tf_op jit(solution)/shard_map/ppermute | solution.py:576
  391.1 32.2 %collective-permute-start.46 = (f32[7,1024]{1,0:T(8,128)}, f32[7,1024]{1,0:T(8,128)S(1)}, u32[]{:S(2)}, u32[]{:S(2)}) collective-permute-start(f32[7,1024]{1,0:T(8,128)} %pad_maximum_fusion.3), channel_id=1, source_target_pairs={{0,16},{4,20},{8,24},{12,28},{16,0},{20,4},{24,8},{28,12},{1,17},{... | collective-permute-start | bytes 86024 | tf_op jit(solution)/shard_map/ppermute | solution.py:576
  402.7 22.9 %collective-permute-start.47 = (f32[7,1024]{1,0:T(8,128)}, f32[7,1024]{1,0:T(8,128)S(1)}, u32[]{:S(2)}, u32[]{:S(2)}) collective-permute-start(f32[7,1024]{1,0:T(8,128)} %pad_maximum_fusion.3), channel_id=1, source_target_pairs={{0,20},{4,16},{8,28},{12,24},{16,4},{20,0},{24,12},{28,8},{1,21},{... | collective-permute-start | bytes 86024 | tf_op jit(solution)/shard_map/ppermute | solution.py:576
  423.3 18.2 %collective-permute-start.59 = (bf16[512,128]{1,0:T(8,128)(2,1)S(1)}, bf16[512,128]{1,0:T(8,128)(2,1)S(1)}, u32[]{:S(2)}, u32[]{:S(2)}) collective-permute-start(bf16[512,128]{1,0:T(8,128)(2,1)S(1)} %copy-done.14), channel_id=1, source_target_pairs={{0,24},{4,28},{8,16},{12,20},{16,8},{20,12},{24,0},{28,4},{1,25},{... | collective-permute-start | bytes 393224 | tf_op jit(solution)/shard_map/ppermute | solution.py:576
  (54 other events, 527.4 us)
Sparse Core Ops, SparseCore 0:
  10.4 48.3 all-gather.2
  131.4 54.0 reduce-scatter.2
  233.7 46.3 all-gather.4
  347.3 58.0 reduce-scatter.4

commit v4 on v3

--- a/solution.py
+++ b/solution.py
@@ -1,4 +1,5 @@
 import functools
+import math
 import jax
 import jax.numpy as jnp
 from jax import lax
@@ -12,6 +13,7 @@
 CONVW = 2 * DK + DV
 HEADW = 2 * DK + 2 * DV
 CHUNK = 128
+SUBS = 2
 EPSILON = 1e-06
 F32 = jnp.float32
 BF16 = jnp.bfloat16
@@ -28,8 +30,13 @@
 def dot3(left, right, dims=NN):
     lh, ll = left if isinstance(left, tuple) else split(left)
     rh, rl = right if isinstance(right, tuple) else split(right)
-    d = functools.partial(lax.dot_general, dimension_numbers=dims, preferred_element_type=F32)
-    return d(lh, rh) + (d(lh, rl) + d(ll, rh))
+    (l_axis,), (r_axis,) = dims[0]
+    return lax.dot_general(
+        jnp.concatenate([lh, lh, ll], axis=l_axis),
+        jnp.concatenate([rh, rl, rh], axis=r_axis),
+        dims,
+        preferred_element_type=F32,
+    )
 
 
 def sigmoid(x):
@@ -86,18 +93,25 @@
     return fade, strict, reach, trail, keep
 
 
-def unit_lower_inverse(lower):
-    square = lower.shape
+def unit_lower_inverses(lowers):
+    square = lowers[0].shape
     row, col = place(square, 0), place(square, 1)
     apart = row ^ col
-    inverse = jnp.where(row == col, 1.0, jnp.where(apart == 1, -lower, 0.0))
+    inverses = [
+        jnp.where(row == col, 1.0, jnp.where(apart == 1, -lower, 0.0)) for lower in lowers
+    ]
     level = 1
     while (1 << level) < square[0]:
-        part = jnp.where((apart >> level) == 1, lower, 0.0)
-        pair = split(inverse)
-        inverse = inverse - dot3(pair, dot3(part, pair))
+        across = (apart >> level) == 1
+        pairs = [split(inverse) for inverse in inverses]
+        inner = [
+            dot3(jnp.where(across, lower, 0.0), pair) for lower, pair in zip(lowers, pairs)
+        ]
+        inverses = [
+            inverse - dot3(pair, part) for inverse, pair, part in zip(inverses, pairs, inner)
+        ]
         level += 1
-    return inverse
+    return inverses
 
 
 def activations(proj_ref, before_ref, conv_ref, docs, doc_before, head):
@@ -120,63 +134,85 @@
 def doc_context(doc_ref, doc_before_ref, chunk):
     docs = doc_ref[...]
     doc_before = jnp.where(chunk > 0, doc_before_ref[...], -1.0)
-    return docs, jnp.transpose(docs), doc_before, doc_before[-1:, :]
+    doc_row = jnp.transpose(docs) if docs.shape[0] == CHUNK else None
+    return docs, doc_row, doc_before, doc_before[-1:, :]
 
 
 def forward_kernel(
-    heads, proj_ref, before_ref, doc_ref, doc_before_ref, conv_ref, vec_ref, gain_ref,
-    gated_ref, recur_ref, inverse_ref, solved_ref, mix_ref, key_ref, tilde_ref, start_ref, state,
+    heads, seq_ref, weight_ref, doc_ref, doc_before_ref, conv_ref, vec_ref, gain_ref,
+    proj_ref, gated_ref, recur_ref, inverse_ref, solved_ref, mix_ref, key_ref, tilde_ref, start_ref, state, before_ref,
 ):
-    chunk = pl.program_id(0)
-
-    @pl.when(chunk == 0)
+    step = pl.program_id(0)
+
+    @pl.when(step == 0)
     def _():
         state[...] = jnp.zeros_like(state)
-
-    docs, doc_row, doc_before, doc_carried = doc_context(doc_ref, doc_before_ref, chunk)
+        before_ref[...] = jnp.zeros_like(before_ref)
+
+    proj_ref[...] = lax.dot_general(
+        seq_ref[...], weight_ref[...], NN, preferred_element_type=F32
+    )
+    docs_all, _, doc_before, doc_carried = doc_context(doc_ref, doc_before_ref, step)
     pair = proj_ref[:, heads * HEADW :]
     decay = -vec_ref[0:1, :] * softplus(pair + vec_ref[1:2, :])
     write = sigmoid(pair)
-    cum = cumulate(decay)
-    eye = place(docs.shape, 0) == place(docs.shape, 1)
-    for head in range(heads):
-        acts = activations(proj_ref, before_ref, conv_ref, docs, doc_before, head)
-        query, key, value = acts[8:]
-        fade, strict, reach, trail, keep = head_decay(cum, 2 * head, docs, doc_row, doc_carried)
-        beta = write[:, 2 * head + 1 : 2 * head + 2]
-        key_pair = split(key)
-        both = dot3(jnp.concatenate([key, query], axis=0), key_pair, NT)
-        key_key = both[:CHUNK] * strict
-        mix = both[CHUNK:] * fade
-        inverse = unit_lower_inverse(beta * key_key)
+    acts = [
+        activations(proj_ref, before_ref, conv_ref, docs_all, doc_before, head)[8:]
+        for head in range(heads)
+    ]
+    units = []
+    for sub in range(docs_all.shape[0] // CHUNK):
+        rows = slice(sub * CHUNK, (sub + 1) * CHUNK)
+        docs = docs_all[rows]
+        doc_row = jnp.transpose(docs)
+        carried = doc_carried if sub == 0 else docs_all[sub * CHUNK - 1 : sub * CHUNK]
+        cum = cumulate(decay[rows])
+        for head in range(heads):
+            query, key, value = [part[rows] for part in acts[head]]
+            decays = head_decay(cum, 2 * head, docs, doc_row, carried)
+            beta = write[rows, 2 * head + 1 : 2 * head + 2]
+            units.append((sub, head, rows, query, key, value, beta, decays))
+    lowers, mixes = [], []
+    for sub, head, rows, query, key, value, beta, decays in units:
+        both = dot3(jnp.concatenate([key, query], axis=0), split(key), NT)
+        key_key = both[:CHUNK] * decays[1]
+        key_ref[sub, head] = key_key
+        lowers.append(beta * key_key)
+        mixes.append(both[CHUNK:] * decays[0])
+    inverses = unit_lower_inverses(lowers)
+    eye = place((CHUNK, CHUNK), 0) == place((CHUNK, CHUNK), 1)
+    ready = []
+    for unit, inverse, mix in zip(units, inverses, mixes):
+        sub, head, rows, query, key, value, beta, (fade, strict, reach, trail, keep) = unit
         rhs = jnp.concatenate([beta * reach * key, beta * value], axis=1)
         solved = dot3(inverse, rhs)
         trailing = jnp.transpose(trail * key)
         outer = dot3(jnp.concatenate([trailing, mix], axis=0), solved)
-        step = jnp.where(eye, keep, 0.0) - outer[:CHUNK, :DK]
-        q_tilde = reach * query - outer[CHUNK:, :DK]
-        tilde = jnp.concatenate([step, q_tilde], axis=0)
+        step_matrix = jnp.where(eye, keep, 0.0) - outer[:CHUNK, :DK]
+        tilde = jnp.concatenate([step_matrix, reach * query - outer[CHUNK:, :DK]], axis=0)
+        inverse_ref[sub, head] = inverse
+        solved_ref[sub, head] = solved
+        mix_ref[sub, head] = mix
+        tilde_ref[sub, head] = tilde
+        ready.append((sub, head, rows, tilde, outer))
+    for sub, head, rows, tilde, outer in ready:
         start = state[head]
+        start_ref[sub, head] = start
         moved = dot3(tilde, start)
         state[head] = moved[:CHUNK] + outer[:CHUNK, DK:]
         recurrent = moved[CHUNK:] + outer[CHUNK:, DK:]
-        inverse_ref[0, head] = inverse
-        solved_ref[0, head] = solved
-        mix_ref[0, head] = mix
-        key_ref[0, head] = key_key
-        tilde_ref[0, head] = tilde
-        start_ref[0, head] = start
-        recur_ref[:, head * DV : (head + 1) * DV] = recurrent
+        recur_ref[rows, head * DV : (head + 1) * DV] = recurrent
         scale = lax.rsqrt(jnp.mean(recurrent * recurrent, axis=-1, keepdims=True) + EPSILON)
-        z = proj_ref[:, head * HEADW + CONVW : (head + 1) * HEADW]
+        z = proj_ref[rows, head * HEADW + CONVW : (head + 1) * HEADW]
         gated = recurrent * scale * gain_ref[...] * (z * sigmoid(z))
-        gated_ref[:, head * DV : (head + 1) * DV] = gated.astype(BF16)
+        gated_ref[rows, head * DV : (head + 1) * DV] = gated.astype(BF16)
+    before_ref[...] = proj_ref[proj_ref.shape[0] - 8 :, :]
 
 
 def backward_kernel(
     heads, chunks, proj_ref, before_ref, doc_ref, doc_before_ref, doc_after_ref,
     conv_ref, vec_ref, gain_ref, recur_ref, inverse_ref, solved_ref, mix_ref, key_ref, tilde_ref,
-    start_ref, grad_ref,
+    start_ref, back_ref, out_weight_ref,
     d_proj_ref, d_conv_ref, d_vec_ref, d_gain_ref, d_state, d_after,
 ):
     step_index = pl.program_id(0)
@@ -201,12 +237,15 @@
     last_row = place(docs.shape, 0) == CHUNK - 1
     d_cum = jnp.zeros_like(docs)
     d_write = jnp.zeros_like(docs)
+    grad_all = lax.dot_general(
+        back_ref[...], out_weight_ref[...], NT, preferred_element_type=F32
+    )
     for head in range(heads):
         acts = activations(proj_ref, before_ref, conv_ref, docs, doc_before, head)
         parts, taps, pre, gate, q_raw, k_raw, q_scale, k_scale, query, key, value = acts
         fade, strict, reach, trail, keep = head_decay(cum, 2 * head, docs, doc_row, doc_carried)
         beta = write[:, 2 * head + 1 : 2 * head + 2]
-        grad = grad_ref[:, head * DV : (head + 1) * DV].astype(F32)
+        grad = grad_all[:, head * DV : (head + 1) * DV]
         recurrent = recur_ref[:, head * DV : (head + 1) * DV]
         scale = lax.rsqrt(jnp.mean(recurrent * recurrent, axis=-1, keepdims=True) + EPSILON)
         z = proj_ref[:, head * HEADW + CONVW : (head + 1) * HEADW]
@@ -305,11 +344,12 @@
     d_vec_ref[1:2, :] += jnp.sum(d_shifted, axis=0, keepdims=True)
 
 
-def chunk_specs(heads, chunks, where):
-    per8 = CHUNK // 8
+def chunk_specs(heads, chunks, where, subs=1):
+    size = subs * CHUNK
+    per8 = size // 8
 
     def rows(width):
-        return pl.BlockSpec((CHUNK, width), lambda c: (where(c), 0))
+        return pl.BlockSpec((size, width), lambda c: (where(c), 0))
 
     def before(width):
         return pl.BlockSpec((8, width), lambda c: (jnp.maximum(where(c) * per8 - 1, 0), 0))
@@ -323,7 +363,7 @@
         return pl.BlockSpec(shape, lambda c: (0,) * len(shape))
 
     def saved(height, width):
-        return pl.BlockSpec((1, heads, height, width), lambda c: (where(c), 0, 0, 0))
+        return pl.BlockSpec((subs, heads, height, width), lambda c: (where(c), 0, 0, 0))
 
     return rows, before, after, whole, saved
 
@@ -333,33 +373,39 @@
     return sizes
 
 
-def mixer_forward(projected, docs, taps, vectors, gain, interpret=False):
-    length, width = projected.shape
+def mixer_forward(seq_rows, weight, docs, taps, vectors, gain, interpret=False):
+    length, features = seq_rows.shape
+    width = weight.shape[1]
     heads = (width - CHUNK) // HEADW
     chunks = length // CHUNK
-    rows, before, _, whole, saved = chunk_specs(heads, chunks, lambda c: c)
+    subs = math.gcd(chunks, SUBS)
+    rows, before, _, whole, saved = chunk_specs(heads, chunks, lambda c: c, subs)
     sizes = saved_shapes()
     return pl.pallas_call(
         functools.partial(forward_kernel, heads),
-        grid=(chunks,),
+        grid=(chunks // subs,),
         in_specs=[
-            rows(width), before(width), rows(CHUNK), before(CHUNK),
+            rows(features), whole((features, width)), rows(CHUNK), before(CHUNK),
             whole((4, heads * CONVW)), whole((8, CHUNK)), whole((1, DV)),
         ],
-        out_specs=[rows(heads * DV), rows(heads * DV)] + [saved(*s) for s in sizes],
+        out_specs=[rows(width), rows(heads * DV), rows(heads * DV)] + [saved(*s) for s in sizes],
         out_shape=[
+            jax.ShapeDtypeStruct((length, width), F32),
             jax.ShapeDtypeStruct((length, heads * DV), BF16),
             jax.ShapeDtypeStruct((length, heads * DV), F32),
         ]
         + [jax.ShapeDtypeStruct((chunks, heads) + s, F32) for s in sizes],
-        scratch_shapes=[pltpu.VMEM((heads, DK, DV), F32)],
+        scratch_shapes=[pltpu.VMEM((heads, DK, DV), F32), pltpu.VMEM((8, width), F32)],
         name="mixer_forward",
         interpret=interpret,
-    )(projected, projected, docs, docs, taps, vectors, gain)
-
-
-def mixer_backward(projected, docs, taps, vectors, gain, kept, grad, interpret=False):
+    )(seq_rows, weight, docs, docs, taps, vectors, gain)
+
+
+def mixer_backward(
+    projected, docs, taps, vectors, gain, kept, back_seq, out_weight, interpret=False
+):
     length, width = projected.shape
+    features = back_seq.shape[1]
     heads = (width - CHUNK) // HEADW
     chunks = length // CHUNK
     rows, before, after, whole, saved = chunk_specs(heads, chunks, lambda c: chunks - 1 - c)
@@ -372,7 +418,7 @@
             whole((4, heads * CONVW)), whole((8, CHUNK)), whole((1, DV)), rows(heads * DV),
         ]
         + [saved(*s) for s in sizes]
-        + [rows(heads * DV)],
+        + [rows(features), whole((heads * DV, features))],
         out_specs=[
             rows(width), whole((4, heads * CONVW)), whole((8, CHUNK)), whole((1, DV)),
         ],
@@ -385,7 +431,7 @@
         scratch_shapes=[pltpu.VMEM((heads, DK, DV), F32), pltpu.VMEM((8, heads * CONVW), F32)],
         name="mixer_backward",
         interpret=interpret,
-    )(projected, projected, docs, docs, docs, taps, vectors, gain, *kept, grad)
+    )(projected, projected, docs, docs, docs, taps, vectors, gain, *kept, back_seq, out_weight)
 
 
 def times_transposed(left, right):
@@ -471,23 +517,15 @@
         out_ref[:, block_source(me_ref, p, CHUNK)] = total[:, p * CHUNK : (p + 1) * CHUNK]
 
 
-UNIT_STEPS = 2
-
-
-def feed_kernel(
-    tok_ref, cot_ref, *refs,
-):
-    weights, outs = (refs[:3], refs[3:6]), (refs[6:9], refs[9:12])
-    d_out, y_out, d_total, y_total = refs[12:]
-    step = pl.program_id(0)
-
-    @pl.when(step == 0)
-    def _():
-        d_total[...] = jnp.zeros_like(d_total)
-        y_total[...] = jnp.zeros_like(y_total)
-
+def feed_kernel(tok_ref, cot_ref, near_ref, far_ref, *refs):
+    outs, (d_out, y_out) = refs[:6], refs[6:8]
+    quarter = near_ref.shape[0] // 3
     tokens, cots = tok_ref[...], cot_ref[...]
-    for (gate_w, up_w, down_w), (gate_out, up_out, hidden_out) in zip(weights, outs):
+    d_total = y_total = 0.0
+    for source, weights in enumerate((near_ref, far_ref)):
+        gate_w, up_w, down_w = [
+            weights.at[pl.ds(index * quarter, quarter)] for index in range(3)
+        ]
         gate_pre = times_transposed(gate_w[...], tokens)
         up_pre = times_transposed(up_w[...], tokens)
         d_hidden = times_transposed(down_w[...], cots)
@@ -496,37 +534,25 @@
         hidden = (silu * up_pre).astype(BF16)
         d_up = (d_hidden * silu).astype(BF16)
         d_gate = (d_hidden * up_pre * (sig * (1.0 + gate_pre * (1.0 - sig)))).astype(BF16)
-        gate_out[...] = d_gate
-        up_out[...] = d_up
-        hidden_out[...] = hidden
-        d_total[...] += transposed_times(d_gate, gate_w[...]) + transposed_times(d_up, up_w[...])
-        y_total[...] += transposed_times(hidden, down_w[...])
-
-    @pl.when(step == UNIT_STEPS - 1)
-    def _():
-        d_out[...] = d_total[...].astype(BF16)
-        y_out[...] = y_total[...].astype(BF16)
+        for ref, value in zip(outs[3 * source : 3 * source + 3], (d_gate, d_up, hidden)):
+            ref[...] = value
+        d_total += transposed_times(d_gate, gate_w[...]) + transposed_times(d_up, up_w[...])
+        y_total += transposed_times(hidden, down_w[...])
+    d_out[...] = d_total.astype(BF16)
+    y_out[...] = y_total.astype(BF16)
 
 
 def feed_call(tokens, cots, near, far):
     count, features = tokens.shape
     quarter = near.shape[0] // 3
-    block = quarter // UNIT_STEPS
-
-    def part(index):
-        return pl.BlockSpec((block, features), lambda i: (UNIT_STEPS * index + i, 0))
-
-    whole = pl.BlockSpec((count, features), lambda i: (0, 0))
-    unit_out = pl.BlockSpec((block, count), lambda i: (i, 0))
+    in_vmem = pl.BlockSpec(memory_space=pltpu.VMEM)
     outs = pl.pallas_call(
         feed_kernel,
-        grid=(UNIT_STEPS,),
-        in_specs=[whole, whole] + [part(index) for index in range(3)] * 2,
-        out_specs=[unit_out] * 6 + [whole, whole],
+        in_specs=[in_vmem] * 4,
+        out_specs=[in_vmem] * 8,
         out_shape=[jax.ShapeDtypeStruct((quarter, count), BF16)] * 6
         + [jax.ShapeDtypeStruct((count, features), BF16)] * 2,
-        scratch_shapes=[pltpu.VMEM((count, features), F32)] * 2,
-    )(tokens, cots, near, near, near, far, far, far)
+    )(tokens, cots, near, far)
     return outs[:3], outs[3:6], outs[6], outs[7]
 
 
@@ -636,8 +662,14 @@
     return sum(piece.astype(F32) for piece in planar_move(half, axis))
 
 
-def tree_sum(value, axis):
-    parts = [value] + [swap(value, axis, mask) for mask in range(1, lax.axis_size(axis))]
+def turned(value, axis):
+    parts = [value]
+    for mask in range(1, lax.axis_size(axis)):
+        parts.append(swap(value, axis, mask))
+    return parts
+
+
+def tree_sum(parts):
     while len(parts) > 1:
         parts = [left + right for left, right in zip(parts[0::2], parts[1::2])]
     return parts[0]
@@ -700,8 +732,7 @@
     near = planar_dp(after(units, (whole_in, whole_out)))
     far_units = swap(after(units, seq_rows), "tensor", 2)
     mate_cot = swap(after(cot, seq_rows), "tensor", 1)
-    projected = times(seq_rows, whole_in)
-    gated, *kept = mixer_forward(projected, docs, conv_mine, vectors, gain_row)
+    projected, gated, *kept = mixer_forward(seq_rows, whole_in, docs, conv_mine, vectors, gain_row)
     mixed_part = times(gated, whole_out).astype(BF16)
     mixed = lax.psum_scatter(mixed_part, "tensor", scatter_dimension=0, tiled=True)
     far = planar_dp(after(far_units, gated))
@@ -716,7 +747,7 @@
     d_from_mate = swap(d_mate, "tensor", 1)
     activations_all = (normed_ffn, mate_normed, cot, mate_cot)
     far_half = unit_grads(after(far_own, d_mate), far_mate, *activations_all)
-    near_half = unit_grads(after(near_own, far_half), near_mate, *activations_all)
+    near_half = unit_grads(after(near_own, far_half[-1]), near_mate, *activations_all)
     d_resid, d_mixed, gain_ffn_part = row_call(
         ffn_back_kernel, [token_f32, token_bf, gain_shape],
         me, resid, cot, d_own, d_from_mate, gain_ffn,
@@ -729,9 +760,8 @@
     from_far = swap(far_grad, "tensor", 2)
     near_moved = planar_move(near_half, 1)
     out_from_mate = swap(out_mate, "tensor", 1)
-    d_gated = times_transposed(mixer_back_seq, whole_out)
     d_projected, d_conv, d_vectors, d_gain_out = mixer_backward(
-        projected, docs, conv_mine, vectors, gain_row, kept, d_gated
+        projected, docs, conv_mine, vectors, gain_row, kept, mixer_back_seq, whole_out
     )
     d_part = times_transposed(d_projected, whole_in).astype(BF16)
     d_normed_in = lax.psum_scatter(d_part, "tensor", scatter_dimension=0, tiled=True)
@@ -740,8 +770,8 @@
     grad_joined = planar_sum(joined_half, 0)
     (gain_in_part,) = row_call(gain_kernel, [gain_shape], me, d_part, seq_later, gain_in)
     out_half = core_half([transposed_times(gated_later, back_later).astype(BF16)])
-    grad_out = planar_sum(after(out_half, joined_half), 1)
-    out_from_mate, near_moved, from_far = after((out_from_mate, near_moved, from_far), joined_half)
+    grad_out = planar_sum(after(out_half, joined_half[-1]), 1)
+    out_from_mate, near_moved, from_far = after((out_from_mate, near_moved, from_far), joined_half[-1])
     (output,) = row_call(output_kernel, [token_bf], me, resid, out_own, out_from_mate)
     grad_units = sum(piece.astype(F32) for piece in near_moved) + from_far.astype(F32)
     (d_inputs,) = row_call(finish_kernel, [token_f32], me, x, d_resid, d_normed_in, gain_in)
@@ -757,15 +787,16 @@
     last = jnp.pad(last, ((0, 0), (0, conv_width - last.shape[1])))
     if conv_width == features:
         table = jnp.concatenate([d_conv, gain_in_part, gain_ffn_part, last], axis=0)
-        table = after(table, joined_half)
-        table = tree_sum(table, "dp") if small_dp() else lax.psum(table, "dp")
-        tables = [table] + [swap(table, "tensor", mask) for mask in range(1, parts)]
+        table = after(table, joined_half[-1])
+        if small_dp():
+            table = turned(table, "dp")
+            table = tree_sum(table)
+        else:
+            table = lax.psum(table, "dp")
+        tables = turned(table, "tensor")
     else:
         raise ValueError("conv width")
-    shared = [t[4:] for t in tables]
-    while len(shared) > 1:
-        shared = [left + right for left, right in zip(shared[0::2], shared[1::2])]
-    shared = shared[0]
+    shared = tree_sum([t[4:] for t in tables])
     grad_conv = jnp.zeros(conv_weight.shape, F32)
     own_rows = jnp.zeros((2, a_log.shape[0]), F32)
     width = out_gain.shape[0]

time: 460 us -> 413 us (0.90)
  Pallas kernels: 142 us -> 113 us
  matrix products: 36 us -> 20.4 us
    pallas_call x3, Pallas kernels: 79.9 us -> 49.1 us  [the longest x1 27.2 us: mixer_forward(): pl.pallas_call(functools.partial(forward_kernel, heads), grid=(chunks //...]
    all_gather x1, waiting for transfers between devices: 28.8 us -> 13.1 us  [layer(): mixer_back_seq = lax.all_gather(d_mixed, 'tensor', axis=0, tiled=True)]
    all_gather x1, waiting for transfers between devices: 0.01 us -> 10.2 us  [layer(): seq_rows = lax.all_gather(normed, 'tensor', axis=0, tiled=True)]
    dot_general x2 -> x1, matrix products: 13.5 us -> 4.18 us  [times(): return lax.dot_general(left, right, NN, preferred_element_type=F32)]
    ppermute x60, waiting for transfers between devices: 123 us -> 133 us  [swap(): return lax.ppermute(value, axis, pairs)]
    dot_general x2 -> x1, matrix products: 12.7 us -> 8.47 us  [times_transposed(): return lax.dot_general(left, right, NT, preferred_element_type=F32)]
    unnamed x75 -> x81, local copies, waits for them, and re-layouts: 17.5 us -> 19.7 us
  transfers between devices with their start and end apart: 64 -> 64, of which waited for: 18 -> 25; matrix products, arithmetic and copies ran while one was open for 18% -> 16% of each run, Pallas kernels for 26% -> 22%
where the time goes in v4:
time: 413 us; the launch traced here: 405 us
  waiting for transfers between devices  161 us (39%)
  Pallas kernels  113 us (27%)
  starting transfers between devices  48.4 us (12%)
  local copies, waits for them, and re-layouts  29.4 us (7%)
  matrix products  20.4 us (5%)
  other arithmetic  17.4 us (4%)
  between operations  14.7 us (4%)
    ppermute x60, waiting for transfers between devices, swap(): return lax.ppermute(value, axis, pairs)  133 us
    ppermute x60, starting transfers between devices, swap(): return lax.ppermute(value, axis, pairs)  47.7 us
    pallas_call x1, Pallas kernels, mixer_backward(): pl.pallas_call(functools.partial(backward_kernel, heads, chunks), grid=(c...  33 us
    pallas_call x8, Pallas kernels, row_call(): pl.pallas_call(kernel, in_specs=[space(a) for a in args], out_specs=[pl.B...  31.1 us
    pallas_call x1, Pallas kernels, mixer_forward(): pl.pallas_call(functools.partial(forward_kernel, heads), grid=(chunks //...  27.2 us
    pallas_call x2, Pallas kernels, feed_call(): pl.pallas_call(feed_kernel, in_specs=[in_vmem] * 4, out_specs=[in_vmem] *...  21.9 us
    unnamed x81, local copies, waits for them, and re-layouts  19.7 us
    all_gather x1, waiting for transfers between devices, layer(): mixer_back_seq = lax.all_gather(d_mixed, 'tensor', axis=0, tiled=True)  13.1 us
  transfers between devices with their start and end apart: 64, of which 25 were waited for; matrix products, arithmetic and copies ran while one was open for 16% of the time, Pallas kernels for 22%

profile of v4, /device:TPU:0, one launch (start us, length us, event | category | flops | bytes accessed | tf_op | source)
XLA Modules:
  0.0 404.7 jit_solution(4599599783981079819)
XLA Ops:
  7.2 2.8 shard_map.254
  11.9 4.0 collective-permute-start.12
  16.6 2.8 collective-permute-start.5
  28.7 4.3 %collective-permute-done.5 = bf16[128,1664]{1,0:T(8,128)(2,1)S(1)} collective-permute-done((bf16[128,1664]{1,0:T(8,128)(2,1)S(1)}, bf16[128,1664]{1,0:T(8,128)(2,1)S(1)}, u32[]{:S(2)}, u32[]{:S(2)}) %collective-permute-start.5) | collective-permute-done | bytes 426016 | tf_op jit(solution)/shard_map/ppermute | solution.py:602
  33.1 7.6 %collective-permute-done.3 = bf16[128,1664]{1,0:T(8,128)(2,1)S(1)} collective-permute-done((bf16[128,1664]{1,0:T(8,128)(2,1)S(1)}, bf16[128,1664]{1,0:T(8,128)(2,1)S(1)}, u32[]{:S(2)}, u32[]{:S(2)}) %collective-permute-start.3) | collective-permute-done | bytes 426016 | tf_op jit(solution)/shard_map/ppermute | solution.py:602
  48.4 10.2 %all-gather.3.cloned.1.call-done.seq_ref.normed_ref = bf16[1024,1024]{1,0:T(8,128)(2,1)} async-done(((bf16[256,1024]{1,0:T(8,128)(2,1)}), bf16[1024,1024]{1,0:T(8,128)(2,1)}) %all-gather.3.cloned.1.call-update) | async-done | bytes 2097168 | tf_op jit(solution)/shard_map/all_gather | solution.py:728
  60.8 27.2 %mixer_forward.1 = (f32[1024,1664]{1,0:T(8,128)}, bf16[1024,512]{1,0:T(8,128)(2,1)}, f32[1024,512]{1,0:T(8,128)}, f32[8,2,128,128]{3,2,1,0:T(8,128)}, f32[8,2,12...) custom-call(bf16[1024,1024]{1,0:T(8,128)(2,1)} %all-gather.3.cloned., ...), custom_call_target="tpu_custom_call" | custom-call | tf_op jit(solution)/shard_map/mixer_forward/pallas_call | solution.py:384
  89.1 4.2 %convolution_convert_fusion.2 = bf16[1024,1024]{1,0:T(8,128)(2,1)} fusion(bf16[1024,512]{1,0:T(8,128)(2,1)} %get-tuple-element.169, bf16[512,1024]{1,0:T(8,128)(2,1)} %copy-done.12), kind=kOutput, calls=%fused_computation.2 | convolution fusion | flops 1074790400 | bytes 4194304 | tf_op jit(solution)/shard_map/dot_general | solution.py:446
  106.2 5.2 %collective-permute-done.27 = bf16[2112,128]{1,0:T(8,128)(2,1)S(1)} collective-permute-done((bf16[2112,128]{1,0:T(8,128)(2,1)}, bf16[2112,128]{1,0:T(8,128)(2,1)S(1)}, u32[]{:S(2)}, u32[]{:S(2)}) %collective-permute-start.27) | collective-permute-done | bytes 540704 | tf_op jit(solution)/shard_map/ppermute | solution.py:602
  111.4 10.7 %collective-permute-done.25 = bf16[2112,128]{1,0:T(8,128)(2,1)S(1)} collective-permute-done((bf16[2112,128]{1,0:T(8,128)(2,1)}, bf16[2112,128]{1,0:T(8,128)(2,1)S(1)}, u32[]{:S(2)}, u32[]{:S(2)}) %collective-permute-start.25) | collective-permute-done | bytes 540704 | tf_op jit(solution)/shard_map/ppermute | solution.py:602
  129.3 13.1 %collective-permute-done.29.cot_ref.cot_m = bf16[256,1024]{1,0:T(8,128)(2,1)S(1)} collective-permute-done((bf16[256,1024]{1,0:T(8,128)(2,1)S(1)}, bf16[256,1024]{1,0:T(8,128)(2,1)S(1)}, u32[]{:S(2)}, u32[]{:S(2)}) %collective-permute-start.29) | collective-permute-done | bytes 524320 | tf_op jit(solution)/shard_map/ppermute | solution.py:602
  142.3 5.3 %reduce-scatter.3.cloned.1.call-done.mixed_ref = bf16[256,1024]{1,0:T(8,128)(2,1)} async-done(((bf16[1024,1024]{1,0:T(8,128)(2,1)}), bf16[256,1024]{1,0:T(8,128)(2,1)}) %reduce-scatter.3.cloned.1.call-update) | async-done | bytes 524304 | tf_op jit(solution)/shard_map/reduce_scatter | solution.py:737
  150.1 10.8 %shard_map.256 = (bf16[704,256]{1,0:T(8,128)(2,1)}, bf16[704,256]{1,0:T(8,128)(2,1)}, bf16[704,256]{1,0:T(8,128)(2,1)}, bf16[704,256]{1,0:T(8,128)(2,1)}, bf16[7...) custom-call(bf16[256,1024]{1,0:T(8,128)(2,1)} %get-tuple-element.114.tok_r, ...), custom_call_target="tpu_custom_call" | custom-call | tf_op jit(solution)/shard_map/pallas_call | solution.py:549
  164.4 11.1 %shard_map.257 = (bf16[704,256]{1,0:T(8,128)(2,1)}, bf16[704,256]{1,0:T(8,128)(2,1)}, bf16[704,256]{1,0:T(8,128)(2,1)}, bf16[704,256]{1,0:T(8,128)(2,1)}, bf16[7...) custom-call(bf16[256,1024]{1,0:T(8,128)(2,1)} %copy-done.7, ...), custom_call_target="tpu_custom_call" | custom-call | tf_op jit(solution)/shard_map/pallas_call | solution.py:549
  175.5 6.7 %shard_map.259 = (bf16[2112,512]{1,0:T(8,128)(2,1)}, bf16[2112,512]{1,0:T(8,128)(2,1)}) custom-call(bf16[704,256]{1,0:T(8,128)(2,1)} %get-tuple-element.130.gate_o, bf16[704,256]{1,0:T(8,128)(2,1)} %get-tuple-element.131.up_o, bf16[704,256]{1,0:T(8,128)(2,1)} %get-tuple-element.132.hid_o, bf16[704,256]{1,0:T(8,128)(2,1)} %get-tuple-element.133.gate_m, ...), custom_call_target="tpu_custom_call" | custom-call | tf_op jit(solution)/shard_map/pallas_call | solution.py:592
  182.6 14.0 %collective-permute-done.31.mate_ref = bf16[256,1024]{1,0:T(8,128)(2,1)S(1)} collective-permute-done((bf16[256,1024]{1,0:T(8,128)(2,1)S(1)}, bf16[256,1024]{1,0:T(8,128)(2,1)S(1)}, u32[]{:S(2)}, u32[]{:S(2)}) %collective-permute-start.31) | collective-permute-done | bytes 524320 | tf_op jit(solution)/shard_map/ppermute | solution.py:602
  197.4 3.5 shard_map.258
  201.0 2.8 add_convert_fusion.2
  207.3 6.9 %shard_map.260 = (bf16[2112,512]{1,0:T(8,128)(2,1)}, bf16[2112,512]{1,0:T(8,128)(2,1)}) custom-call(bf16[704,256]{1,0:T(8,128)(2,1)} %get-tuple-element.138.gate_o, bf16[704,256]{1,0:T(8,128)(2,1)} %get-tuple-element.139.up_o, bf16[704,256]{1,0:T(8,128)(2,1)} %get-tuple-element.140.hid_o, bf16[704,256]{1,0:T(8,128)(2,1)} %get-tuple-element.141.gate_m, ...), custom_call_target="tpu_custom_call" | custom-call | tf_op jit(solution)/shard_map/pallas_call | solution.py:592
  214.1 5.0 %collective-permute-done.35 = bf16[2112,128]{1,0:T(8,128)(2,1)S(1)} collective-permute-done((bf16[2112,128]{1,0:T(8,128)(2,1)}, bf16[2112,128]{1,0:T(8,128)(2,1)S(1)}, u32[]{:S(2)}, u32[]{:S(2)}) %collective-permute-start.35) | collective-permute-done | bytes 540704 | tf_op jit(solution)/shard_map/ppermute | solution.py:602
  219.1 11.5 %collective-permute-done.36 = bf16[2112,128]{1,0:T(8,128)(2,1)} collective-permute-done((bf16[2112,128]{1,0:T(8,128)(2,1)}, bf16[2112,128]{1,0:T(8,128)(2,1)}, u32[]{:S(2)}, u32[]{:S(2)}) %collective-permute-start.36) | collective-permute-done | bytes 540704 | tf_op jit(solution)/shard_map/ppermute | solution.py:602
  233.2 13.1 %all-gather.5.cloned.1.call-done.back_ref = bf16[1024,1024]{1,0:T(8,128)(2,1)} async-done(((bf16[256,1024]{1,0:T(8,128)(2,1)}), bf16[1024,1024]{1,0:T(8,128)(2,1)}) %all-gather.5.cloned.1.call-update) | async-done | bytes 2097168 | tf_op jit(solution)/shard_map/all_gather | solution.py:756
  246.3 33.0 %mixer_backward.1 = (bf16[1024,1664]{1,0:T(8,128)(2,1)}, f32[4,1024]{1,0:T(4,128)}, f32[8,128]{1,0:T(8,128)}, f32[1,256]{1,0:T(1,128)}) custom-call(f32[1024,1664]{1,0:T(8,128)} %get-tuple-element.151.proj_ref.before_ref, f32[1024,1664]{1,0:T(8,128)} %get-tuple-element.151.proj_ref.before_ref, ...), custom_call_target="tpu_custom_call" | custom-call | tf_op jit(solution)/shard_map/mixer_backward/pallas_call | solution.py:413
  279.3 8.5 %convolution_convert_fusion.1.grad_ref = bf16[1024,1024]{1,0:T(8,128)(2,1)} fusion(bf16[1024,1664]{1,0:T(8,128)(2,1)} %get-tuple-element.159, bf16[1024,1664]{1,0:T(8,128)(2,1)} %copy-done.8), kind=kOutput, calls=%fused_computation.1 | convolution fusion | flops 3490709504 | bytes 8912896 | tf_op jit(solution)/shard_map/dot_general | solution.py:438
  287.8 6.4 %convolution_convert_fusion = bf16[1024,1664]{1,0:T(8,128)(2,1)S(1)} fusion(bf16[1024,1024]{1,0:T(8,128)(2,1)S(1)} %copy-done.3, bf16[1024,1664]{1,0:T(8,128)(2,1)} %get-tuple-element.159), kind=kOutput, calls=%fused_computation | convolution fusion | flops 3491364864 | bytes 8912896 | tf_op jit(solution)/shard_map/dot_general | solution.py:442
  299.3 3.2 shard_map.263
  314.3 35.8 %collective-permute-done.32.mate_ref = bf16[256,1024]{1,0:T(8,128)(2,1)S(1)} collective-permute-done((bf16[256,1024]{1,0:T(8,128)(2,1)}, bf16[256,1024]{1,0:T(8,128)(2,1)S(1)}, u32[]{:S(2)}, u32[]{:S(2)}) %collective-permute-start.32) | collective-permute-done | bytes 524320 | tf_op jit(solution)/shard_map/ppermute | solution.py:602
  366.2 2.9 collective-permute-start.52
  372.0 5.1 %collective-permute-done.51 = f32[7,1024]{1,0:T(8,128)S(1)} collective-permute-done((f32[7,1024]{1,0:T(8,128)S(1)}, f32[7,1024]{1,0:T(8,128)S(1)}, u32[]{:S(2)}, u32[]{:S(2)}) %collective-permute-start.51) | collective-permute-done | bytes 28704 | tf_op jit(solution)/shard_map/ppermute | solution.py:602
  377.7 3.3 collective-permute-done.50
  385.9 3.4 collective-permute-done.53
  394.9 3.0 shard_map.262
  (256 shorter events, 102.7 us)
Async XLA Ops:
  7.2 51.4 %all-gather.3.cloned.1.call-start = ((), (), s32[]{:S(2)}) async-start(), calls=%async_computation.2 | async-start | bytes 2621440 | tf_op jit(solution)/shard_map/all_gather | solution.py:728
  10.0 137.6 %reduce-scatter.3.cloned.1.call-start = ((), (), s32[]{:S(2)}) async-start(), calls=%async_computation.3 | async-start | bytes 2621440 | tf_op jit(solution)/shard_map/reduce_scatter | solution.py:737
  16.6 16.5 %collective-permute-start.5 = (bf16[128,1664]{1,0:T(8,128)(2,1)S(1)}, bf16[128,1664]{1,0:T(8,128)(2,1)S(1)}, u32[]{:S(2)}, u32[]{:S(2)}) collective-permute-start(bf16[128,1664]{1,0:T(8,128)(2,1)S(1)} %fusion.1), channel_id=1, source_target_pairs={{0,24},{4,28},{8,16},{12,20},{16,8},{20,12},{24,0},{28,4},{1,25},{... | collective-permute-start | bytes 1277960 | tf_op jit(solution)/shard_map/ppermute | solution.py:602
  23.8 16.9 %collective-permute-start.3 = (bf16[128,1664]{1,0:T(8,128)(2,1)S(1)}, bf16[128,1664]{1,0:T(8,128)(2,1)S(1)}, u32[]{:S(2)}, u32[]{:S(2)}) collective-permute-start(bf16[128,1664]{1,0:T(8,128)(2,1)S(1)} %fusion.1), channel_id=1, source_target_pairs={{0,16},{4,20},{8,24},{12,28},{16,0},{20,4},{24,8},{28,12},{1,17},{... | collective-permute-start | bytes 1277960 | tf_op jit(solution)/shard_map/ppermute | solution.py:602
  24.6 16.4 %collective-permute-start.1 = (bf16[128,1664]{1,0:T(8,128)(2,1)S(1)}, bf16[128,1664]{1,0:T(8,128)(2,1)S(1)}, u32[]{:S(2)}, u32[]{:S(2)}) collective-permute-start(bf16[128,1664]{1,0:T(8,128)(2,1)S(1)} %fusion.1), channel_id=1, source_target_pairs={{0,8},{4,12},{8,0},{12,4},{16,24},{20,28},{24,16},{28,20},{1,9},{5... | collective-permute-start | bytes 1277960 | tf_op jit(solution)/shard_map/ppermute | solution.py:602
  43.3 44.7 %collective-permute-start.16 = (bf16[2112,128]{1,0:T(8,128)(2,1)}, bf16[2112,128]{1,0:T(8,128)(2,1)}, u32[]{:S(2)}, u32[]{:S(2)}) collective-permute-start(bf16[2112,128]{1,0:T(8,128)(2,1)} %pad_maximum_fusion.1), channel_id=1, source_target_pairs={{0,24},{4,28},{8,16},{12,20},{16,8},{20,12},{24,0},{28,4},{1,25},{... | collective-permute-start | bytes 1622024 | tf_op jit(solution)/shard_map/ppermute | solution.py:602
  45.8 42.2 %collective-permute-start.15 = (bf16[2112,128]{1,0:T(8,128)(2,1)}, bf16[2112,128]{1,0:T(8,128)(2,1)}, u32[]{:S(2)}, u32[]{:S(2)}) collective-permute-start(bf16[2112,128]{1,0:T(8,128)(2,1)} %pad_maximum_fusion.1), channel_id=1, source_target_pairs={{0,16},{4,20},{8,24},{12,28},{16,0},{20,4},{24,8},{28,12},{1,17},{... | collective-permute-start | bytes 1622024 | tf_op jit(solution)/shard_map/ppermute | solution.py:602
  46.5 41.5 %collective-permute-start.14 = (bf16[2112,128]{1,0:T(8,128)(2,1)}, bf16[2112,128]{1,0:T(8,128)(2,1)}, u32[]{:S(2)}, u32[]{:S(2)}) collective-permute-start(bf16[2112,128]{1,0:T(8,128)(2,1)} %pad_maximum_fusion.1), channel_id=1, source_target_pairs={{0,8},{4,12},{8,0},{12,4},{16,24},{20,28},{24,16},{28,20},{1,9},{5... | collective-permute-start | bytes 1622024 | tf_op jit(solution)/shard_map/ppermute | solution.py:602
  58.6 36.5 %collective-permute-start.21 = (bf16[2112,128]{1,0:T(8,128)(2,1)}, bf16[2112,128]{1,0:T(8,128)(2,1)}, u32[]{:S(2)}, u32[]{:S(2)}) collective-permute-start(bf16[2112,128]{1,0:T(8,128)(2,1)} %pad_maximum_fusion.1), channel_id=1, source_target_pairs={{0,2},{1,3},{2,0},{3,1},{4,6},{5,7},{6,4},{7,5},{8,10},{9,11},{10,... | collective-permute-start | bytes 1622024 | tf_op jit(solution)/shard_map/ppermute | solution.py:602
  88.7 16.4 %collective-permute-start.20 = (bf16[2112,128]{1,0:T(8,128)(2,1)}, bf16[2112,128]{1,0:T(8,128)(2,1)S(1)}, u32[]{:S(2)}, u32[]{:S(2)}) collective-permute-start(bf16[2112,128]{1,0:T(8,128)(2,1)} %collective-permute-done.16), channel_id=1, source_target_pairs={{0,4},{4,0},{8,12},{12,8},{16,20},{20,16},{24,28},{28,24},{1,5},{5... | collective-permute-start | bytes 1622024 | tf_op jit(solution)/shard_map/ppermute | solution.py:602
  93.3 152.9 %all-gather.5.cloned.1.call-start = ((), (), s32[]{:S(2)}) async-start(), calls=%async_computation.4 | async-start | bytes 2621440 | tf_op jit(solution)/shard_map/all_gather | solution.py:756
  95.1 16.4 %collective-permute-start.27 = (bf16[2112,128]{1,0:T(8,128)(2,1)}, bf16[2112,128]{1,0:T(8,128)(2,1)S(1)}, u32[]{:S(2)}, u32[]{:S(2)}) collective-permute-start(bf16[2112,128]{1,0:T(8,128)(2,1)} %collective-permute-done.21), channel_id=1, source_target_pairs={{0,24},{4,28},{8,16},{12,20},{16,8},{20,12},{24,0},{28,4},{1,25},{... | collective-permute-start | bytes 1622024 | tf_op jit(solution)/shard_map/ppermute | solution.py:602
  99.5 22.6 %collective-permute-start.25 = (bf16[2112,128]{1,0:T(8,128)(2,1)}, bf16[2112,128]{1,0:T(8,128)(2,1)S(1)}, u32[]{:S(2)}, u32[]{:S(2)}) collective-permute-start(bf16[2112,128]{1,0:T(8,128)(2,1)} %collective-permute-done.21), channel_id=1, source_target_pairs={{0,16},{4,20},{8,24},{12,28},{16,0},{20,4},{24,8},{28,12},{1,17},{... | collective-permute-start | bytes 1622024 | tf_op jit(solution)/shard_map/ppermute | solution.py:602
  101.5 20.7 %collective-permute-start.23 = (bf16[2112,128]{1,0:T(8,128)(2,1)}, bf16[2112,128]{1,0:T(8,128)(2,1)S(1)}, u32[]{:S(2)}, u32[]{:S(2)}) collective-permute-start(bf16[2112,128]{1,0:T(8,128)(2,1)} %collective-permute-done.21), channel_id=1, source_target_pairs={{0,8},{4,12},{8,0},{12,4},{16,24},{20,28},{24,16},{28,20},{1,9},{5... | collective-permute-start | bytes 1622024 | tf_op jit(solution)/shard_map/ppermute | solution.py:602
  103.6 19.0 %collective-permute-start.22 = (bf16[2112,128]{1,0:T(8,128)(2,1)}, bf16[2112,128]{1,0:T(8,128)(2,1)S(1)}, u32[]{:S(2)}, u32[]{:S(2)}) collective-permute-start(bf16[2112,128]{1,0:T(8,128)(2,1)} %collective-permute-done.21), channel_id=1, source_target_pairs={{0,4},{4,0},{8,12},{12,8},{16,20},{20,16},{24,28},{28,24},{1,5},{5... | collective-permute-start | bytes 1622024 | tf_op jit(solution)/shard_map/ppermute | solution.py:602
  105.1 37.2 %collective-permute-start.29 = (bf16[256,1024]{1,0:T(8,128)(2,1)S(1)}, bf16[256,1024]{1,0:T(8,128)(2,1)S(1)}, u32[]{:S(2)}, u32[]{:S(2)}) collective-permute-start(bf16[256,1024]{1,0:T(8,128)(2,1)S(1)} %copy-done.5), channel_id=1, source_target_pairs={{0,1},{1,0},{2,3},{3,2},{4,5},{5,4},{6,7},{7,6},{8,9},{9,8},{10,11... | collective-permute-start | bytes 1572872 | tf_op jit(solution)/shard_map/ppermute | solution.py:602
  111.4 16.9 %collective-permute-start.28 = (bf16[2112,128]{1,0:T(8,128)(2,1)S(1)}, bf16[2112,128]{1,0:T(8,128)(2,1)S(1)}, u32[]{:S(2)}, u32[]{:S(2)}) collective-permute-start(bf16[2112,128]{1,0:T(8,128)(2,1)S(1)} %collective-permute-done.27), channel_id=1, source_target_pairs={{0,4},{4,0},{8,12},{12,8},{16,20},{20,16},{24,28},{28,24},{1,5},{5... | collective-permute-start | bytes 1622024 | tf_op jit(solution)/shard_map/ppermute | solution.py:602
  182.2 18.8 %collective-permute-start.33 = (bf16[2112,512]{1,0:T(8,128)(2,1)}, bf16[2112,512]{1,0:T(8,128)(2,1)}, u32[]{:S(2)}, u32[]{:S(2)}) collective-permute-start(bf16[2112,512]{1,0:T(8,128)(2,1)} %get-tuple-element.137), channel_id=1, source_target_pairs={{0,4},{4,0},{8,12},{12,8},{16,20},{20,16},{24,28},{28,24},{1,5},{5... | collective-permute-start | bytes 6488072 | tf_op jit(solution)/shard_map/ppermute | solution.py:602
  200.9 194.0 %reduce-scatter.5.cloned.1.call-start = ((), (), s32[]{:S(2)}) async-start(), calls=%async_computation.5 | async-start | bytes 2621440 | tf_op jit(solution)/shard_map/reduce_scatter | solution.py:767
  203.8 15.4 %collective-permute-start.35 = (bf16[2112,128]{1,0:T(8,128)(2,1)}, bf16[2112,128]{1,0:T(8,128)(2,1)S(1)}, u32[]{:S(2)}, u32[]{:S(2)}) collective-permute-start(bf16[2112,128]{1,0:T(8,128)(2,1)} %get-tuple-element.197), channel_id=1, source_target_pairs={{0,8},{4,12},{8,0},{12,4},{16,24},{20,28},{24,16},{28,20},{1,9},{5... | collective-permute-start | bytes 1622024 | tf_op jit(solution)/shard_map/ppermute | solution.py:602
  205.3 25.4 %collective-permute-start.36 = (bf16[2112,128]{1,0:T(8,128)(2,1)}, bf16[2112,128]{1,0:T(8,128)(2,1)}, u32[]{:S(2)}, u32[]{:S(2)}) collective-permute-start(bf16[2112,128]{1,0:T(8,128)(2,1)} %get-tuple-element.198), channel_id=1, source_target_pairs={{0,16},{4,20},{8,24},{12,28},{16,0},{20,4},{24,8},{28,12},{1,17},{... | collective-permute-start | bytes 1622024 | tf_op jit(solution)/shard_map/ppermute | solution.py:602
  206.7 23.9 %collective-permute-start.37 = (bf16[2112,128]{1,0:T(8,128)(2,1)S(1)}, bf16[2112,128]{1,0:T(8,128)(2,1)}, u32[]{:S(2)}, u32[]{:S(2)}) collective-permute-start(bf16[2112,128]{1,0:T(8,128)(2,1)S(1)} %get-tuple-element.199), channel_id=1, source_target_pairs={{0,24},{4,28},{8,16},{12,20},{16,8},{20,12},{24,0},{28,4},{1,25},{... | collective-permute-start | bytes 1622024 | tf_op jit(solution)/shard_map/ppermute | solution.py:602
  214.1 90.4 %collective-permute-start.34 = (bf16[2112,512]{1,0:T(8,128)(2,1)}, bf16[2112,512]{1,0:T(8,128)(2,1)}, u32[]{:S(2)}, u32[]{:S(2)}) collective-permute-start(bf16[2112,512]{1,0:T(8,128)(2,1)} %get-tuple-element.145), channel_id=1, source_target_pairs={{0,4},{4,0},{8,12},{12,8},{16,20},{20,16},{24,28},{28,24},{1,5},{5... | collective-permute-start | bytes 6488072 | tf_op jit(solution)/shard_map/ppermute | solution.py:602
  302.7 47.4 %collective-permute-start.32 = (bf16[256,1024]{1,0:T(8,128)(2,1)}, bf16[256,1024]{1,0:T(8,128)(2,1)S(1)}, u32[]{:S(2)}, u32[]{:S(2)}) collective-permute-start(bf16[256,1024]{1,0:T(8,128)(2,1)} %get-tuple-element.123), channel_id=1, source_target_pairs={{0,1},{1,0},{2,3},{3,2},{4,5},{5,4},{6,7},{7,6},{8,9},{9,8},{10,11... | collective-permute-start | bytes 1572872 | tf_op jit(solution)/shard_map/ppermute | solution.py:602
  306.8 45.5 %collective-permute-start.38 = (bf16[2112,128]{1,0:T(8,128)(2,1)S(1)}, bf16[2112,128]{1,0:T(8,128)(2,1)S(1)}, u32[]{:S(2)}, u32[]{:S(2)}) collective-permute-start(bf16[2112,128]{1,0:T(8,128)(2,1)S(1)} %get-tuple-element.147), channel_id=1, source_target_pairs={{0,8},{4,12},{8,0},{12,4},{16,24},{20,28},{24,16},{28,20},{1,9},{5... | collective-permute-start | bytes 1622024 | tf_op jit(solution)/shard_map/ppermute | solution.py:602
  308.3 44.5 %collective-permute-start.39 = (bf16[2112,128]{1,0:T(8,128)(2,1)S(1)}, bf16[2112,128]{1,0:T(8,128)(2,1)S(1)}, u32[]{:S(2)}, u32[]{:S(2)}) collective-permute-start(bf16[2112,128]{1,0:T(8,128)(2,1)S(1)} %get-tuple-element.148), channel_id=1, source_target_pairs={{0,16},{4,20},{8,24},{12,28},{16,0},{20,4},{24,8},{28,12},{1,17},{... | collective-permute-start | bytes 1622024 | tf_op jit(solution)/shard_map/ppermute | solution.py:602
  309.8 44.1 %collective-permute-start.40 = (bf16[2112,128]{1,0:T(8,128)(2,1)S(1)}, bf16[2112,128]{1,0:T(8,128)(2,1)S(1)}, u32[]{:S(2)}, u32[]{:S(2)}) collective-permute-start(bf16[2112,128]{1,0:T(8,128)(2,1)S(1)} %get-tuple-element.149), channel_id=1, source_target_pairs={{0,24},{4,28},{8,16},{12,20},{16,8},{20,12},{24,0},{28,4},{1,25},{... | collective-permute-start | bytes 1622024 | tf_op jit(solution)/shard_map/ppermute | solution.py:602
  310.4 44.2 %collective-permute-start.41 = (bf16[2112,128]{1,0:T(8,128)(2,1)S(1)}, bf16[2112,128]{1,0:T(8,128)(2,1)S(1)}, u32[]{:S(2)}, u32[]{:S(2)}) collective-permute-start(bf16[2112,128]{1,0:T(8,128)(2,1)S(1)} %copy-done.14), channel_id=1, source_target_pairs={{0,2},{1,3},{2,0},{3,1},{4,6},{5,7},{6,4},{7,5},{8,10},{9,11},{10,... | collective-permute-start | bytes 1622024 | tf_op jit(solution)/shard_map/ppermute | solution.py:602
  360.7 31.3 %collective-permute-start.55 = (bf16[128,1664]{1,0:T(8,128)(2,1)S(1)}, bf16[128,1664]{1,0:T(8,128)(2,1)S(1)}, u32[]{:S(2)}, u32[]{:S(2)}) collective-permute-start(bf16[128,1664]{1,0:T(8,128)(2,1)S(1)} %get-tuple-element.196), channel_id=1, source_target_pairs={{0,24},{4,28},{8,16},{12,20},{16,8},{20,12},{24,0},{28,4},{1,25},{... | collective-permute-start | bytes 1277960 | tf_op jit(solution)/shard_map/ppermute | solution.py:602
  362.7 21.1 %collective-permute-start.57 = (bf16[512,128]{1,0:T(8,128)(2,1)S(1)}, bf16[512,128]{1,0:T(8,128)(2,1)S(1)}, u32[]{:S(2)}, u32[]{:S(2)}) collective-permute-start(bf16[512,128]{1,0:T(8,128)(2,1)S(1)} %get-tuple-element.172), channel_id=1, source_target_pairs={{0,8},{4,12},{8,0},{12,4},{16,24},{20,28},{24,16},{28,20},{1,9},{5... | collective-permute-start | bytes 393224 | tf_op jit(solution)/shard_map/ppermute | solution.py:602
  363.2 21.9 %collective-permute-start.58 = (bf16[512,128]{1,0:T(8,128)(2,1)S(1)}, bf16[512,128]{1,0:T(8,128)(2,1)S(1)}, u32[]{:S(2)}, u32[]{:S(2)}) collective-permute-start(bf16[512,128]{1,0:T(8,128)(2,1)S(1)} %get-tuple-element.173), channel_id=1, source_target_pairs={{0,16},{4,20},{8,24},{12,28},{16,0},{20,4},{24,8},{28,12},{1,17},{... | collective-permute-start | bytes 393224 | tf_op jit(solution)/shard_map/ppermute | solution.py:602
  364.2 21.0 %collective-permute-start.59 = (bf16[512,128]{1,0:T(8,128)(2,1)S(1)}, bf16[512,128]{1,0:T(8,128)(2,1)S(1)}, u32[]{:S(2)}, u32[]{:S(2)}) collective-permute-start(bf16[512,128]{1,0:T(8,128)(2,1)S(1)} %get-tuple-element.174), channel_id=1, source_target_pairs={{0,24},{4,28},{8,16},{12,20},{16,8},{20,12},{24,0},{28,4},{1,25},{... | collective-permute-start | bytes 393224 | tf_op jit(solution)/shard_map/ppermute | solution.py:602
  (57 other events, 539.0 us)
Sparse Core Ops, SparseCore 0:
  10.2 48.3 all-gather.2
  93.5 54.1 reduce-scatter.2
  201.0 45.1 all-gather.4
  287.9 64.6 reduce-scatter.4
